TPU v7x, 512 devices: a whole 4x4x16 slice. The times are simulated.
512 devices in a mesh: narrow: 16 (over z_lo, x), wide: 32 (over y, z_hi, core).
Axes of the slice: x: 4, y: 4, z: 16 (z_hi: 4, z_lo: 4; z = z_hi * 4 + z_lo), core: 2. Of those that a mesh axis runs over, the one named last changes fastest.
Arguments:
- slices: bfloat16 [32, 4096, 4096], P(None, 'narrow', 'wide'), may hold values from -6 to 6
- mode_one: bfloat16 [4096, 512], P('narrow', 'wide'), may hold values from -6 to 6
- mode_two: bfloat16 [4096, 512], P('wide', 'narrow'), may hold values from -6 to 6
- slice_table: bfloat16 [1024, 512], replicated, may hold values from 0.0099487305 to 0.079589844
- chosen: int32 [32], replicated, may hold values from 0 to 1023
Outputs:
- new_one: bfloat16 [4096, 512], P('narrow', 'wide')
- new_two: bfloat16 [4096, 512], P('wide', 'narrow')
All inputs are finite; a program needn't handle non-finite values.
Results may differ from a plain program's by a relative error of at most 0.006.
Values may be sent and summed in bfloat16 or wider, within the bound.
No kernel may reach another device: no remote copies, remote signals or barrier semaphores. Data moves between devices by JAX's collectives and lax.ppermute only.
A program may use at most 64 MiB of HBM per device.

v0:
```python
import jax
import jax.numpy as jnp
from jax import lax
from jax.sharding import PartitionSpec as P

R = 512


epsilon = 1e-06
step_size = 0.5


def body(slices, mode_one, mode_two, slice_table, chosen):
    one_hot = (
        chosen[:, None]
        == lax.broadcasted_iota(jnp.int32, (chosen.shape[0], slice_table.shape[0]), 1)
    ).astype(jnp.bfloat16)
    slice_rows = jnp.dot(one_hot, slice_table, preferred_element_type=jnp.float32)
    target = slices.astype(jnp.float32)
    full_two = lax.all_gather(mode_two, "narrow", axis=1, tiled=True)
    full_one = lax.all_gather(mode_one, "wide", axis=1, tiled=True)
    scaled_two = (full_two.astype(jnp.float32)[None, :, :] * slice_rows[:, None, :]).astype(
        jnp.bfloat16
    )
    model_one = jnp.einsum("ir,kjr->kij", full_one, scaled_two, preferred_element_type=jnp.float32)
    error_one = jnp.tanh(model_one - target).astype(jnp.bfloat16)
    partial_one = jnp.einsum(
        "kij,kjr->ir", error_one, scaled_two, preferred_element_type=jnp.float32
    )
    grad_own = lax.psum_scatter(partial_one, "wide", scatter_dimension=1, tiled=True)
    squares = lax.psum(jnp.sum(grad_own * grad_own, axis=1), "wide")
    inverse = lax.rsqrt(squares / R + epsilon)
    new_one = (mode_one.astype(jnp.float32) - step_size * grad_own * inverse[:, None]).astype(
        jnp.bfloat16
    )
    new_full = lax.all_gather(new_one, "wide", axis=1, tiled=True)
    scaled_one = (new_full.astype(jnp.float32)[None, :, :] * slice_rows[:, None, :]).astype(
        jnp.bfloat16
    )
    model_two = jnp.einsum("kir,jr->kij", scaled_one, full_two, preferred_element_type=jnp.float32)
    error_two = jnp.tanh(model_two - target).astype(jnp.bfloat16)
    partial_two = jnp.einsum(
        "kij,kir->jr", error_two, scaled_one, preferred_element_type=jnp.float32
    )
    grad_two = lax.psum_scatter(partial_two, "narrow", scatter_dimension=1, tiled=True)
    squares_two = lax.psum(jnp.sum(grad_two * grad_two, axis=1), "narrow")
    inverse_two = lax.rsqrt(squares_two / R + epsilon)
    new_two = (mode_two.astype(jnp.float32) - step_size * grad_two * inverse_two[:, None]).astype(
        jnp.bfloat16
    )
    return (new_one, new_two)


def solution(mesh):
    in_specs = (P(None, "narrow", "wide"), P("narrow", "wide"), P("wide", "narrow"), P(), P())
    out_specs = (P("narrow", "wide"), P("wide", "narrow"))
    return jax.shard_map(body, mesh=mesh, in_specs=in_specs, out_specs=out_specs, check_vma=False)
```

profile of v0, /device:TPU:8, one launch (start us, length us, event | category | flops | bytes accessed | tf_op | source)
XLA Modules:
  0.0 495.0 jit_solution(15734614822737043066)
XLA Ops:
  7.2 0.0 copy-start
  7.2 0.0 reduce-scatter.3.cloned.1.call-start
  7.2 44.6 %all_gather.9 = bf16[128,512]{0,1:T(8,128)(2,1)S(1)} all-gather(bf16[128,32]{0,1:T(8,128)(2,1)} %param.7), channel_id=1, replica_groups=mesh['narrow'=16,'wide'=32] {'narrow'}, dimensions={1}, use_global_device_ids=true | all-gather | bytes 139264 | tf_op jit(solution)/shard_map/all_gather | solution.py:20
  51.8 53.2 %all_gather.10 = bf16[256,512]{0,1:T(8,128)(2,1)S(1)} all-gather(bf16[256,16]{0,1:T(8,128)(2,1)} %param.6), channel_id=1, replica_groups=mesh['narrow'=16,'wide'=32] {'wide'}, dimensions={1}, use_global_device_ids=true | all-gather | bytes 270336 | tf_op jit(solution)/shard_map/all_gather | solution.py:21
  105.1 0.0 copy-done
  105.1 1.0 fusion.25
  106.0 0.0 copy-start.1
  106.0 7.1 %fusion.17 = f32[256,512]{0,1:T(8,128)} fusion(f32[32,512]{1,0:T(8,128)S(1)} %fusion.25, f32[128,512]{0,1:T(8,128)S(1)} %convert_element_type.35, bf16[32,256,128]{2,1,0:T(8,128)(2,1)} %param.5, bf16[256,512]{0,1:T(8,128)(2,1)S(1)} %all_gather.10), kind=kOutput, calls=%fused_computation.20 | convolution fusion | flops 2159017984 | bytes 3211264 | tf_op jit(solution)/shard_map/kij,kjr->ir/dot_general | solution.py:27
  113.1 0.0 reduce-scatter.3.cloned.1.call-update
  113.2 0.0 reduce-scatter.5.cloned.1.call-start
  113.2 103.9 %reduce-scatter.3.cloned.1.call-done = f32[256,16]{0,1:T(8,128)} async-done(((f32[256,512]{0,1:T(8,128)}), f32[256,16]{0,1:T(8,128)}) %reduce-scatter.3.cloned.1.call-update) | async-done | bytes 16400 | tf_op jit(solution)/shard_map/reduce_scatter | solution.py:30
  217.1 0.7 multiply_reduce_fusion.1
  217.8 76.1 %psum.14 = f32[256]{0:T(256)S(1)} all-reduce(f32[256]{0:T(256)S(1)} %multiply_reduce_fusion.1), channel_id=1, replica_groups=mesh['narrow'=16,'wide'=32] {'wide'}, use_global_device_ids=true, to_apply=%region_2.0 | all-reduce | flops 256 | bytes 2048 | tf_op jit(solution)/shard_map/psum | solution.py:31
  293.9 0.0 copy-done.1
  293.9 0.7 subtract_convert_fusion.1
  294.7 0.0 copy-start.3
  294.7 54.9 %all_gather.11 = bf16[256,512]{0,1:T(8,128)(2,1)S(1)} all-gather(bf16[256,16]{0,1:T(8,128)(2,1)S(1)} %subtract_convert_fusion.1), channel_id=1, replica_groups=mesh['narrow'=16,'wide'=32] {'wide'}, dimensions={1}, use_global_device_ids=true | all-gather | bytes 270336 | tf_op jit(solution)/shard_map/all_gather | solution.py:36
  349.6 6.6 %fusion.11.clone.5 = bf16[32,256,128]{2,1,0:T(8,128)(2,1)S(1)} fusion(bf16[32,256,128]{2,1,0:T(8,128)(2,1)} %param.5, f32[32,512]{1,0:T(8,128)S(1)} %fusion.25, f32[256,512]{0,1:T(8,128)S(1)} %convert_element_type.41, bf16[128,512]{0,1:T(8,128)(2,1)S(1)} %all_gather.9), kind=kOutput, calls=%fused_computation.15.clone.clone.clone.2 | convolution fusion | flops 1085276160 | bytes 4915200 | tf_op jit(solution)/shard_map/kir,jr->kij/dot_general | solution.py:40
  356.2 0.0 copy-done.3
  356.2 0.0 copy-start.2
  356.2 3.1 fusion.20
  359.3 0.0 reduce-scatter.5.cloned.1.call-update
  359.3 88.1 %reduce-scatter.5.cloned.1.call-done = f32[128,32]{0,1:T(8,128)} async-done(((f32[128,512]{0,1:T(8,128)}), f32[128,32]{0,1:T(8,128)}) %reduce-scatter.5.cloned.1.call-update) | async-done | bytes 16400 | tf_op jit(solution)/shard_map/reduce_scatter | solution.py:45
  447.5 0.7 multiply_reduce_fusion
  448.2 38.6 %psum.15 = f32[128]{0:T(128)S(1)} all-reduce(f32[128]{0:T(128)S(1)} %multiply_reduce_fusion), channel_id=1, replica_groups=mesh['narrow'=16,'wide'=32] {'narrow'}, use_global_device_ids=true, to_apply=%region_5.0 | all-reduce | flops 128 | bytes 1024 | tf_op jit(solution)/shard_map/psum | solution.py:46
  486.8 0.0 copy-done.2
  486.8 1.3 subtract_convert_fusion
  (4 shorter events, 0.1 us)
Async XLA Ops:
  7.2 97.9 %copy-start = (bf16[1024,512]{1,0:T(8,128)(2,1)S(1)}, bf16[1024,512]{1,0:T(8,128)(2,1)}, u32[]{:S(2)}) copy-start(bf16[1024,512]{1,0:T(8,128)(2,1)} %param.8) | copy-start | bytes 3145732
  7.2 209.9 %reduce-scatter.3.cloned.1.call-start = ((), (), s32[]{:S(2)}) async-start(), calls=%async_computation.2 | async-start | bytes 540672 | tf_op jit(solution)/shard_map/reduce_scatter | solution.py:30
  106.0 187.9 %copy-start.1 = (bf16[256,16]{0,1:T(8,128)(2,1)S(1)}, bf16[256,16]{0,1:T(8,128)(2,1)}, u32[]{:S(2)}) copy-start(bf16[256,16]{0,1:T(8,128)(2,1)} %param.6) | copy-start | bytes 24580
  113.2 334.3 %reduce-scatter.5.cloned.1.call-start = ((), (), s32[]{:S(2)}) async-start(), calls=%async_computation.3 | async-start | bytes 278528 | tf_op jit(solution)/shard_map/reduce_scatter | solution.py:45
  294.7 61.5 %copy-start.3 = (bf16[256,16]{0,1:T(8,128)(2,1)}, bf16[256,16]{0,1:T(8,128)(2,1)S(1)}, u32[]{:S(2)}) copy-start(bf16[256,16]{0,1:T(8,128)(2,1)S(1)} %subtract_convert_fusion.1) | copy-start | bytes 24580
  356.2 130.6 %copy-start.2 = (bf16[128,32]{0,1:T(8,128)(2,1)S(1)}, bf16[128,32]{0,1:T(8,128)(2,1)}, u32[]{:S(2)}) copy-start(bf16[128,32]{0,1:T(8,128)(2,1)} %param.7) | copy-start | bytes 24580
Sparse Core Ops, SparseCore 0:
  113.3 103.7 reduce-scatter.2
  359.5 87.9 reduce-scatter.4
where the time goes:
time: 496 us; the launch traced here: 495 us
  blocking collectives  267 us (54%)
  waiting for transfers between devices  192 us (39%)
  matrix products  17.7 us (4%)
  between operations  14.1 us (3%)
    reduce_scatter x1, waiting for transfers between devices, body(): lax.psum_scatter(partial_one, 'wide', scatter_dimension=1, tiled=True)  104 us
    reduce_scatter x1, waiting for transfers between devices, body(): lax.psum_scatter(partial_two, 'narrow', scatter_dimension=1, tiled=True)  88.1 us
    psum x1, blocking collectives, body(): squares = lax.psum(jnp.sum(grad_own * grad_own, axis=1), 'wide')  76.1 us
    all_gather x1, blocking collectives, body(): new_full = lax.all_gather(new_one, 'wide', axis=1, tiled=True)  54.9 us
    all_gather x1, blocking collectives, body(): full_one = lax.all_gather(mode_one, 'wide', axis=1, tiled=True)  53.2 us
    all_gather x1, blocking collectives, body(): full_two = lax.all_gather(mode_two, 'narrow', axis=1, tiled=True)  44.6 us
    psum x1, blocking collectives, body(): squares_two = lax.psum(jnp.sum(grad_two * grad_two, axis=1), 'narrow')  38.6 us
  transfers between devices with their start and end apart: 2, of which 2 were waited for; matrix products, arithmetic and copies ran while one was open for 0% of the time, Pallas kernels for 0%

commit v1 on v0

v1 whole, which is shorter than its diff:
```python
import jax
import jax.numpy as jnp
from jax import lax
from jax.sharding import Mesh, PartitionSpec as P

R = 512


epsilon = 1e-06
step_size = 0.5

YZ = ("y", "zh")
NARROW = ("zl", "x")
WIDE = ("y", "zh", "c")
bf16 = jnp.bfloat16
f32 = jnp.float32


def spread(block, axes, count):
    copies = jnp.broadcast_to(block[None], (count,) + block.shape)
    return lax.all_to_all(copies, axes, 0, 0, tiled=True)


def renew(rows, grad):
    inverse = lax.rsqrt(jnp.sum(grad * grad, axis=1, keepdims=True) / R + epsilon)
    return (rows.astype(f32) - step_size * grad * inverse).astype(bf16)


def body(slices, mode_one, mode_two, slice_table, chosen):
    yz, c = lax.axis_index(YZ), lax.axis_index("c")
    n, w = lax.axis_index(NARROW), lax.axis_index(WIDE)
    one_hot = (
        chosen[:, None]
        == lax.broadcasted_iota(jnp.int32, (chosen.shape[0], slice_table.shape[0]), 1)
    ).astype(bf16)
    slice_rows = jnp.dot(one_hot, slice_table, preferred_element_type=f32)
    target = slices.astype(f32)

    two_t = spread(mode_two.T, NARROW, 16).reshape(R, 128)
    full_two = two_t.T
    one_t = spread(mode_one.T, YZ, 16)
    one_t = lax.all_gather(one_t, "c", axis=0).transpose(1, 0, 2, 3).reshape(R, 256)
    full_one = one_t.T

    scaled_two = (full_two.astype(f32)[None, :, :] * slice_rows[:, None, :]).astype(bf16)
    model_one = jnp.einsum("ir,kjr->kij", full_one, scaled_two, preferred_element_type=f32)
    error_one = jnp.tanh(model_one - target).astype(bf16)
    partial_one = jnp.einsum("kij,kjr->ir", error_one, scaled_two, preferred_element_type=f32)

    pair = lax.all_gather(partial_one.astype(bf16), "c", axis=0)
    half = lax.dynamic_slice_in_dim(pair, c * 128, 128, axis=1).astype(f32)
    half = (half[0] + half[1]).astype(bf16)
    parts = lax.all_to_all(half.reshape(16, 8, R), YZ, 0, 0, tiled=True)
    grad_one = jnp.sum(parts.astype(f32), axis=0)
    own = lax.dynamic_slice_in_dim(full_one, c * 128 + yz * 8, 8, axis=0)
    new_rows = renew(own, grad_one)
    new_half = spread(new_rows, YZ, 16).reshape(128, R)
    new_full = lax.all_gather(new_half, "c", axis=0, tiled=True)
    new_one = lax.dynamic_slice_in_dim(new_full, w * 16, 16, axis=1)

    scaled_one = (new_full.astype(f32)[None, :, :] * slice_rows[:, None, :]).astype(bf16)
    model_two = jnp.einsum("kir,jr->kij", scaled_one, full_two, preferred_element_type=f32)
    error_two = jnp.tanh(model_two - target).astype(bf16)
    partial_two = jnp.einsum("kij,kir->jr", error_two, scaled_one, preferred_element_type=f32)

    parts_two = lax.all_to_all(partial_two.astype(bf16).reshape(16, 8, R), NARROW, 0, 0, tiled=True)
    grad_two = jnp.sum(parts_two.astype(f32), axis=0)
    own_two = lax.dynamic_slice_in_dim(full_two, n * 8, 8, axis=0)
    rows_two = renew(own_two, grad_two)
    blocks = rows_two.reshape(8, 16, 32).transpose(1, 0, 2)
    new_two = lax.all_to_all(blocks, NARROW, 0, 0, tiled=True).reshape(128, 32)
    return (new_one, new_two)


def solution(mesh):
    fine = Mesh(mesh.devices.reshape(4, 4, 4, 4, 2), ("zl", "x", "y", "zh", "c"))
    in_specs = (P(None, NARROW, WIDE), P(NARROW, WIDE), P(WIDE, NARROW), P(), P())
    out_specs = (P(NARROW, WIDE), P(WIDE, NARROW))
    return jax.shard_map(body, mesh=fine, in_specs=in_specs, out_specs=out_specs, check_vma=False)
```

time: 496 us -> 143 us (0.29)
  the two profiles are of different devices: /device:TPU:8 before, /device:TPU:1 now
where the time goes in v1:
time: 143 us; the launch traced here: 142 us
  blocking collectives  65.7 us (46%)
  waiting for transfers between devices  26.7 us (19%)
  starting transfers between devices  21.7 us (15%)
  matrix products  12.5 us (9%)
  local copies, waits for them, and re-layouts  11.3 us (8%)
  other arithmetic  2.97 us (2%)
    all_to_all x2, blocking collectives, spread(): return lax.all_to_all(copies, axes, 0, 0, tiled=True)  53.7 us
    all_to_all x1, waiting for transfers between devices, body(): parts = lax.all_to_all(half.reshape(16, 8, R), YZ, 0, 0, tiled=True)  13.2 us
    all_to_all x1, waiting for transfers between devices, body(): lax.all_to_all(partial_two.astype(bf16).reshape(16, 8, R), NARROW, 0, 0,...  7.58 us
    all_to_all x1, starting transfers between devices, spread(): return lax.all_to_all(copies, axes, 0, 0, tiled=True)  7.49 us
    unnamed x13, local copies, waits for them, and re-layouts  6.48 us
    all_to_all x1, starting transfers between devices, body(): lax.all_to_all(partial_two.astype(bf16).reshape(16, 8, R), NARROW, 0, 0,...  6.32 us
    dot_general x1, matrix products, body(): jnp.einsum('kij,kir->jr', error_two, scaled_one, preferred_element_type=f32)  6.02 us
    all_to_all x1, waiting for transfers between devices, body(): new_two = lax.all_to_all(blocks, NARROW, 0, 0, tiled=True).reshape(128, 32)  5.93 us
  transfers between devices with their start and end apart: 4, of which 3 were waited for; matrix products, arithmetic and copies ran while one was open for 5% of the time, Pallas kernels for 0%

profile of v1, /device:TPU:1, one launch (start us, length us, event | category | flops | bytes accessed | tf_op | source)
XLA Modules:
  0.0 141.7 jit_solution(7302511565406352871)
XLA Ops:
  0.6 0.0 copy-start
  0.6 0.8 broadcast_in_dim.6
  1.4 33.8 %all_to_all.30 = bf16[16,16,256]{2,1,0:T(8,128)(2,1)S(1)} all-to-all(bf16[16,16,256]{2,1,0:T(8,128)(2,1)S(1)} %broadcast_in_dim.6), channel_id=1, replica_groups=mesh['zl'=4,'x'=4,'y'=4,'zh'=4,'c'=2] {'y','zh'}, dimensions={0} | all-to-all | bytes 262144 | tf_op jit(solution)/shard_map/all_to_all | solution.py:21
  35.2 1.4 broadcast_in_dim.7
  36.6 7.5 %all-to-all-start.1 = ((bf16[16,32,128]{2,1,0:T(8,128)(2,1)}), bf16[16,32,128]{2,1,0:T(8,128)(2,1)S(1)}, u32[]{:S(2)}, u32[]{:S(2)}) async-start(bf16[16,32,128]{2,1,0:T(8,128)(2,1)} %broadcast_in_dim.7), calls=%async_computation.1 | async-start | bytes 262144 | tf_op jit(solution)/shard_map/all_to_all | solution.py:21
  44.1 0.0 copy-start.2
  44.1 3.3 %copy.29 = bf16[32,256,128]{1,2,0:T(8,128)(2,1)S(1)} copy(bf16[32,256,128]{2,1,0:T(8,128)(2,1)} %param.5) | data formatting | bytes 4194304 | tf_op args[0]
  47.4 0.0 copy-done
  47.4 0.0 copy-done.2
  47.4 0.9 fusion.28
  48.4 3.0 %all-gather = bf16[32,16,256]{2,1,0:T(8,128)(2,1)S(1)} all-gather(bf16[16,16,256]{2,1,0:T(8,128)(2,1)S(1)} %all_to_all.30), channel_id=2, replica_groups=mesh['zl'=4,'x'=4,'y'=4,'zh'=4,'c'=2] {'c'}, dimensions={0}, use_global_device_ids=true | all-gather | bytes 393216 | tf_op jit(solution)/shard_map/all_gather | solution.py:42
  51.4 0.7 copy.26
  52.1 0.0 all-to-all-done.1
  52.1 0.8 copy.28
  53.0 5.5 %fusion.20 = bf16[256,512]{1,0:T(8,128)(2,1)} fusion(f32[32,512]{1,0:T(8,128)} %fusion.28, f32[128,512]{1,0:T(8,128)} %copy.28, bf16[32,256,128]{1,2,0:T(8,128)(2,1)S(1)} %copy.29, bf16[512,256,1]{1,0,2:T(8,128)(2,1)} %bitcast.54), kind=kOutput, calls=%fused_computation.21 | convolution fusion | flops 2159149056 | bytes 2949120 | tf_op jit(solution)/shard_map/kij,kjr->ir/dot_general | solution.py:48
  58.5 0.0 copy-start.1
  58.5 4.5 %all-gather.1 = bf16[512,512]{1,0:T(8,128)(2,1)S(1)} all-gather(bf16[256,512]{1,0:T(8,128)(2,1)} %fusion.20), channel_id=3, replica_groups=mesh['zl'=4,'x'=4,'y'=4,'zh'=4,'c'=2] {'c'}, dimensions={0}, use_global_device_ids=true | all-gather | bytes 786432 | tf_op jit(solution)/shard_map/all_gather | solution.py:50
  63.1 0.7 fusion.27
  63.7 4.2 %all-to-all-start.2 = ((bf16[16,8,512]{2,1,0:T(8,128)(2,1)}), bf16[16,8,512]{2,1,0:T(8,128)(2,1)}, u32[]{:S(2)}, u32[]{:S(2)}) async-start(bf16[16,8,512]{2,1,0:T(8,128)(2,1)} %fusion.27), calls=%async_computation.2 | async-start | bytes 262144 | tf_op jit(solution)/shard_map/all_to_all | solution.py:53
  67.9 0.0 copy-done.1
  67.9 0.7 constant_dynamic-slice_fusion.2
  68.7 1.0 copy.38
  69.7 13.2 %all-to-all-done.2 = bf16[16,8,512]{2,1,0:T(8,128)(2,1)} async-done(((bf16[16,8,512]{2,1,0:T(8,128)(2,1)}), bf16[16,8,512]{2,1,0:T(8,128)(2,1)}, u32[]{:S(2)}, u32[]{:S(2)}) %all-to-all-start.2) | async-done | bytes 131104 | tf_op jit(solution)/shard_map/all_to_all | solution.py:53
  82.9 0.9 convert_reduce_fusion.1
  83.8 0.1 multiply_reduce_fusion.1
  83.9 0.1 fusion.31
  84.0 19.9 %all_to_all.31 = bf16[16,8,512]{2,1,0:T(8,128)(2,1)S(1)} all-to-all(bf16[16,8,512]{2,1,0:T(8,128)(2,1)S(1)} %broadcast_in_dim.8), channel_id=1, replica_groups=mesh['zl'=4,'x'=4,'y'=4,'zh'=4,'c'=2] {'y','zh'}, dimensions={0} | all-to-all | bytes 262144 | tf_op jit(solution)/shard_map/all_to_all | solution.py:21
  104.0 4.5 %all_gather.19 = bf16[256,512]{1,0:T(8,128)(2,1)S(1)} all-gather(bf16[128,512]{1,0:T(8,128)(2,1)S(1)} %bitcast.56), channel_id=1, replica_groups=mesh['zl'=4,'x'=4,'y'=4,'zh'=4,'c'=2] {'c'}, dimensions={0}, use_global_device_ids=true | all-gather | bytes 393216 | tf_op jit(solution)/shard_map/all_gather | solution.py:58
  108.5 0.8 convert_element_type.80
  109.3 6.0 %fusion.25 = bf16[16,8,512]{2,1,0:T(8,128)(2,1)} fusion(f32[32,512]{1,0:T(8,128)} %fusion.28, f32[256,512]{1,0:T(8,128)} %convert_element_type.80, bf16[32,256,128]{1,2,0:T(8,128)(2,1)S(1)} %copy.29, bf16[512,128,1]{1,0,2:T(8,128)(2,1)S(1)} %bitcast.50), kind=kOutput, calls=%fused_computation.24 | convolution fusion | flops 2167472128 | bytes 2949120 | tf_op jit(solution)/shard_map/kij,kir->jr/dot_general | solution.py:64
  115.3 6.3 %all-to-all-start.4 = ((bf16[16,8,512]{2,1,0:T(8,128)(2,1)}), bf16[16,8,512]{2,1,0:T(8,128)(2,1)S(1)}, u32[]{:S(2)}, u32[]{:S(2)}) async-start(bf16[16,8,512]{2,1,0:T(8,128)(2,1)} %fusion.25), calls=%async_computation.4 | async-start | bytes 262144 | tf_op jit(solution)/shard_map/all_to_all | solution.py:66
  121.7 0.1 constant_dynamic-slice_fusion
  121.8 0.1 copy.39
  121.8 7.6 %all-to-all-done.4 = bf16[16,8,512]{2,1,0:T(8,128)(2,1)S(1)} async-done(((bf16[16,8,512]{2,1,0:T(8,128)(2,1)}), bf16[16,8,512]{2,1,0:T(8,128)(2,1)S(1)}, u32[]{:S(2)}, u32[]{:S(2)}) %all-to-all-start.4) | async-done | bytes 131104 | tf_op jit(solution)/shard_map/all_to_all | solution.py:66
  129.4 0.1 multiply_reduce_fusion
  129.6 0.1 fusion.30
  129.7 0.1 reshape.54
  129.8 0.7 reshape.62
  130.5 3.7 %all-to-all-start.5 = ((bf16[16,2,128]{2,1,0:T(2,128)(2,1)}), bf16[16,2,128]{2,1,0:T(2,128)(2,1)S(1)}, u32[]{:S(2)}, u32[]{:S(2)}) async-start(bf16[16,2,128]{2,1,0:T(2,128)(2,1)} %reshape.62), calls=%async_computation.5 | async-start | bytes 16384 | tf_op jit(solution)/shard_map/all_to_all | solution.py:71
  134.2 0.1 constant_dynamic-slice_fusion.1
  134.3 0.7 copy.34
  135.0 5.9 %all-to-all-done.5 = bf16[16,2,128]{2,1,0:T(2,128)(2,1)S(1)} async-done(((bf16[16,2,128]{2,1,0:T(2,128)(2,1)}), bf16[16,2,128]{2,1,0:T(2,128)(2,1)S(1)}, u32[]{:S(2)}, u32[]{:S(2)}) %all-to-all-start.5) | async-done | bytes 8224 | tf_op jit(solution)/shard_map/all_to_all | solution.py:71
  140.9 0.1 reshape.63
  141.0 0.7 copy.35
  (7 shorter events, 0.1 us)
Async XLA Ops:
  0.6 46.8 %copy-start = (bf16[1024,512]{1,0:T(8,128)(2,1)S(1)}, bf16[1024,512]{1,0:T(8,128)(2,1)}, u32[]{:S(2)}) copy-start(bf16[1024,512]{1,0:T(8,128)(2,1)} %param.8) | copy-start | bytes 3145732
  36.6 15.5 %all-to-all-start.1 = ((bf16[16,32,128]{2,1,0:T(8,128)(2,1)}), bf16[16,32,128]{2,1,0:T(8,128)(2,1)S(1)}, u32[]{:S(2)}, u32[]{:S(2)}) async-start(bf16[16,32,128]{2,1,0:T(8,128)(2,1)} %broadcast_in_dim.7), calls=%async_computation.1 | async-start | bytes 262144 | tf_op jit(solution)/shard_map/all_to_all | solution.py:21
  44.1 3.3 %copy-start.2 = (s32[32]{0:T(128)S(1)}, s32[32]{0:T(128)}, u32[]{:S(2)}) copy-start(s32[32]{0:T(128)} %param.9) | copy-start | bytes 388
  58.5 9.4 %copy-start.1 = (bf16[16,2,16,256]{3,2,1,0:T(8,128)(2,1)S(1)}, bf16[16,2,16,256]{3,2,1,0:T(8,128)(2,1)}, u32[]{:S(2)}) copy-start(bf16[16,2,16,256]{3,2,1,0:T(8,128)(2,1)} %copy.26) | copy-start | bytes 786436
  63.7 19.1 %all-to-all-start.2 = ((bf16[16,8,512]{2,1,0:T(8,128)(2,1)}), bf16[16,8,512]{2,1,0:T(8,128)(2,1)}, u32[]{:S(2)}, u32[]{:S(2)}) async-start(bf16[16,8,512]{2,1,0:T(8,128)(2,1)} %fusion.27), calls=%async_computation.2 | async-start | bytes 262144 | tf_op jit(solution)/shard_map/all_to_all | solution.py:53
  115.3 14.1 %all-to-all-start.4 = ((bf16[16,8,512]{2,1,0:T(8,128)(2,1)}), bf16[16,8,512]{2,1,0:T(8,128)(2,1)S(1)}, u32[]{:S(2)}, u32[]{:S(2)}) async-start(bf16[16,8,512]{2,1,0:T(8,128)(2,1)} %fusion.25), calls=%async_computation.4 | async-start | bytes 262144 | tf_op jit(solution)/shard_map/all_to_all | solution.py:66
  130.5 10.4 %all-to-all-start.5 = ((bf16[16,2,128]{2,1,0:T(2,128)(2,1)}), bf16[16,2,128]{2,1,0:T(2,128)(2,1)S(1)}, u32[]{:S(2)}, u32[]{:S(2)}) async-start(bf16[16,2,128]{2,1,0:T(2,128)(2,1)} %reshape.62), calls=%async_computation.5 | async-start | bytes 16384 | tf_op jit(solution)/shard_map/all_to_all | solution.py:71

commit v2 on v1

v2 whole, which is shorter than its diff:
```python
import jax
import jax.numpy as jnp
from jax import lax
from jax.experimental import pallas as pl
from jax.experimental.pallas import tpu as pltpu
from jax.sharding import Mesh, PartitionSpec as P

R = 512


epsilon = 1e-06
step_size = 0.5

YZ = ("y", "zh")
NARROW = ("zl", "x")
WIDE = ("y", "zh", "c")
bf16 = jnp.bfloat16
f32 = jnp.float32

NN = (((1,), (0,)), ((), ()))
NT = (((1,), (1,)), ((), ()))
TN = (((0,), (0,)), ((), ()))
CHUNKS = 4
BATCH = 32


def dot(a, b, dims):
    return lax.dot_general(a, b, dims, preferred_element_type=f32)


def pick(first, count, total):
    col = lax.broadcasted_iota(jnp.int32, (count, total), 1)
    row = lax.broadcasted_iota(jnp.int32, (count, total), 0)
    return (col == row + first).astype(bf16)


def fetch_kernel(t_hbm, t, sems):
    size = BATCH // CHUNKS
    copies = [
        pltpu.make_async_copy(t_hbm.at[pl.ds(q * size, size)], t.at[pl.ds(q * size, size)], sems.at[q])
        for q in range(CHUNKS)
    ]
    for copy in copies:
        copy.start()
    for copy in copies:
        copy.wait()


def errors(s, left, two, t, k):
    scaled = jnp.concatenate([two[...] * s[0:1], two[...] * s[1:2]], axis=0).astype(bf16)
    model = dot(left, scaled, NT)
    target = jnp.concatenate([t[k], t[k + 1]], axis=1).astype(f32)
    return scaled, jnp.tanh(model - target).astype(bf16)


def first_kernel(pos, s_ref, one_ref, two_ref, t, out_ref, own_ref, one_t, one, two, acc):
    for b in range(16):
        for c in range(2):
            one_t[pl.ds(32 * b + 16 * c, 16), :] = one_ref[c, b]
    one[...] = one_t[...].T
    two[...] = two_ref[...].reshape(R, 128).astype(f32).T
    acc[...] = jnp.zeros_like(acc)
    own_ref[...] = dot(pick(pos[0], 8, 256), one[...], NN)
    for k in range(0, BATCH, 2):
        scaled, error = errors(s_ref[k : k + 2, :], one[...], two, t, k)
        acc[...] += dot(error, scaled, NN)
    out_ref[...] = acc[...].astype(bf16)


def second_kernel(pos, s_ref, new_ref, two_ref, t, out_ref, block_ref, own_ref, two, acc):
    two[...] = two_ref[...].reshape(R, 128).astype(f32).T
    acc[...] = jnp.zeros_like(acc)
    block_ref[...] = dot(pick(pos[1], 16, R), new_ref[...], NT).astype(bf16)
    own_ref[...] = dot(pick(pos[2], 8, 128), two[...].astype(bf16), NN)
    for k in range(0, BATCH, 2):
        s = s_ref[k : k + 2, :]
        _, error = errors(s, new_ref[...], two, t, k)
        both = dot(error, new_ref[...], TN)
        acc[...] += both[:128] * s[0:1] + both[128:] * s[1:2]
    out_ref[...] = acc[...].astype(bf16).reshape(16, 8, R)


def pair_kernel(pos, pair_ref, out_ref):
    rows = pl.ds(pl.multiple_of(pos[3], 128), 128)
    total = pair_ref[0, rows, :].astype(f32) + pair_ref[1, rows, :].astype(f32)
    out_ref[...] = total.astype(bf16).reshape(16, 8, R)


def renew(own, parts):
    grad = jnp.sum(parts.astype(f32), axis=0)
    inverse = lax.rsqrt(jnp.sum(grad * grad, axis=1, keepdims=True) / R + epsilon)
    return own - step_size * grad * inverse


def renew_one_kernel(own_ref, parts_ref, out_ref):
    new = renew(own_ref[...], parts_ref[...]).astype(bf16)
    for b in range(16):
        out_ref[b] = new


def renew_two_kernel(own_ref, parts_ref, out_ref):
    new = renew(own_ref[...], parts_ref[...])
    for b in range(16):
        group = new[:, 128 * (b // 4) : 128 * (b // 4) + 128]
        turn = (128 - 32 * (b % 4)) % 128
        out_ref[b] = (pltpu.roll(group, turn, 1) if turn else group).astype(bf16)


def last_kernel(in_ref, out_ref):
    out_ref[...] = in_ref[...].reshape(128, 128).astype(f32).T[:32].astype(bf16)


VM = pl.BlockSpec(memory_space=pltpu.VMEM)
SM = pl.BlockSpec(memory_space=pltpu.SMEM)
HB = pl.BlockSpec(memory_space=pltpu.HBM)


def call(kernel, outs, specs, scratch=(), flops=0, nbytes=0, vmem=4):
    shapes = [jax.ShapeDtypeStruct(shape, dtype) for shape, dtype in outs]
    single = len(outs) == 1
    return pl.pallas_call(
        kernel,
        out_shape=shapes[0] if single else shapes,
        in_specs=specs,
        out_specs=VM if single else [VM] * len(outs),
        scratch_shapes=list(scratch),
        compiler_params=pltpu.CompilerParams(vmem_limit_bytes=vmem << 20),
        cost_estimate=pl.CostEstimate(flops=flops, bytes_accessed=nbytes, transcendentals=0),
    )


def spread(block, axes, count):
    copies = jnp.broadcast_to(block[None], (count,) + block.shape)
    return lax.all_to_all(copies, axes, 0, 0, tiled=True)


def body(slices, mode_one, mode_two, slice_table, chosen):
    yz, c = lax.axis_index(YZ), lax.axis_index("c")
    n, w = lax.axis_index(NARROW), lax.axis_index(WIDE)
    pos = jnp.stack([c * 128 + yz * 8, w * 16, n * 8, c * 128]).astype(jnp.int32)

    one_g = spread(mode_one.T, YZ, 16)
    two_g = spread(mode_two.T, NARROW, 16)
    one_hot = (
        chosen[:, None]
        == lax.broadcasted_iota(jnp.int32, (chosen.shape[0], slice_table.shape[0]), 1)
    ).astype(bf16)
    slice_rows = jnp.dot(one_hot, slice_table, preferred_element_type=f32)
    one_g = lax.all_gather(one_g, "c", axis=0)

    t = call(fetch_kernel, [((BATCH, 256, 128), bf16)], [HB], (pltpu.SemaphoreType.DMA((CHUNKS,)),), nbytes=1 << 21)(slices)
    half, own_one = call(
        first_kernel,
        [((256, R), bf16), ((8, R), f32)],
        [SM, VM, VM, VM, VM],
        (pltpu.VMEM((R, 256), bf16), pltpu.VMEM((256, R), bf16), pltpu.VMEM((128, R), f32), pltpu.VMEM((256, R), f32)),
        flops=1 << 31,
        vmem=16,
        nbytes=1 << 21,
    )(pos, slice_rows, one_g, two_g, t)
    pair = lax.all_gather(half, "c", axis=0)
    half = call(pair_kernel, [((16, 8, R), bf16)], [SM, VM])(pos, pair)
    parts = lax.all_to_all(half, YZ, 0, 0, tiled=True)
    copies = call(renew_one_kernel, [((16, 8, R), bf16)], [VM, VM])(own_one, parts)
    new_half = lax.all_to_all(copies, YZ, 0, 0, tiled=True).reshape(128, R)
    new_full = lax.all_gather(new_half, "c", axis=0, tiled=True)

    partial_two, new_one_t, own_two = call(
        second_kernel,
        [((16, 8, R), bf16), ((16, 256), bf16), ((8, R), f32)],
        [SM, VM, VM, VM, VM],
        (pltpu.VMEM((128, R), f32), pltpu.VMEM((128, R), f32)),
        flops=1 << 31,
        vmem=16,
        nbytes=1 << 21,
    )(pos, slice_rows, new_full, two_g, t)
    parts_two = lax.all_to_all(partial_two, NARROW, 0, 0, tiled=True)
    blocks = call(renew_two_kernel, [((16, 8, 128), bf16)], [VM, VM])(own_two, parts_two)
    blocks = lax.all_to_all(blocks, NARROW, 0, 0, tiled=True)
    new_two_t = call(last_kernel, [((32, 128), bf16)], [VM])(blocks)
    return (new_one_t.T, new_two_t.T)


def solution(mesh):
    fine = Mesh(mesh.devices.reshape(4, 4, 4, 4, 2), ("zl", "x", "y", "zh", "c"))
    in_specs = (P(None, NARROW, WIDE), P(NARROW, WIDE), P(WIDE, NARROW), P(), P())
    out_specs = (P(NARROW, WIDE), P(WIDE, NARROW))

    return jax.shard_map(body, mesh=fine, in_specs=in_specs, out_specs=out_specs, check_vma=False)
```

time: 143 us -> 131 us (0.916)
  blocking collectives: 65.7 us -> 106 us
  waiting for transfers between devices: 26.7 us -> 1.33 us
  starting transfers between devices: 21.7 us -> 7.49 us
  matrix products: 12.5 us -> 0.94 us
  Pallas kernels: 0 us -> 8.37 us
  local copies, waits for them, and re-layouts: 11.3 us -> 4.97 us
  other arithmetic: 2.97 us -> 0.08 us
    all_to_all x0 -> x4, blocking collectives: none -> 61.1 us  [the longest x1 20.1 us: body(): new_half = lax.all_to_all(copies, YZ, 0, 0, tiled=True).reshape(128, R)]
    all_to_all x3 -> x0, waiting for transfers between devices: 26.7 us -> none  [the longest x1 13.2 us: body(): parts = lax.all_to_all(half.reshape(16, 8, R), YZ, 0, 0, tiled=True)]
    all_to_all x2 -> x1, blocking collectives: 53.7 us -> 33.9 us  [spread(): return lax.all_to_all(copies, axes, 0, 0, tiled=True)]
    all_to_all x3 -> x0, starting transfers between devices: 14.2 us -> none  [the longest x1 6.32 us: body(): lax.all_to_all(partial_two.astype(bf16).reshape(16, 8, R), NARROW, 0, 0,...]
    dot_general x2 -> x0, matrix products: 11.6 us -> none  [the longest x1 6.02 us: body(): jnp.einsum('kij,kir->jr', error_two, scaled_one, preferred_element_type=f32)]
    pallas_call x0 -> x7, Pallas kernels: none -> 8.37 us  [the longest x1 3.33 us: body(): call(second_kernel, [((16, 8, R), bf16), ((16, 256), bf16), ((8, R), f32)...]
    unnamed x13 -> x8, local copies, waits for them, and re-layouts: 6.48 us -> 2.81 us
    convert_element_type x6 -> x0, other arithmetic: 1.77 us -> none  [the longest x1 0.85 us: body(): new_full.astype(f32)[None, :, :] * slice_rows[:, None, :]]
  transfers between devices with their start and end apart: 4 -> 1, of which waited for: 3 -> 1; matrix products, arithmetic and copies ran while one was open for 5% -> 1% of each run, Pallas kernels for 0% -> 0%
where the time goes in v2:
time: 131 us; the launch traced here: 130 us
  blocking collectives  106 us (81%)
  Pallas kernels  8.37 us (6%)
  starting transfers between devices  7.49 us (6%)
  local copies, waits for them, and re-layouts  4.97 us (4%)
  waiting for transfers between devices  1.33 us (1%)
    all_to_all x1, blocking collectives, spread(): return lax.all_to_all(copies, axes, 0, 0, tiled=True)  33.9 us
    all_to_all x1, blocking collectives, body(): new_half = lax.all_to_all(copies, YZ, 0, 0, tiled=True).reshape(128, R)  20.1 us
    all_to_all x1, blocking collectives, body(): parts = lax.all_to_all(half, YZ, 0, 0, tiled=True)  17.5 us
    all_to_all x1, blocking collectives, body(): parts_two = lax.all_to_all(partial_two, NARROW, 0, 0, tiled=True)  13.1 us
    all_to_all x1, blocking collectives, body(): blocks = lax.all_to_all(blocks, NARROW, 0, 0, tiled=True)  10.5 us
    all_to_all x1, starting transfers between devices, spread(): return lax.all_to_all(copies, axes, 0, 0, tiled=True)  7.49 us
    all_gather x1, blocking collectives, body(): pair = lax.all_gather(half, 'c', axis=0)  4.37 us
    all_gather x1, blocking collectives, body(): new_full = lax.all_gather(new_half, 'c', axis=0, tiled=True)  3.51 us
  transfers between devices with their start and end apart: 1, of which 1 were waited for; matrix products, arithmetic and copies ran while one was open for 1% of the time, Pallas kernels for 0%

profile of v2, /device:TPU:1, one launch (start us, length us, event | category | flops | bytes accessed | tf_op | source)
XLA Modules:
  0.0 130.1 jit_solution(1562401564483925402)
XLA Ops:
  0.6 0.0 copy-start
  0.6 0.8 broadcast_in_dim.4
  1.4 33.9 %all_to_all.30 = bf16[16,16,256]{2,1,0:T(8,128)(2,1)} all-to-all(bf16[16,16,256]{2,1,0:T(8,128)(2,1)S(1)} %broadcast_in_dim.4), channel_id=1, replica_groups=mesh['zl'=4,'x'=4,'y'=4,'zh'=4,'c'=2] {'y','zh'}, dimensions={0} | all-to-all | bytes 262144 | tf_op jit(solution)/shard_map/all_to_all | solution.py:134
  35.3 1.4 %broadcast_in_dim.5 = bf16[16,32,128]{2,1,0:T(8,128)(2,1)} broadcast(bf16[32,128]{1,0:T(8,128)(2,1)} %bitcast.16), dimensions={1,2} | broadcast | bytes 139264 | tf_op jit(solution)/shard_map/broadcast_in_dim | solution.py:133
  36.7 7.5 %all-to-all-start.1 = ((bf16[16,32,128]{2,1,0:T(8,128)(2,1)}), bf16[16,32,128]{2,1,0:T(8,128)(2,1)S(1)}, u32[]{:S(2)}, u32[]{:S(2)}) async-start(bf16[16,32,128]{2,1,0:T(8,128)(2,1)} %broadcast_in_dim.5), calls=%async_computation.1 | async-start | bytes 262144 | tf_op jit(solution)/shard_map/all_to_all | solution.py:134
  44.2 0.0 copy-start.1
  44.2 1.6 %copy-done.1 = bf16[32,256,128]{2,1,0:T(8,128)(2,1)S(1)} copy-done((bf16[32,256,128]{2,1,0:T(8,128)(2,1)S(1)}, bf16[32,256,128]{2,1,0:T(8,128)(2,1)}, u32[]{:S(2)}) %copy-start.1) | copy-done | bytes 2097176
  45.8 0.0 copy-start.3
  45.8 0.2 shard_map.68.t
  46.0 0.1 pad_add_fusion.pos
  46.1 0.0 copy-done
  46.1 0.4 copy-done.3
  46.5 0.9 fusion.s_ref
  47.4 3.2 %all-gather = bf16[32,16,256]{2,1,0:T(8,128)(2,1)S(1)} all-gather(bf16[16,16,256]{2,1,0:T(8,128)(2,1)} %all_to_all.30), channel_id=2, replica_groups=mesh['zl'=4,'x'=4,'y'=4,'zh'=4,'c'=2] {'c'}, dimensions={0}, use_global_device_ids=true | all-gather | bytes 393216 | tf_op jit(solution)/shard_map/all_gather | solution.py:149
  50.7 1.3 %all-to-all-done.1.two_ref = bf16[16,32,128]{2,1,0:T(8,128)(2,1)S(1)} async-done(((bf16[16,32,128]{2,1,0:T(8,128)(2,1)}), bf16[16,32,128]{2,1,0:T(8,128)(2,1)S(1)}, u32[]{:S(2)}, u32[]{:S(2)}) %all-to-all-start.1) | async-done | bytes 131104 | tf_op jit(solution)/shard_map/all_to_all | solution.py:134
  52.0 0.0 copy-start.2
  52.0 0.8 copy-done.2
  52.8 3.3 %shard_map.69 = (bf16[256,512]{1,0:T(8,128)(2,1)S(1)}, f32[8,512]{1,0:T(8,128)S(1)}) custom-call(s32[4]{0:T(128)S(1)} %pad_add_fusion.pos, f32[32,512]{1,0:T(8,128)S(1)} %copy-done.2, bf16[2,16,16,256]{3,2,1,0:T(8,128)(2,1)S(1)} %bitcast.13, bf16[16,32,128]{2,1,0:T(8,128)(2,1)S(1)} %all-to-all-done.1.two_ref, bf16[32,256,128]{2,1,0:T(8,128)(2,1)S(1)} %shard_map.68.t), custom_call_target="tpu_custom_call" | custom-call | flops 2147483648 | bytes 2097152 | tf_op jit(solution)/shard_map/pallas_call | solution.py:152
  56.2 4.4 %all-gather.1 = bf16[512,512]{1,0:T(8,128)(2,1)S(1)} all-gather(bf16[256,512]{1,0:T(8,128)(2,1)S(1)} %get-tuple-element.8), channel_id=3, replica_groups=mesh['zl'=4,'x'=4,'y'=4,'zh'=4,'c'=2] {'c'}, dimensions={0}, use_global_device_ids=true | all-gather | bytes 786432 | tf_op jit(solution)/shard_map/all_gather | solution.py:161
  60.5 0.6 shard_map.70
  61.1 17.5 %all_to_all.31.parts_ref = bf16[16,8,512]{2,1,0:T(8,128)(2,1)S(1)} all-to-all(bf16[16,8,512]{2,1,0:T(8,128)(2,1)S(1)} %shard_map.70), channel_id=1, replica_groups=mesh['zl'=4,'x'=4,'y'=4,'zh'=4,'c'=2] {'y','zh'}, dimensions={0} | all-to-all | bytes 262144 | tf_op jit(solution)/shard_map/all_to_all | solution.py:163
  78.6 0.1 shard_map.71
  78.7 20.1 %all_to_all.32 = bf16[16,8,512]{2,1,0:T(8,128)(2,1)S(1)} all-to-all(bf16[16,8,512]{2,1,0:T(8,128)(2,1)S(1)} %shard_map.71), channel_id=1, replica_groups=mesh['zl'=4,'x'=4,'y'=4,'zh'=4,'c'=2] {'y','zh'}, dimensions={0} | all-to-all | bytes 262144 | tf_op jit(solution)/shard_map/all_to_all | solution.py:165
  98.7 3.5 %all_gather.19.new_ref = bf16[256,512]{1,0:T(8,128)(2,1)S(1)} all-gather(bf16[128,512]{1,0:T(8,128)(2,1)S(1)} %bitcast.14), channel_id=1, replica_groups=mesh['zl'=4,'x'=4,'y'=4,'zh'=4,'c'=2] {'c'}, dimensions={0}, use_global_device_ids=true | all-gather | bytes 393216 | tf_op jit(solution)/shard_map/all_gather | solution.py:166
  102.3 3.3 %shard_map.72 = (bf16[16,8,512]{2,1,0:T(8,128)(2,1)S(1)}, bf16[16,256]{1,0:T(8,128)(2,1)}, f32[8,512]{1,0:T(8,128)S(1)}) custom-call(s32[4]{0:T(128)S(1)} %pad_add_fusion.pos, f32[32,512]{1,0:T(8,128)S(1)} %copy-done.2, bf16[256,512]{1,0:T(8,128)(2,1)S(1)} %all_gather.19.new_ref, bf16[16,32,128]{2,1,0:T(8,128)(2,1)S(1)} %all-to-all-done.1.two_ref, ...), custom_call_target="tpu_custom_call" | custom-call | flops 2147483648 | bytes 2097152 | tf_op jit(solution)/shard_map/pallas_call | solution.py:168
  105.6 13.1 %all_to_all.33.parts_ref = bf16[16,8,512]{2,1,0:T(8,128)(2,1)S(1)} all-to-all(bf16[16,8,512]{2,1,0:T(8,128)(2,1)S(1)} %get-tuple-element.11), channel_id=1, replica_groups=mesh['zl'=4,'x'=4,'y'=4,'zh'=4,'c'=2] {'zl','x'}, dimensions={0} | all-to-all | bytes 262144 | tf_op jit(solution)/shard_map/all_to_all | solution.py:177
  118.7 0.2 shard_map.73
  118.9 10.5 %all_to_all.34.in_ref = bf16[16,8,128]{2,1,0:T(8,128)(2,1)S(1)} all-to-all(bf16[16,8,128]{2,1,0:T(8,128)(2,1)S(1)} %shard_map.73), channel_id=1, replica_groups=mesh['zl'=4,'x'=4,'y'=4,'zh'=4,'c'=2] {'zl','x'}, dimensions={0} | all-to-all | bytes 65536 | tf_op jit(solution)/shard_map/all_to_all | solution.py:179
  129.4 0.7 shard_map.74
Async XLA Ops:
  0.6 45.5 %copy-start = (bf16[1024,512]{1,0:T(8,128)(2,1)S(1)}, bf16[1024,512]{1,0:T(8,128)(2,1)}, u32[]{:S(2)}) copy-start(bf16[1024,512]{1,0:T(8,128)(2,1)} %param.8) | copy-start | bytes 3145732
  36.7 15.3 %all-to-all-start.1 = ((bf16[16,32,128]{2,1,0:T(8,128)(2,1)}), bf16[16,32,128]{2,1,0:T(8,128)(2,1)S(1)}, u32[]{:S(2)}, u32[]{:S(2)}) async-start(bf16[16,32,128]{2,1,0:T(8,128)(2,1)} %broadcast_in_dim.5), calls=%async_computation.1 | async-start | bytes 262144 | tf_op jit(solution)/shard_map/all_to_all | solution.py:134
  44.2 1.6 %copy-start.1 = (bf16[32,256,128]{2,1,0:T(8,128)(2,1)S(1)}, bf16[32,256,128]{2,1,0:T(8,128)(2,1)}, u32[]{:S(2)}) copy-start(bf16[32,256,128]{2,1,0:T(8,128)(2,1)} %t_hbm.1) | copy-start | bytes 6291460
  45.8 0.7 copy-start.3
  52.0 0.8 copy-start.2

commit v3 on v2

--- a/solution.py
+++ b/solution.py
@@ -60,7 +60,7 @@
     one[...] = one_t[...].T
     two[...] = two_ref[...].reshape(R, 128).astype(f32).T
     acc[...] = jnp.zeros_like(acc)
-    own_ref[...] = dot(pick(pos[0], 8, 256), one[...], NN)
+    own_ref[...] = dot(pick(pos[0], 32, 256), one[...], NN)
     for k in range(0, BATCH, 2):
         scaled, error = errors(s_ref[k : k + 2, :], one[...], two, t, k)
         acc[...] += dot(error, scaled, NN)
@@ -83,7 +83,13 @@
 def pair_kernel(pos, pair_ref, out_ref):
     rows = pl.ds(pl.multiple_of(pos[3], 128), 128)
     total = pair_ref[0, rows, :].astype(f32) + pair_ref[1, rows, :].astype(f32)
-    out_ref[...] = total.astype(bf16).reshape(16, 8, R)
+    out_ref[...] = total.astype(bf16).reshape(4, 32, R)
+
+
+def sum_kernel(parts_ref, out_ref):
+    total = jnp.sum(parts_ref[...].astype(f32), axis=0).astype(bf16)
+    for b in range(4):
+        out_ref[b] = total
 
 
 def renew(own, parts):
@@ -94,7 +100,7 @@
 
 def renew_one_kernel(own_ref, parts_ref, out_ref):
     new = renew(own_ref[...], parts_ref[...]).astype(bf16)
-    for b in range(16):
+    for b in range(4):
         out_ref[b] = new
 
 
@@ -135,12 +141,13 @@
 
 
 def body(slices, mode_one, mode_two, slice_table, chosen):
-    yz, c = lax.axis_index(YZ), lax.axis_index("c")
+    y, c = lax.axis_index("y"), lax.axis_index("c")
     n, w = lax.axis_index(NARROW), lax.axis_index(WIDE)
-    pos = jnp.stack([c * 128 + yz * 8, w * 16, n * 8, c * 128]).astype(jnp.int32)
+    pos = jnp.stack([c * 128 + y * 32, w * 16, n * 8, c * 128]).astype(jnp.int32)
 
     one_g = spread(mode_one.T, YZ, 16)
-    two_g = spread(mode_two.T, NARROW, 16)
+    two_g = lax.all_gather(mode_two.T, "x", axis=0)
+    two_g = lax.all_gather(two_g, "zl", axis=0).reshape(16, 32, 128)
     one_hot = (
         chosen[:, None]
         == lax.broadcasted_iota(jnp.int32, (chosen.shape[0], slice_table.shape[0]), 1)
@@ -151,7 +158,7 @@
     t = call(fetch_kernel, [((BATCH, 256, 128), bf16)], [HB], (pltpu.SemaphoreType.DMA((CHUNKS,)),), nbytes=1 << 21)(slices)
     half, own_one = call(
         first_kernel,
-        [((256, R), bf16), ((8, R), f32)],
+        [((256, R), bf16), ((32, R), f32)],
         [SM, VM, VM, VM, VM],
         (pltpu.VMEM((R, 256), bf16), pltpu.VMEM((256, R), bf16), pltpu.VMEM((128, R), f32), pltpu.VMEM((256, R), f32)),
         flops=1 << 31,
@@ -159,10 +166,12 @@
         nbytes=1 << 21,
     )(pos, slice_rows, one_g, two_g, t)
     pair = lax.all_gather(half, "c", axis=0)
-    half = call(pair_kernel, [((16, 8, R), bf16)], [SM, VM])(pos, pair)
-    parts = lax.all_to_all(half, YZ, 0, 0, tiled=True)
-    copies = call(renew_one_kernel, [((16, 8, R), bf16)], [VM, VM])(own_one, parts)
-    new_half = lax.all_to_all(copies, YZ, 0, 0, tiled=True).reshape(128, R)
+    half = call(pair_kernel, [((4, 32, R), bf16)], [SM, VM])(pos, pair)
+    parts = lax.all_to_all(half, "y", 0, 0, tiled=True)
+    sums = call(sum_kernel, [((4, 32, R), bf16)], [VM])(parts)
+    parts = lax.all_to_all(sums, "zh", 0, 0, tiled=True)
+    copies = call(renew_one_kernel, [((4, 32, R), bf16)], [VM, VM])(own_one, parts)
+    new_half = lax.all_to_all(copies, "y", 0, 0, tiled=True).reshape(128, R)
     new_full = lax.all_gather(new_half, "c", axis=0, tiled=True)
 
     partial_two, new_one_t, own_two = call(

time: 131 us -> 131 us (level)
  starting transfers between devices: 7.49 us -> 18.4 us
  blocking collectives: 106 us -> 99.1 us
  local copies, waits for them, and re-layouts: 4.97 us -> 3.54 us
  waiting for transfers between devices: 1.33 us -> 0.01 us
    all_to_all x3, blocking collectives: 71.4 us -> 40.1 us  [the longest x1 23 us: body(): parts = lax.all_to_all(sums, 'zh', 0, 0, tiled=True)]
    all_gather x0 -> x2, blocking collectives: none -> 20.5 us  [the longest x1 10.6 us: body(): two_g = lax.all_gather(two_g, 'zl', axis=0).reshape(16, 32, 128)]
    all_to_all x1, starting transfers between devices: 7.49 us -> 18.4 us  [spread(): return lax.all_to_all(copies, axes, 0, 0, tiled=True)]
    all_gather x1, blocking collectives: 3.25 us -> 7.69 us  [body(): one_g = lax.all_gather(one_g, 'c', axis=0)]
    all_gather x1, blocking collectives: 3.51 us -> 5.74 us  [body(): new_full = lax.all_gather(new_half, 'c', axis=0, tiled=True)]
    all_gather x1, blocking collectives: 4.37 us -> 2.18 us  [body(): pair = lax.all_gather(half, 'c', axis=0)]
    all_to_all x1, waiting for transfers between devices: 1.33 us -> 0.01 us  [spread(): return lax.all_to_all(copies, axes, 0, 0, tiled=True)]
    pallas_call x3 -> x4, Pallas kernels: 4.01 us -> 4.04 us  [the longest x1 3.33 us: body(): call(first_kernel, [((256, R), bf16), ((32, R), f32)], [SM, VM, VM, VM, V...]
  transfers between devices with their start and end apart: 1 -> 1, of which waited for: 1 -> 0; matrix products, arithmetic and copies ran while one was open for 1% -> 0% of each run, Pallas kernels for 0% -> 0%
where the time goes in v3:
time: 131 us
  blocking collectives  99.1 us (76%)
  starting transfers between devices  18.4 us (14%)
  Pallas kernels  8.72 us (7%)
  local copies, waits for them, and re-layouts  3.54 us (3%)
    all_to_all x1, blocking collectives, body(): parts = lax.all_to_all(sums, 'zh', 0, 0, tiled=True)  23 us
    all_to_all x1, starting transfers between devices, spread(): return lax.all_to_all(copies, axes, 0, 0, tiled=True)  18.4 us
    all_to_all x1, blocking collectives, body(): parts_two = lax.all_to_all(partial_two, NARROW, 0, 0, tiled=True)  12.4 us
    all_gather x1, blocking collectives, body(): two_g = lax.all_gather(two_g, 'zl', axis=0).reshape(16, 32, 128)  10.6 us
    all_to_all x1, blocking collectives, body(): blocks = lax.all_to_all(blocks, NARROW, 0, 0, tiled=True)  10.5 us
    all_gather x1, blocking collectives, body(): two_g = lax.all_gather(mode_two.T, 'x', axis=0)  9.88 us
    all_to_all x1, blocking collectives, body(): parts = lax.all_to_all(half, 'y', 0, 0, tiled=True)  9.08 us
    all_to_all x1, blocking collectives, body(): new_half = lax.all_to_all(copies, 'y', 0, 0, tiled=True).reshape(128, R)  8.05 us
  transfers between devices with their start and end apart: 1, of which 0 were waited for; matrix products, arithmetic and copies ran while one was open for 0% of the time, Pallas kernels for 0%

profile of v3, /device:TPU:1, one launch (start us, length us, event | category | flops | bytes accessed | tf_op | source)
XLA Modules:
  0.0 130.9 jit_solution(7436374278074873815)
XLA Ops:
  0.6 0.0 copy-start
  0.6 1.4 %broadcast_in_dim.2 = bf16[16,16,256]{2,1,0:T(8,128)(2,1)} broadcast(bf16[16,256]{1,0:T(8,128)(2,1)} %bitcast.17), dimensions={1,2} | broadcast | bytes 139264 | tf_op jit(solution)/shard_map/broadcast_in_dim | solution.py:139
  2.1 18.4 %all-to-all-start = ((bf16[16,16,256]{2,1,0:T(8,128)(2,1)}), bf16[16,16,256]{2,1,0:T(8,128)(2,1)S(1)}, u32[]{:S(2)}, u32[]{:S(2)}) async-start(bf16[16,16,256]{2,1,0:T(8,128)(2,1)} %broadcast_in_dim.2), calls=%async_computation | async-start | bytes 262144 | tf_op jit(solution)/shard_map/all_to_all | solution.py:140
  20.5 0.0 copy-start.1
  20.5 1.6 %copy-done.1 = bf16[32,256,128]{2,1,0:T(8,128)(2,1)S(1)} copy-done((bf16[32,256,128]{2,1,0:T(8,128)(2,1)S(1)}, bf16[32,256,128]{2,1,0:T(8,128)(2,1)}, u32[]{:S(2)}) %copy-start.1) | copy-done | bytes 2097176
  22.1 0.0 copy-start.2
  22.1 0.0 copy-start.3
  22.1 0.2 shard_map.68.t
  22.3 0.5 copy-done.2
  22.8 9.9 %all-gather.1 = bf16[128,128]{1,0:T(8,128)(2,1)S(1)} all-gather(bf16[32,128]{1,0:T(8,128)(2,1)S(1)} %bitcast.18), channel_id=3, replica_groups=mesh['zl'=4,'x'=4,'y'=4,'zh'=4,'c'=2] {'x'}, dimensions={0}, use_global_device_ids=true | all-gather | bytes 40960 | tf_op jit(solution)/shard_map/all_gather | solution.py:149
  32.6 10.6 %all-gather.2.two_ref = bf16[16,32,128]{2,1,0:T(8,128)(2,1)S(1)} all-gather(bf16[4,32,128]{2,1,0:T(8,128)(2,1)S(1)} %bitcast.16), channel_id=4, replica_groups=mesh['zl'=4,'x'=4,'y'=4,'zh'=4,'c'=2] {'zl'}, dimensions={0}, use_global_device_ids=true | all-gather | bytes 163840 | tf_op jit(solution)/shard_map/all_gather | solution.py:150
  43.3 0.1 pad_add_fusion.pos
  43.3 0.0 copy-done
  43.3 0.0 copy-done.3
  43.3 0.3 fusion.s_ref
  43.7 0.0 all-to-all-done
  43.7 7.7 %all-gather = bf16[32,16,256]{2,1,0:T(8,128)(2,1)S(1)} all-gather(bf16[16,16,256]{2,1,0:T(8,128)(2,1)S(1)} %all-to-all-done), channel_id=2, replica_groups=mesh['zl'=4,'x'=4,'y'=4,'zh'=4,'c'=2] {'c'}, dimensions={0}, use_global_device_ids=true | all-gather | bytes 393216 | tf_op jit(solution)/shard_map/all_gather | solution.py:156
  51.4 3.3 %shard_map.69 = (bf16[256,512]{1,0:T(8,128)(2,1)S(1)}, f32[32,512]{1,0:T(8,128)S(1)}) custom-call(s32[4]{0:T(128)S(1)} %pad_add_fusion.pos, f32[32,512]{1,0:T(8,128)S(1)} %fusion.s_ref, bf16[2,16,16,256]{3,2,1,0:T(8,128)(2,1)S(1)} %bitcast.14, bf16[16,32,128]{2,1,0:T(8,128)(2,1)S(1)} %all-gather.2.two_ref, bf16[32,256,128]{2,1,0:T(8,128)(2,1)S(1)} %shard_map.68.t), custom_call_target="tpu_custom_call" | custom-call | flops 2147483648 | bytes 2097152 | tf_op jit(solution)/shard_map/pallas_call | solution.py:159
  54.7 2.2 %all-gather.3 = bf16[512,512]{1,0:T(8,128)(2,1)S(1)} all-gather(bf16[256,512]{1,0:T(8,128)(2,1)S(1)} %get-tuple-element.8), channel_id=5, replica_groups=mesh['zl'=4,'x'=4,'y'=4,'zh'=4,'c'=2] {'c'}, dimensions={0}, use_global_device_ids=true | all-gather | bytes 786432 | tf_op jit(solution)/shard_map/all_gather | solution.py:168
  56.9 0.6 shard_map.70
  57.5 9.1 %all_to_all.30.parts_ref = bf16[4,32,512]{2,1,0:T(8,128)(2,1)S(1)} all-to-all(bf16[4,32,512]{2,1,0:T(8,128)(2,1)S(1)} %shard_map.70), channel_id=1, replica_groups=mesh['zl'=4,'x'=4,'y'=4,'zh'=4,'c'=2] {'y'}, dimensions={0} | all-to-all | bytes 262144 | tf_op jit(solution)/shard_map/all_to_all | solution.py:170
  66.6 23.0 %all_to_all.31.parts_ref = bf16[4,32,512]{2,1,0:T(8,128)(2,1)S(1)} all-to-all(bf16[4,32,512]{2,1,0:T(8,128)(2,1)S(1)} %shard_map.71), channel_id=1, replica_groups=mesh['zl'=4,'x'=4,'y'=4,'zh'=4,'c'=2] {'zh'}, dimensions={0} | all-to-all | bytes 262144 | tf_op jit(solution)/shard_map/all_to_all | solution.py:172
  89.5 0.1 shard_map.72
  89.7 8.0 %all_to_all.32 = bf16[4,32,512]{2,1,0:T(8,128)(2,1)S(1)} all-to-all(bf16[4,32,512]{2,1,0:T(8,128)(2,1)S(1)} %shard_map.72), channel_id=1, replica_groups=mesh['zl'=4,'x'=4,'y'=4,'zh'=4,'c'=2] {'y'}, dimensions={0} | all-to-all | bytes 262144 | tf_op jit(solution)/shard_map/all_to_all | solution.py:174
  97.7 5.7 %all_gather.35.new_ref = bf16[256,512]{1,0:T(8,128)(2,1)S(1)} all-gather(bf16[128,512]{1,0:T(8,128)(2,1)S(1)} %bitcast.15), channel_id=1, replica_groups=mesh['zl'=4,'x'=4,'y'=4,'zh'=4,'c'=2] {'c'}, dimensions={0}, use_global_device_ids=true | all-gather | bytes 393216 | tf_op jit(solution)/shard_map/all_gather | solution.py:175
  103.5 3.6 %shard_map.73 = (bf16[16,8,512]{2,1,0:T(8,128)(2,1)S(1)}, bf16[16,256]{1,0:T(8,128)(2,1)}, f32[8,512]{1,0:T(8,128)S(1)}) custom-call(s32[4]{0:T(128)S(1)} %pad_add_fusion.pos, f32[32,512]{1,0:T(8,128)S(1)} %fusion.s_ref, bf16[256,512]{1,0:T(8,128)(2,1)S(1)} %all_gather.35.new_ref, bf16[16,32,128]{2,1,0:T(8,128)(2,1)S(1)} %all-gather.2.two_ref, ...), custom_call_target="tpu_custom_call" | custom-call | flops 2147483648 | bytes 2097152 | tf_op jit(solution)/shard_map/pallas_call | solution.py:177
  107.1 12.4 %all_to_all.33.parts_ref = bf16[16,8,512]{2,1,0:T(8,128)(2,1)S(1)} all-to-all(bf16[16,8,512]{2,1,0:T(8,128)(2,1)S(1)} %get-tuple-element.11), channel_id=1, replica_groups=mesh['zl'=4,'x'=4,'y'=4,'zh'=4,'c'=2] {'zl','x'}, dimensions={0} | all-to-all | bytes 262144 | tf_op jit(solution)/shard_map/all_to_all | solution.py:186
  119.5 0.2 shard_map.74
  119.7 10.5 %all_to_all.34.in_ref = bf16[16,8,128]{2,1,0:T(8,128)(2,1)S(1)} all-to-all(bf16[16,8,128]{2,1,0:T(8,128)(2,1)S(1)} %shard_map.74), channel_id=1, replica_groups=mesh['zl'=4,'x'=4,'y'=4,'zh'=4,'c'=2] {'zl','x'}, dimensions={0} | all-to-all | bytes 65536 | tf_op jit(solution)/shard_map/all_to_all | solution.py:188
  130.2 0.7 shard_map.75
  (1 shorter events, 0.0 us)
Async XLA Ops:
  0.6 42.7 %copy-start = (bf16[1024,512]{1,0:T(8,128)(2,1)S(1)}, bf16[1024,512]{1,0:T(8,128)(2,1)}, u32[]{:S(2)}) copy-start(bf16[1024,512]{1,0:T(8,128)(2,1)} %param.8) | copy-start | bytes 3145732
  2.1 41.6 %all-to-all-start = ((bf16[16,16,256]{2,1,0:T(8,128)(2,1)}), bf16[16,16,256]{2,1,0:T(8,128)(2,1)S(1)}, u32[]{:S(2)}, u32[]{:S(2)}) async-start(bf16[16,16,256]{2,1,0:T(8,128)(2,1)} %broadcast_in_dim.2), calls=%async_computation | async-start | bytes 262144 | tf_op jit(solution)/shard_map/all_to_all | solution.py:140
  20.5 1.6 %copy-start.1 = (bf16[32,256,128]{2,1,0:T(8,128)(2,1)S(1)}, bf16[32,256,128]{2,1,0:T(8,128)(2,1)}, u32[]{:S(2)}) copy-start(bf16[32,256,128]{2,1,0:T(8,128)(2,1)} %t_hbm.1) | copy-start | bytes 6291460
  22.1 0.7 copy-start.2
  22.1 21.3 %copy-start.3 = (s32[32]{0:T(128)S(1)}, s32[32]{0:T(128)}, u32[]{:S(2)}) copy-start(s32[32]{0:T(128)} %param.9) | copy-start | bytes 388

commit v4 on v3

--- a/solution.py
+++ b/solution.py
@@ -11,9 +11,9 @@
 epsilon = 1e-06
 step_size = 0.5
 
-YZ = ("y", "zh")
 NARROW = ("zl", "x")
 WIDE = ("y", "zh", "c")
+ALL = ("zl", "x", "y", "zh", "c")
 bf16 = jnp.bfloat16
 f32 = jnp.float32
 
@@ -53,12 +53,14 @@
     return scaled, jnp.tanh(model - target).astype(bf16)
 
 
-def first_kernel(pos, s_ref, one_ref, two_ref, t, out_ref, own_ref, one_t, one, two, acc):
+def first_kernel(pos, s_ref, both_ref, t, out_ref, own_ref, two_ref, one, two_t, two, acc):
+    one[...] = both_ref[0].reshape(R, 256).T
     for b in range(16):
-        for c in range(2):
-            one_t[pl.ds(32 * b + 16 * c, 16), :] = one_ref[c, b]
-    one[...] = one_t[...].T
-    two[...] = two_ref[...].reshape(R, 128).astype(f32).T
+        block = both_ref[1, b, pos[4]]
+        two_t[pl.ds(32 * b, 16), :] = block[:, :128]
+        two_t[pl.ds(32 * b + 16, 16), :] = block[:, 128:]
+    two[...] = two_t[...].astype(f32).T
+    two_ref[...] = two[...]
     acc[...] = jnp.zeros_like(acc)
     own_ref[...] = dot(pick(pos[0], 32, 256), one[...], NN)
     for k in range(0, BATCH, 2):
@@ -67,8 +69,7 @@
     out_ref[...] = acc[...].astype(bf16)
 
 
-def second_kernel(pos, s_ref, new_ref, two_ref, t, out_ref, block_ref, own_ref, two, acc):
-    two[...] = two_ref[...].reshape(R, 128).astype(f32).T
+def second_kernel(pos, s_ref, new_ref, two, t, out_ref, block_ref, own_ref, acc):
     acc[...] = jnp.zeros_like(acc)
     block_ref[...] = dot(pick(pos[1], 16, R), new_ref[...], NT).astype(bf16)
     own_ref[...] = dot(pick(pos[2], 8, 128), two[...].astype(bf16), NN)
@@ -78,6 +79,12 @@
         both = dot(error, new_ref[...], TN)
         acc[...] += both[:128] * s[0:1] + both[128:] * s[1:2]
     out_ref[...] = acc[...].astype(bf16).reshape(16, 8, R)
+
+
+def pack_kernel(one_ref, two_ref, out_ref):
+    out_ref[0] = one_ref[...]
+    out_ref[1, :, :128] = two_ref[:16]
+    out_ref[1, :, 128:] = two_ref[16:]
 
 
 def pair_kernel(pos, pair_ref, out_ref):
@@ -135,36 +142,38 @@
     )
 
 
-def spread(block, axes, count):
-    copies = jnp.broadcast_to(block[None], (count,) + block.shape)
-    return lax.all_to_all(copies, axes, 0, 0, tiled=True)
+def groups():
+    device = lambda n, yz, c: (n * 16 + yz) * 2 + c
+    first = [[device(n, yz, 0) for yz in range(16)] for n in range(16)]
+    second = [[device(n, yz, 1) for n in range(16)] for yz in range(16)]
+    return first + second
 
 
 def body(slices, mode_one, mode_two, slice_table, chosen):
     y, c = lax.axis_index("y"), lax.axis_index("c")
     n, w = lax.axis_index(NARROW), lax.axis_index(WIDE)
-    pos = jnp.stack([c * 128 + y * 32, w * 16, n * 8, c * 128]).astype(jnp.int32)
-
-    one_g = spread(mode_one.T, YZ, 16)
-    two_g = lax.all_gather(mode_two.T, "x", axis=0)
-    two_g = lax.all_gather(two_g, "zl", axis=0).reshape(16, 32, 128)
+    pos = jnp.stack([c * 128 + y * 32, w * 16, n * 8, c * 128, c]).astype(jnp.int32)
+
+    mine = call(pack_kernel, [((2, 16, 256), bf16)], [VM, VM])(mode_one.T, mode_two.T)
+    mine = lax.all_to_all(mine, "c", 0, 0, tiled=True)
+    mine = jnp.broadcast_to(mine[None], (16, 2, 16, 256))
+    both = lax.all_to_all(mine, ALL, 0, 0, axis_index_groups=groups(), tiled=True)
     one_hot = (
         chosen[:, None]
         == lax.broadcasted_iota(jnp.int32, (chosen.shape[0], slice_table.shape[0]), 1)
     ).astype(bf16)
     slice_rows = jnp.dot(one_hot, slice_table, preferred_element_type=f32)
-    one_g = lax.all_gather(one_g, "c", axis=0)
-
+    both = lax.all_gather(both, "c", axis=0)
     t = call(fetch_kernel, [((BATCH, 256, 128), bf16)], [HB], (pltpu.SemaphoreType.DMA((CHUNKS,)),), nbytes=1 << 21)(slices)
-    half, own_one = call(
+    half, own_one, two = call(
         first_kernel,
-        [((256, R), bf16), ((32, R), f32)],
-        [SM, VM, VM, VM, VM],
-        (pltpu.VMEM((R, 256), bf16), pltpu.VMEM((256, R), bf16), pltpu.VMEM((128, R), f32), pltpu.VMEM((256, R), f32)),
+        [((256, R), bf16), ((32, R), f32), ((128, R), f32)],
+        [SM, VM, VM, VM],
+        (pltpu.VMEM((256, R), bf16), pltpu.VMEM((R, 128), bf16), pltpu.VMEM((128, R), f32), pltpu.VMEM((256, R), f32)),
         flops=1 << 31,
         vmem=16,
         nbytes=1 << 21,
-    )(pos, slice_rows, one_g, two_g, t)
+    )(pos, slice_rows, both, t)
     pair = lax.all_gather(half, "c", axis=0)
     half = call(pair_kernel, [((4, 32, R), bf16)], [SM, VM])(pos, pair)
     parts = lax.all_to_all(half, "y", 0, 0, tiled=True)
@@ -178,11 +187,11 @@
         second_kernel,
         [((16, 8, R), bf16), ((16, 256), bf16), ((8, R), f32)],
         [SM, VM, VM, VM, VM],
-        (pltpu.VMEM((128, R), f32), pltpu.VMEM((128, R), f32)),
+        (pltpu.VMEM((128, R), f32),),
         flops=1 << 31,
         vmem=16,
         nbytes=1 << 21,
-    )(pos, slice_rows, new_full, two_g, t)
+    )(pos, slice_rows, new_full, two, t)
     parts_two = lax.all_to_all(partial_two, NARROW, 0, 0, tiled=True)
     blocks = call(renew_two_kernel, [((16, 8, 128), bf16)], [VM, VM])(own_two, parts_two)
     blocks = lax.all_to_all(blocks, NARROW, 0, 0, tiled=True)

time: 131 us -> 118 us (0.901)
  starting transfers between devices: 18.4 us -> 3.53 us
  waiting for transfers between devices: 0.01 us -> 6.22 us
  blocking collectives: 99.1 us -> 93.4 us
    all_to_all x1, starting transfers between devices: 18.4 us -> 3.53 us  [body(): lax.all_to_all(mine, ALL, 0, 0, axis_index_groups=groups(), tiled=True)]
    all_to_all x0 -> x1, blocking collectives: none -> 10.2 us  [body(): mine = lax.all_to_all(mine, 'c', 0, 0, tiled=True)]
    all_gather x3 -> x1, blocking collectives: 28.2 us -> 20.5 us  [body(): both = lax.all_gather(both, 'c', axis=0)]
    all_to_all x1, blocking collectives: 23 us -> 15.9 us  [body(): parts = lax.all_to_all(sums, 'zh', 0, 0, tiled=True)]
    all_to_all x1, waiting for transfers between devices: 0.01 us -> 6.22 us  [body(): lax.all_to_all(mine, ALL, 0, 0, axis_index_groups=groups(), tiled=True)]
    all_to_all x1, blocking collectives: 9.08 us -> 7.23 us  [body(): parts = lax.all_to_all(half, 'y', 0, 0, tiled=True)]
    unnamed x8 -> x10, local copies, waits for them, and re-layouts: 2.09 us -> 3.43 us
    pallas_call x1 -> x2, Pallas kernels: 3.33 us -> 3.34 us  [the longest x1 3.34 us: body(): call(first_kernel, [((256, R), bf16), ((32, R), f32), ((128, R), f32)], [...]
  transfers between devices with their start and end apart: 1 -> 1, of which waited for: 0 -> 1; matrix products, arithmetic and copies ran while one was open for 0% -> 0% of each run, Pallas kernels for 0% -> 0%
where the time goes in v4:
time: 118 us; the launch traced here: 117 us
  blocking collectives  93.4 us (79%)
  Pallas kernels  8.79 us (7%)
  waiting for transfers between devices  6.22 us (5%)
  local copies, waits for them, and re-layouts  4.24 us (4%)
  starting transfers between devices  3.53 us (3%)
    all_gather x1, blocking collectives, body(): both = lax.all_gather(both, 'c', axis=0)  20.5 us
    all_to_all x1, blocking collectives, body(): parts = lax.all_to_all(sums, 'zh', 0, 0, tiled=True)  15.9 us
    all_to_all x1, blocking collectives, body(): parts_two = lax.all_to_all(partial_two, NARROW, 0, 0, tiled=True)  13 us
    all_to_all x1, blocking collectives, body(): blocks = lax.all_to_all(blocks, NARROW, 0, 0, tiled=True)  10.5 us
    all_to_all x1, blocking collectives, body(): mine = lax.all_to_all(mine, 'c', 0, 0, tiled=True)  10.2 us
    all_to_all x1, blocking collectives, body(): parts = lax.all_to_all(half, 'y', 0, 0, tiled=True)  7.23 us
    all_to_all x1, blocking collectives, body(): new_half = lax.all_to_all(copies, 'y', 0, 0, tiled=True).reshape(128, R)  7.21 us
    all_gather x1, blocking collectives, body(): new_full = lax.all_gather(new_half, 'c', axis=0, tiled=True)  6.74 us
  transfers between devices with their start and end apart: 1, of which 1 were waited for; matrix products, arithmetic and copies ran while one was open for 0% of the time, Pallas kernels for 0%

profile of v4, /device:TPU:1, one launch (start us, length us, event | category | flops | bytes accessed | tf_op | source)
XLA Modules:
  0.0 117.2 jit_solution(16522197671652097394)
XLA Ops:
  0.6 0.0 copy-start
  0.6 0.0 copy-start.2
  0.7 0.8 copy-done.2
  1.4 0.0 copy-start.3
  1.4 0.7 copy-done.3
  2.1 10.2 %all_to_all.35 = bf16[2,16,256]{2,1,0:T(8,128)(2,1)S(1)} all-to-all(bf16[2,16,256]{2,1,0:T(8,128)(2,1)S(1)} %shard_map.68), channel_id=1, replica_groups=mesh['zl'=4,'x'=4,'y'=4,'zh'=4,'c'=2] {'c'}, dimensions={0} | all-to-all | bytes 32768 | tf_op jit(solution)/shard_map/all_to_all | solution.py:158
  12.3 0.7 broadcast_in_dim.2
  13.1 3.5 %all-to-all-start.1 = ((bf16[16,2,16,256]{3,2,1,0:T(8,128)(2,1)}), bf16[16,2,16,256]{3,2,1,0:T(8,128)(2,1)S(1)}, u32[]{:S(2)}, u32[]{:S(2)}) async-start(bf16[16,2,16,256]{3,2,1,0:T(8,128)(2,1)} %broadcast_in_dim.2), calls=%async_computation.1 | async-start | bytes 524288 | tf_op jit(solution)/shard_map/all_to_all | solution.py:160
  16.6 0.0 copy-start.1
  16.6 1.6 %copy-done.1 = bf16[32,256,128]{2,1,0:T(8,128)(2,1)S(1)} copy-done((bf16[32,256,128]{2,1,0:T(8,128)(2,1)S(1)}, bf16[32,256,128]{2,1,0:T(8,128)(2,1)}, u32[]{:S(2)}) %copy-start.1) | copy-done | bytes 2097176
  18.2 0.0 copy-start.4
  18.2 0.2 shard_map.69.t
  18.4 0.1 stack.23.pos
  18.5 0.0 copy-done
  18.5 0.4 copy-done.4
  18.9 0.3 fusion.s_ref
  19.2 6.2 %all-to-all-done.1 = bf16[16,2,16,256]{3,2,1,0:T(8,128)(2,1)S(1)} async-done(((bf16[16,2,16,256]{3,2,1,0:T(8,128)(2,1)}), bf16[16,2,16,256]{3,2,1,0:T(8,128)(2,1)S(1)}, u32[]{:S(2)}, u32[]{:S(2)}) %all-to-all-start.1) | async-done | bytes 262176 | tf_op jit(solution)/shard_map/all_to_all | solution.py:160
  25.4 20.5 %all-gather = bf16[32,2,16,256]{3,2,1,0:T(8,128)(2,1)S(1)} all-gather(bf16[16,2,16,256]{3,2,1,0:T(8,128)(2,1)S(1)} %all-to-all-done.1), channel_id=2, replica_groups=mesh['zl'=4,'x'=4,'y'=4,'zh'=4,'c'=2] {'c'}, dimensions={0}, use_global_device_ids=true | all-gather | bytes 786432 | tf_op jit(solution)/shard_map/all_gather | solution.py:166
  45.8 3.3 %shard_map.70 = (bf16[256,512]{1,0:T(8,128)(2,1)S(1)}, f32[32,512]{1,0:T(8,128)S(1)}, f32[128,512]{1,0:T(8,128)S(1)}) custom-call(s32[5]{0:T(128)S(1)} %stack.23.pos, f32[32,512]{1,0:T(8,128)S(1)} %fusion.s_ref, bf16[2,16,2,16,256]{4,3,2,1,0:T(8,128)(2,1)S(1)} %bitcast.14, bf16[32,256,128]{2,1,0:T(8,128)(2,1)S(1)} %shard_map.69.t), custom_call_target="tpu_custom_call" | custom-call | flops 2147483648 | bytes 2097152 | tf_op jit(solution)/shard_map/pallas_call | solution.py:168
  49.2 2.2 %all-gather.1 = bf16[512,512]{1,0:T(8,128)(2,1)S(1)} all-gather(bf16[256,512]{1,0:T(8,128)(2,1)S(1)} %get-tuple-element.9), channel_id=3, replica_groups=mesh['zl'=4,'x'=4,'y'=4,'zh'=4,'c'=2] {'c'}, dimensions={0}, use_global_device_ids=true | all-gather | bytes 786432 | tf_op jit(solution)/shard_map/all_gather | solution.py:177
  51.4 0.6 shard_map.71
  52.0 7.2 %all_to_all.36.parts_ref = bf16[4,32,512]{2,1,0:T(8,128)(2,1)S(1)} all-to-all(bf16[4,32,512]{2,1,0:T(8,128)(2,1)S(1)} %shard_map.71), channel_id=1, replica_groups=mesh['zl'=4,'x'=4,'y'=4,'zh'=4,'c'=2] {'y'}, dimensions={0} | all-to-all | bytes 262144 | tf_op jit(solution)/shard_map/all_to_all | solution.py:179
  59.2 15.9 %all_to_all.37.parts_ref = bf16[4,32,512]{2,1,0:T(8,128)(2,1)S(1)} all-to-all(bf16[4,32,512]{2,1,0:T(8,128)(2,1)S(1)} %shard_map.72), channel_id=1, replica_groups=mesh['zl'=4,'x'=4,'y'=4,'zh'=4,'c'=2] {'zh'}, dimensions={0} | all-to-all | bytes 262144 | tf_op jit(solution)/shard_map/all_to_all | solution.py:181
  75.1 0.1 shard_map.73
  75.2 7.2 %all_to_all.38 = bf16[4,32,512]{2,1,0:T(8,128)(2,1)S(1)} all-to-all(bf16[4,32,512]{2,1,0:T(8,128)(2,1)S(1)} %shard_map.73), channel_id=1, replica_groups=mesh['zl'=4,'x'=4,'y'=4,'zh'=4,'c'=2] {'y'}, dimensions={0} | all-to-all | bytes 262144 | tf_op jit(solution)/shard_map/all_to_all | solution.py:183
  82.4 6.7 %all_gather.19.new_ref = bf16[256,512]{1,0:T(8,128)(2,1)S(1)} all-gather(bf16[128,512]{1,0:T(8,128)(2,1)S(1)} %bitcast.17), channel_id=1, replica_groups=mesh['zl'=4,'x'=4,'y'=4,'zh'=4,'c'=2] {'c'}, dimensions={0}, use_global_device_ids=true | all-gather | bytes 393216 | tf_op jit(solution)/shard_map/all_gather | solution.py:184
  89.1 3.7 %shard_map.74 = (bf16[16,8,512]{2,1,0:T(8,128)(2,1)S(1)}, bf16[16,256]{1,0:T(8,128)(2,1)}, f32[8,512]{1,0:T(8,128)S(1)}) custom-call(s32[5]{0:T(128)S(1)} %stack.23.pos, f32[32,512]{1,0:T(8,128)S(1)} %fusion.s_ref, bf16[256,512]{1,0:T(8,128)(2,1)S(1)} %all_gather.19.new_ref, f32[128,512]{1,0:T(8,128)S(1)} %get-tuple-element.10.two, ...), custom_call_target="tpu_custom_call" | custom-call | flops 2147483648 | bytes 2097152 | tf_op jit(solution)/shard_map/pallas_call | solution.py:186
  92.8 13.0 %all_to_all.39.parts_ref = bf16[16,8,512]{2,1,0:T(8,128)(2,1)S(1)} all-to-all(bf16[16,8,512]{2,1,0:T(8,128)(2,1)S(1)} %get-tuple-element.13), channel_id=1, replica_groups=mesh['zl'=4,'x'=4,'y'=4,'zh'=4,'c'=2] {'zl','x'}, dimensions={0} | all-to-all | bytes 262144 | tf_op jit(solution)/shard_map/all_to_all | solution.py:195
  105.8 0.2 shard_map.75
  106.0 10.5 %all_to_all.40.in_ref = bf16[16,8,128]{2,1,0:T(8,128)(2,1)S(1)} all-to-all(bf16[16,8,128]{2,1,0:T(8,128)(2,1)S(1)} %shard_map.75), channel_id=1, replica_groups=mesh['zl'=4,'x'=4,'y'=4,'zh'=4,'c'=2] {'zl','x'}, dimensions={0} | all-to-all | bytes 65536 | tf_op jit(solution)/shard_map/all_to_all | solution.py:197
  116.5 0.7 shard_map.76
  (2 shorter events, 0.0 us)
Async XLA Ops:
  0.6 17.9 %copy-start = (bf16[1024,512]{1,0:T(8,128)(2,1)S(1)}, bf16[1024,512]{1,0:T(8,128)(2,1)}, u32[]{:S(2)}) copy-start(bf16[1024,512]{1,0:T(8,128)(2,1)} %param.8) | copy-start | bytes 3145732
  0.6 0.8 copy-start.2
  1.4 0.7 copy-start.3
  13.1 12.3 %all-to-all-start.1 = ((bf16[16,2,16,256]{3,2,1,0:T(8,128)(2,1)}), bf16[16,2,16,256]{3,2,1,0:T(8,128)(2,1)S(1)}, u32[]{:S(2)}, u32[]{:S(2)}) async-start(bf16[16,2,16,256]{3,2,1,0:T(8,128)(2,1)} %broadcast_in_dim.2), calls=%async_computation.1 | async-start | bytes 524288 | tf_op jit(solution)/shard_map/all_to_all | solution.py:160
  16.6 1.6 %copy-start.1 = (bf16[32,256,128]{2,1,0:T(8,128)(2,1)S(1)}, bf16[32,256,128]{2,1,0:T(8,128)(2,1)}, u32[]{:S(2)}) copy-start(bf16[32,256,128]{2,1,0:T(8,128)(2,1)} %t_hbm.1) | copy-start | bytes 6291460
  18.2 0.7 copy-start.4

commit v5 on v4

--- a/solution.py
+++ b/solution.py
@@ -32,6 +32,13 @@
     col = lax.broadcasted_iota(jnp.int32, (count, total), 1)
     row = lax.broadcasted_iota(jnp.int32, (count, total), 0)
     return (col == row + first).astype(bf16)
+
+
+def errors(s, left, two, t, k):
+    scaled = jnp.concatenate([two[...] * s[0:1], two[...] * s[1:2]], axis=0).astype(bf16)
+    model = dot(left, scaled, NT)
+    target = jnp.concatenate([t[k], t[k + 1]], axis=1).astype(f32)
+    return scaled, jnp.tanh(model - target).astype(bf16)
 
 
 def fetch_kernel(t_hbm, t, sems):
@@ -46,20 +53,13 @@
         copy.wait()
 
 
-def errors(s, left, two, t, k):
-    scaled = jnp.concatenate([two[...] * s[0:1], two[...] * s[1:2]], axis=0).astype(bf16)
-    model = dot(left, scaled, NT)
-    target = jnp.concatenate([t[k], t[k + 1]], axis=1).astype(f32)
-    return scaled, jnp.tanh(model - target).astype(bf16)
-
-
-def first_kernel(pos, s_ref, both_ref, t, out_ref, own_ref, two_ref, one, two_t, two, acc):
-    one[...] = both_ref[0].reshape(R, 256).T
+def first_kernel(pos, s_ref, both_ref, t, out_ref, own_ref, two_ref, one_t, one, two, acc):
     for b in range(16):
-        block = both_ref[1, b, pos[4]]
-        two_t[pl.ds(32 * b, 16), :] = block[:, :128]
-        two_t[pl.ds(32 * b + 16, 16), :] = block[:, 128:]
-    two[...] = two_t[...].astype(f32).T
+        for c in range(2):
+            for h in range(2):
+                one_t[pl.ds(32 * b + 16 * c, 16), pl.ds(128 * h, 128)] = both_ref[1, b, c, pl.ds(16 * h, 16), :]
+    one[...] = one_t[...].T
+    two[...] = both_ref[0, :, pos[4]].reshape(R, 128).astype(f32).T
     two_ref[...] = two[...]
     acc[...] = jnp.zeros_like(acc)
     own_ref[...] = dot(pick(pos[0], 32, 256), one[...], NN)
@@ -81,10 +81,12 @@
     out_ref[...] = acc[...].astype(bf16).reshape(16, 8, R)
 
 
-def pack_kernel(one_ref, two_ref, out_ref):
-    out_ref[0] = one_ref[...]
-    out_ref[1, :, :128] = two_ref[:16]
-    out_ref[1, :, 128:] = two_ref[16:]
+def spread_kernel(pos, blocks_ref, out_ref):
+    kind = pos[4]
+    for c in range(2):
+        block = blocks_ref[c, kind]
+        for b in range(16):
+            out_ref[b, c] = block
 
 
 def pair_kernel(pos, pair_ref, out_ref):
@@ -144,8 +146,8 @@
 
 def groups():
     device = lambda n, yz, c: (n * 16 + yz) * 2 + c
-    first = [[device(n, yz, 0) for yz in range(16)] for n in range(16)]
-    second = [[device(n, yz, 1) for n in range(16)] for yz in range(16)]
+    first = [[device(n, yz, 1) for yz in range(16)] for n in range(16)]
+    second = [[device(n, yz, 0) for n in range(16)] for yz in range(16)]
     return first + second
 
 
@@ -154,22 +156,22 @@
     n, w = lax.axis_index(NARROW), lax.axis_index(WIDE)
     pos = jnp.stack([c * 128 + y * 32, w * 16, n * 8, c * 128, c]).astype(jnp.int32)
 
-    mine = call(pack_kernel, [((2, 16, 256), bf16)], [VM, VM])(mode_one.T, mode_two.T)
-    mine = lax.all_to_all(mine, "c", 0, 0, tiled=True)
-    mine = jnp.broadcast_to(mine[None], (16, 2, 16, 256))
+    one_t = mode_one.T
+    blocks = jnp.concatenate([mode_two.T, one_t[:, :128], one_t[:, 128:]], axis=0)
+    blocks = lax.all_gather(blocks, "c", axis=0).reshape(2, 2, 32, 128)
+    mine = call(spread_kernel, [((16, 2, 32, 128), bf16)], [SM, VM])(pos, blocks)
     both = lax.all_to_all(mine, ALL, 0, 0, axis_index_groups=groups(), tiled=True)
+    both = lax.all_gather(both, "c", axis=0)
     one_hot = (
-        chosen[:, None]
-        == lax.broadcasted_iota(jnp.int32, (chosen.shape[0], slice_table.shape[0]), 1)
+        chosen[:, None] == lax.broadcasted_iota(jnp.int32, (chosen.shape[0], slice_table.shape[0]), 1)
     ).astype(bf16)
     slice_rows = jnp.dot(one_hot, slice_table, preferred_element_type=f32)
-    both = lax.all_gather(both, "c", axis=0)
     t = call(fetch_kernel, [((BATCH, 256, 128), bf16)], [HB], (pltpu.SemaphoreType.DMA((CHUNKS,)),), nbytes=1 << 21)(slices)
     half, own_one, two = call(
         first_kernel,
         [((256, R), bf16), ((32, R), f32), ((128, R), f32)],
         [SM, VM, VM, VM],
-        (pltpu.VMEM((256, R), bf16), pltpu.VMEM((R, 128), bf16), pltpu.VMEM((128, R), f32), pltpu.VMEM((256, R), f32)),
+        (pltpu.VMEM((R, 256), bf16), pltpu.VMEM((256, R), bf16), pltpu.VMEM((128, R), f32), pltpu.VMEM((256, R), f32)),
         flops=1 << 31,
         vmem=16,
         nbytes=1 << 21,

time: 118 us -> 115 us (0.975)
  blocking collectives: 93.4 us -> 73.2 us
  starting transfers between devices: 3.53 us -> 12.2 us
  waiting for transfers between devices: 6.22 us -> 14.4 us
  Pallas kernels: 8.79 us -> 10.2 us
  local copies, waits for them, and re-layouts: 4.24 us -> 2.92 us
    all_gather x1, blocking collectives: 20.5 us -> 2.17 us  [body(): both = lax.all_gather(both, 'c', axis=0)]
    all_to_all x1 -> x0, blocking collectives: 10.2 us -> none  [body(): mine = lax.all_to_all(mine, 'c', 0, 0, tiled=True)]
    all_to_all x1, starting transfers between devices: 3.53 us -> 12.2 us  [body(): lax.all_to_all(mine, ALL, 0, 0, axis_index_groups=groups(), tiled=True)]
    all_gather x0 -> x1, blocking collectives: none -> 8.31 us  [body(): blocks = lax.all_gather(blocks, 'c', axis=0).reshape(2, 2, 32, 128)]
    all_to_all x1, waiting for transfers between devices: 6.22 us -> 14.4 us  [body(): lax.all_to_all(mine, ALL, 0, 0, axis_index_groups=groups(), tiled=True)]
    unnamed x10 -> x6, local copies, waits for them, and re-layouts: 3.43 us -> 2.05 us
    pallas_call x1, Pallas kernels: 0.01 us -> 1.29 us  [body(): call(spread_kernel, [((16, 2, 32, 128), bf16)], [SM, VM])(pos, blocks)]
where the time goes in v5:
time: 115 us
  blocking collectives  73.2 us (64%)
  waiting for transfers between devices  14.4 us (13%)
  starting transfers between devices  12.2 us (11%)
  Pallas kernels  10.2 us (9%)
  local copies, waits for them, and re-layouts  2.92 us (3%)
    all_to_all x1, blocking collectives, body(): parts = lax.all_to_all(sums, 'zh', 0, 0, tiled=True)  15.5 us
    all_to_all x1, waiting for transfers between devices, body(): lax.all_to_all(mine, ALL, 0, 0, axis_index_groups=groups(), tiled=True)  14.4 us
    all_to_all x1, blocking collectives, body(): parts_two = lax.all_to_all(partial_two, NARROW, 0, 0, tiled=True)  14.1 us
    all_to_all x1, starting transfers between devices, body(): lax.all_to_all(mine, ALL, 0, 0, axis_index_groups=groups(), tiled=True)  12.2 us
    all_to_all x1, blocking collectives, body(): blocks = lax.all_to_all(blocks, NARROW, 0, 0, tiled=True)  10.5 us
    all_gather x1, blocking collectives, body(): blocks = lax.all_gather(blocks, 'c', axis=0).reshape(2, 2, 32, 128)  8.31 us
    all_to_all x1, blocking collectives, body(): parts = lax.all_to_all(half, 'y', 0, 0, tiled=True)  7.32 us
    all_to_all x1, blocking collectives, body(): new_half = lax.all_to_all(copies, 'y', 0, 0, tiled=True).reshape(128, R)  7.21 us
  transfers between devices with their start and end apart: 1, of which 1 were waited for; matrix products, arithmetic and copies ran while one was open for 0% of the time, Pallas kernels for 0%

profile of v5, /device:TPU:1, one launch (start us, length us, event | category | flops | bytes accessed | tf_op | source)
XLA Modules:
  0.0 114.7 jit_solution(6340506426737613702)
XLA Ops:
  0.6 0.0 copy-start
  0.7 0.8 fusion.2
  1.4 0.7 pad_maximum_fusion
  2.1 8.3 %all-gather = bf16[128,128]{1,0:T(8,128)(2,1)S(1)} all-gather(bf16[64,128]{1,0:T(8,128)(2,1)S(1)} %pad_maximum_fusion), channel_id=2, replica_groups=mesh['zl'=4,'x'=4,'y'=4,'zh'=4,'c'=2] {'c'}, dimensions={0}, use_global_device_ids=true | all-gather | bytes 49152 | tf_op jit(solution)/shard_map/all_gather | solution.py:161
  10.5 0.1 stack.23.pos
  10.5 1.3 %shard_map.68 = bf16[16,2,32,128]{3,2,1,0:T(8,128)(2,1)} custom-call(s32[5]{0:T(128)S(1)} %stack.23.pos, bf16[2,2,32,128]{3,2,1,0:T(8,128)(2,1)S(1)} %bitcast.16), custom_call_target="tpu_custom_call" | custom-call | tf_op jit(solution)/shard_map/pallas_call | solution.py:162
  11.8 12.2 %all-to-all-start = ((bf16[16,2,32,128]{3,2,1,0:T(8,128)(2,1)}), bf16[16,2,32,128]{3,2,1,0:T(8,128)(2,1)S(1)}, u32[]{:S(2)}, u32[]{:S(2)}) async-start(bf16[16,2,32,128]{3,2,1,0:T(8,128)(2,1)} %shard_map.68), calls=%async_computation | async-start | bytes 524288 | tf_op jit(solution)/shard_map/all_to_all | solution.py:163
  24.0 0.0 copy-start.1
  24.1 1.6 %copy-done.1 = bf16[32,256,128]{2,1,0:T(8,128)(2,1)S(1)} copy-done((bf16[32,256,128]{2,1,0:T(8,128)(2,1)S(1)}, bf16[32,256,128]{2,1,0:T(8,128)(2,1)}, u32[]{:S(2)}) %copy-start.1) | copy-done | bytes 2097176
  25.6 0.0 copy-start.2
  25.6 0.2 shard_map.69.t
  25.8 0.0 copy-done
  25.8 0.5 copy-done.2
  26.3 0.3 fusion.s_ref
  26.6 14.4 %all-to-all-done = bf16[16,2,32,128]{3,2,1,0:T(8,128)(2,1)S(1)} async-done(((bf16[16,2,32,128]{3,2,1,0:T(8,128)(2,1)}), bf16[16,2,32,128]{3,2,1,0:T(8,128)(2,1)S(1)}, u32[]{:S(2)}, u32[]{:S(2)}) %all-to-all-start) | async-done | bytes 262176 | tf_op jit(solution)/shard_map/all_to_all | solution.py:163
  41.1 2.2 %all-gather.1 = bf16[32,2,32,128]{3,2,1,0:T(8,128)(2,1)S(1)} all-gather(bf16[16,2,32,128]{3,2,1,0:T(8,128)(2,1)S(1)} %all-to-all-done), channel_id=3, replica_groups=mesh['zl'=4,'x'=4,'y'=4,'zh'=4,'c'=2] {'c'}, dimensions={0}, use_global_device_ids=true | all-gather | bytes 786432 | tf_op jit(solution)/shard_map/all_gather | solution.py:164
  43.2 3.4 %shard_map.70 = (bf16[256,512]{1,0:T(8,128)(2,1)S(1)}, f32[32,512]{1,0:T(8,128)S(1)}, f32[128,512]{1,0:T(8,128)S(1)}) custom-call(s32[5]{0:T(128)S(1)} %stack.23.pos, f32[32,512]{1,0:T(8,128)S(1)} %fusion.s_ref, bf16[2,16,2,32,128]{4,3,2,1,0:T(8,128)(2,1)S(1)} %bitcast.15, bf16[32,256,128]{2,1,0:T(8,128)(2,1)S(1)} %shard_map.69.t), custom_call_target="tpu_custom_call" | custom-call | flops 2147483648 | bytes 2097152 | tf_op jit(solution)/shard_map/pallas_call | solution.py:170
  46.6 2.2 %all-gather.2 = bf16[512,512]{1,0:T(8,128)(2,1)S(1)} all-gather(bf16[256,512]{1,0:T(8,128)(2,1)S(1)} %get-tuple-element.9), channel_id=4, replica_groups=mesh['zl'=4,'x'=4,'y'=4,'zh'=4,'c'=2] {'c'}, dimensions={0}, use_global_device_ids=true | all-gather | bytes 786432 | tf_op jit(solution)/shard_map/all_gather | solution.py:179
  48.8 0.6 shard_map.71
  49.4 7.3 %all_to_all.30.parts_ref = bf16[4,32,512]{2,1,0:T(8,128)(2,1)S(1)} all-to-all(bf16[4,32,512]{2,1,0:T(8,128)(2,1)S(1)} %shard_map.71), channel_id=1, replica_groups=mesh['zl'=4,'x'=4,'y'=4,'zh'=4,'c'=2] {'y'}, dimensions={0} | all-to-all | bytes 262144 | tf_op jit(solution)/shard_map/all_to_all | solution.py:181
  56.8 15.5 %all_to_all.31.parts_ref = bf16[4,32,512]{2,1,0:T(8,128)(2,1)S(1)} all-to-all(bf16[4,32,512]{2,1,0:T(8,128)(2,1)S(1)} %shard_map.72), channel_id=1, replica_groups=mesh['zl'=4,'x'=4,'y'=4,'zh'=4,'c'=2] {'zh'}, dimensions={0} | all-to-all | bytes 262144 | tf_op jit(solution)/shard_map/all_to_all | solution.py:183
  72.3 0.1 shard_map.73
  72.4 7.2 %all_to_all.32 = bf16[4,32,512]{2,1,0:T(8,128)(2,1)S(1)} all-to-all(bf16[4,32,512]{2,1,0:T(8,128)(2,1)S(1)} %shard_map.73), channel_id=1, replica_groups=mesh['zl'=4,'x'=4,'y'=4,'zh'=4,'c'=2] {'y'}, dimensions={0} | all-to-all | bytes 262144 | tf_op jit(solution)/shard_map/all_to_all | solution.py:185
  79.6 5.9 %all_gather.27.new_ref = bf16[256,512]{1,0:T(8,128)(2,1)S(1)} all-gather(bf16[128,512]{1,0:T(8,128)(2,1)S(1)} %bitcast.17), channel_id=1, replica_groups=mesh['zl'=4,'x'=4,'y'=4,'zh'=4,'c'=2] {'c'}, dimensions={0}, use_global_device_ids=true | all-gather | bytes 393216 | tf_op jit(solution)/shard_map/all_gather | solution.py:186
  85.5 3.7 %shard_map.74 = (bf16[16,8,512]{2,1,0:T(8,128)(2,1)S(1)}, bf16[16,256]{1,0:T(8,128)(2,1)}, f32[8,512]{1,0:T(8,128)S(1)}) custom-call(s32[5]{0:T(128)S(1)} %stack.23.pos, f32[32,512]{1,0:T(8,128)S(1)} %fusion.s_ref, bf16[256,512]{1,0:T(8,128)(2,1)S(1)} %all_gather.27.new_ref, f32[128,512]{1,0:T(8,128)S(1)} %get-tuple-element.10.two, ...), custom_call_target="tpu_custom_call" | custom-call | flops 2147483648 | bytes 2097152 | tf_op jit(solution)/shard_map/pallas_call | solution.py:188
  89.3 14.1 %all_to_all.33.parts_ref = bf16[16,8,512]{2,1,0:T(8,128)(2,1)S(1)} all-to-all(bf16[16,8,512]{2,1,0:T(8,128)(2,1)S(1)} %get-tuple-element.13), channel_id=1, replica_groups=mesh['zl'=4,'x'=4,'y'=4,'zh'=4,'c'=2] {'zl','x'}, dimensions={0} | all-to-all | bytes 262144 | tf_op jit(solution)/shard_map/all_to_all | solution.py:197
  103.3 0.2 shard_map.75
  103.5 10.5 %all_to_all.34.in_ref = bf16[16,8,128]{2,1,0:T(8,128)(2,1)S(1)} all-to-all(bf16[16,8,128]{2,1,0:T(8,128)(2,1)S(1)} %shard_map.75), channel_id=1, replica_groups=mesh['zl'=4,'x'=4,'y'=4,'zh'=4,'c'=2] {'zl','x'}, dimensions={0} | all-to-all | bytes 65536 | tf_op jit(solution)/shard_map/all_to_all | solution.py:199
  114.0 0.7 shard_map.76
  (1 shorter events, 0.0 us)
Async XLA Ops:
  0.6 25.2 %copy-start = (bf16[1024,512]{1,0:T(8,128)(2,1)S(1)}, bf16[1024,512]{1,0:T(8,128)(2,1)}, u32[]{:S(2)}) copy-start(bf16[1024,512]{1,0:T(8,128)(2,1)} %param.8) | copy-start | bytes 3145732
  11.8 29.2 %all-to-all-start = ((bf16[16,2,32,128]{3,2,1,0:T(8,128)(2,1)}), bf16[16,2,32,128]{3,2,1,0:T(8,128)(2,1)S(1)}, u32[]{:S(2)}, u32[]{:S(2)}) async-start(bf16[16,2,32,128]{3,2,1,0:T(8,128)(2,1)} %shard_map.68), calls=%async_computation | async-start | bytes 524288 | tf_op jit(solution)/shard_map/all_to_all | solution.py:163
  24.0 1.6 %copy-start.1 = (bf16[32,256,128]{2,1,0:T(8,128)(2,1)S(1)}, bf16[32,256,128]{2,1,0:T(8,128)(2,1)}, u32[]{:S(2)}) copy-start(bf16[32,256,128]{2,1,0:T(8,128)(2,1)} %t_hbm.1) | copy-start | bytes 6291460
  25.6 0.7 copy-start.2

commit v6 on v5

--- a/solution.py
+++ b/solution.py
@@ -41,19 +41,19 @@
     return scaled, jnp.tanh(model - target).astype(bf16)
 
 
-def fetch_kernel(t_hbm, t, sems):
+def first_kernel(
+    pos, table_hbm, both_ref, t_hbm, out_ref, own_ref, two_ref, s_ref,
+    t, sems, table, one_t, one, two, acc,
+):
     size = BATCH // CHUNKS
-    copies = [
+    rows = pltpu.make_async_copy(table_hbm, table, sems.at[CHUNKS])
+    rows.start()
+    loads = [
         pltpu.make_async_copy(t_hbm.at[pl.ds(q * size, size)], t.at[pl.ds(q * size, size)], sems.at[q])
         for q in range(CHUNKS)
     ]
-    for copy in copies:
-        copy.start()
-    for copy in copies:
-        copy.wait()
-
-
-def first_kernel(pos, s_ref, both_ref, t, out_ref, own_ref, two_ref, one_t, one, two, acc):
+    for load in loads:
+        load.start()
     for b in range(16):
         for c in range(2):
             for h in range(2):
@@ -63,7 +63,17 @@
     two_ref[...] = two[...]
     acc[...] = jnp.zeros_like(acc)
     own_ref[...] = dot(pick(pos[0], 32, 256), one[...], NN)
+    row = lax.broadcasted_iota(jnp.int32, (BATCH, 128), 0)
+    lane = lax.broadcasted_iota(jnp.int32, (BATCH, 128), 1)
+    index = jnp.zeros((BATCH, 128), jnp.int32)
+    for k in range(BATCH):
+        index = jnp.where(row == k, pos[5 + k], index)
+    hot = [(lane + first == index).astype(f32) for first in range(0, table.shape[0], 128)]
+    rows.wait()
+    s_ref[...] = dot(jnp.concatenate(hot, axis=1).astype(bf16), table[...], NN)
     for k in range(0, BATCH, 2):
+        if k % size == 0:
+            loads[k // size].wait()
         scaled, error = errors(s_ref[k : k + 2, :], one[...], two, t, k)
         acc[...] += dot(error, scaled, NN)
     out_ref[...] = acc[...].astype(bf16)
@@ -155,6 +165,7 @@
     y, c = lax.axis_index("y"), lax.axis_index("c")
     n, w = lax.axis_index(NARROW), lax.axis_index(WIDE)
     pos = jnp.stack([c * 128 + y * 32, w * 16, n * 8, c * 128, c]).astype(jnp.int32)
+    pos = jnp.concatenate([pos, chosen])
 
     one_t = mode_one.T
     blocks = jnp.concatenate([mode_two.T, one_t[:, :128], one_t[:, 128:]], axis=0)
@@ -162,20 +173,15 @@
     mine = call(spread_kernel, [((16, 2, 32, 128), bf16)], [SM, VM])(pos, blocks)
     both = lax.all_to_all(mine, ALL, 0, 0, axis_index_groups=groups(), tiled=True)
     both = lax.all_gather(both, "c", axis=0)
-    one_hot = (
-        chosen[:, None] == lax.broadcasted_iota(jnp.int32, (chosen.shape[0], slice_table.shape[0]), 1)
-    ).astype(bf16)
-    slice_rows = jnp.dot(one_hot, slice_table, preferred_element_type=f32)
-    t = call(fetch_kernel, [((BATCH, 256, 128), bf16)], [HB], (pltpu.SemaphoreType.DMA((CHUNKS,)),), nbytes=1 << 21)(slices)
-    half, own_one, two = call(
+    half, own_one, two, slice_rows = call(
         first_kernel,
-        [((256, R), bf16), ((32, R), f32), ((128, R), f32)],
-        [SM, VM, VM, VM],
-        (pltpu.VMEM((R, 256), bf16), pltpu.VMEM((256, R), bf16), pltpu.VMEM((128, R), f32), pltpu.VMEM((256, R), f32)),
+        [((256, R), bf16), ((32, R), f32), ((128, R), f32), ((BATCH, R), f32)],
+        [SM, HB, VM, HB],
+        (pltpu.VMEM((BATCH, 256, 128), bf16), pltpu.SemaphoreType.DMA((CHUNKS + 1,)), pltpu.VMEM((1024, R), bf16), pltpu.VMEM((R, 256), bf16), pltpu.VMEM((256, R), bf16), pltpu.VMEM((128, R), f32), pltpu.VMEM((256, R), f32)),
         flops=1 << 31,
-        vmem=16,
+        vmem=52,
         nbytes=1 << 21,
-    )(pos, slice_rows, both, t)
+    )(pos, slice_table, both, slices)
     pair = lax.all_gather(half, "c", axis=0)
     half = call(pair_kernel, [((4, 32, R), bf16)], [SM, VM])(pos, pair)
     parts = lax.all_to_all(half, "y", 0, 0, tiled=True)
@@ -193,7 +199,7 @@
         flops=1 << 31,
         vmem=16,
         nbytes=1 << 21,
-    )(pos, slice_rows, new_full, two, t)
+    )(pos, slice_rows, new_full, two, slices)
     parts_two = lax.all_to_all(partial_two, NARROW, 0, 0, tiled=True)
     blocks = call(renew_two_kernel, [((16, 8, 128), bf16)], [VM, VM])(own_two, parts_two)
     blocks = lax.all_to_all(blocks, NARROW, 0, 0, tiled=True)

time: 115 us -> 117 us (1.017)
  blocking collectives: 73.2 us -> 102 us
  waiting for transfers between devices: 14.4 us -> 0 us
  starting transfers between devices: 12.2 us -> 0 us
  local copies, waits for them, and re-layouts: 2.92 us -> 1.45 us
  Pallas kernels: 10.2 us -> 11.5 us
    all_to_all x0 -> x1, blocking collectives: none -> 29 us  [body(): lax.all_to_all(mine, ALL, 0, 0, axis_index_groups=groups(), tiled=True)]
    all_to_all x1 -> x0, waiting for transfers between devices: 14.4 us -> none  [body(): lax.all_to_all(mine, ALL, 0, 0, axis_index_groups=groups(), tiled=True)]
    all_to_all x1 -> x0, starting transfers between devices: 12.2 us -> none  [body(): lax.all_to_all(mine, ALL, 0, 0, axis_index_groups=groups(), tiled=True)]
    pallas_call x2 -> x1, Pallas kernels: 3.6 us -> 5.66 us  [body(): call(first_kernel, [((256, R), bf16), ((32, R), f32), ((128, R), f32), ((...]
    unnamed x6 -> x2, local copies, waits for them, and re-layouts: 2.05 us -> 0.01 us
  transfers between devices with their start and end apart: 1 -> 0, of which waited for: 1 -> 0; matrix products, arithmetic and copies ran while one was open for 0% -> 0% of each run, Pallas kernels for 0% -> 0%
where the time goes in v6:
time: 117 us
  blocking collectives  102 us (87%)
  Pallas kernels  11.5 us (10%)
  local copies, waits for them, and re-layouts  1.45 us (1%)
    all_to_all x1, blocking collectives, body(): lax.all_to_all(mine, ALL, 0, 0, axis_index_groups=groups(), tiled=True)  29 us
    all_to_all x1, blocking collectives, body(): parts = lax.all_to_all(sums, 'zh', 0, 0, tiled=True)  15.5 us
    all_to_all x1, blocking collectives, body(): parts_two = lax.all_to_all(partial_two, NARROW, 0, 0, tiled=True)  14.1 us
    all_to_all x1, blocking collectives, body(): blocks = lax.all_to_all(blocks, NARROW, 0, 0, tiled=True)  10.5 us
    all_gather x1, blocking collectives, body(): blocks = lax.all_gather(blocks, 'c', axis=0).reshape(2, 2, 32, 128)  8.31 us
    all_to_all x1, blocking collectives, body(): parts = lax.all_to_all(half, 'y', 0, 0, tiled=True)  7.32 us
    all_to_all x1, blocking collectives, body(): new_half = lax.all_to_all(copies, 'y', 0, 0, tiled=True).reshape(128, R)  7.21 us
    all_gather x1, blocking collectives, body(): new_full = lax.all_gather(new_half, 'c', axis=0, tiled=True)  5.89 us

profile of v6, /device:TPU:1, one launch (start us, length us, event | category | flops | bytes accessed | tf_op | source)
XLA Modules:
  0.0 116.7 jit_solution(12546811467391235254)
XLA Ops:
  0.6 0.7 fusion
  1.3 0.7 pad_maximum_fusion
  2.0 8.3 %all-gather = bf16[128,128]{1,0:T(8,128)(2,1)S(1)} all-gather(bf16[64,128]{1,0:T(8,128)(2,1)S(1)} %pad_maximum_fusion), channel_id=2, replica_groups=mesh['zl'=4,'x'=4,'y'=4,'zh'=4,'c'=2] {'c'}, dimensions={0}, use_global_device_ids=true | all-gather | bytes 49152 | tf_op jit(solution)/shard_map/all_gather | solution.py:172
  10.4 0.7 concatenate.6.pos
  11.1 0.6 shard_map.68
  11.7 29.0 %all_to_all.30 = bf16[16,2,32,128]{3,2,1,0:T(8,128)(2,1)S(1)} all-to-all(bf16[16,2,32,128]{3,2,1,0:T(8,128)(2,1)S(1)} %shard_map.68), channel_id=1, replica_groups={{1,3,5,7,9,11,13,15,17,19,21,23,25,27,29,31},{33,35,37,39,41,43,45,47,4..., dimensions={0} | all-to-all | bytes 524288 | tf_op jit(solution)/shard_map/all_to_all | solution.py:174
  40.7 2.2 %all-gather.1 = bf16[32,2,32,128]{3,2,1,0:T(8,128)(2,1)S(1)} all-gather(bf16[16,2,32,128]{3,2,1,0:T(8,128)(2,1)S(1)} %all_to_all.30), channel_id=3, replica_groups=mesh['zl'=4,'x'=4,'y'=4,'zh'=4,'c'=2] {'c'}, dimensions={0}, use_global_device_ids=true | all-gather | bytes 786432 | tf_op jit(solution)/shard_map/all_gather | solution.py:175
  42.9 5.7 %shard_map.69 = (bf16[256,512]{1,0:T(8,128)(2,1)S(1)}, f32[32,512]{1,0:T(8,128)S(1)}, f32[128,512]{1,0:T(8,128)S(1)}, f32[32,512]{1,0:T(8,128)S(1)}) custom-call(s32[37]{0:T(128)S(1)} %concatenate.6.pos, bf16[1024,512]{1,0:T(8,128)(2,1)} %table_hbm.1, bf16[2,16,2,32,128]{4,3,2,1,0:T(8,128)(2,1)S(1)} %bitcast.14, bf16[32,256,128]{2,1,0:T(8,128)(2,1)} %t.1), custom_call_target="tpu_custom_call" | custom-call | flops 2147483648 | bytes 2097152 | tf_op jit(solution)/shard_map/pallas_call | solution.py:176
  48.5 0.0 copy-start
  48.5 2.3 %all-gather.2 = bf16[512,512]{1,0:T(8,128)(2,1)S(1)} all-gather(bf16[256,512]{1,0:T(8,128)(2,1)S(1)} %get-tuple-element.11), channel_id=4, replica_groups=mesh['zl'=4,'x'=4,'y'=4,'zh'=4,'c'=2] {'c'}, dimensions={0}, use_global_device_ids=true | all-gather | bytes 786432 | tf_op jit(solution)/shard_map/all_gather | solution.py:185
  50.9 0.6 shard_map.70
  51.4 7.3 %all_to_all.31.parts_ref = bf16[4,32,512]{2,1,0:T(8,128)(2,1)S(1)} all-to-all(bf16[4,32,512]{2,1,0:T(8,128)(2,1)S(1)} %shard_map.70), channel_id=1, replica_groups=mesh['zl'=4,'x'=4,'y'=4,'zh'=4,'c'=2] {'y'}, dimensions={0} | all-to-all | bytes 262144 | tf_op jit(solution)/shard_map/all_to_all | solution.py:187
  58.8 15.5 %all_to_all.32.parts_ref = bf16[4,32,512]{2,1,0:T(8,128)(2,1)S(1)} all-to-all(bf16[4,32,512]{2,1,0:T(8,128)(2,1)S(1)} %shard_map.71), channel_id=1, replica_groups=mesh['zl'=4,'x'=4,'y'=4,'zh'=4,'c'=2] {'zh'}, dimensions={0} | all-to-all | bytes 262144 | tf_op jit(solution)/shard_map/all_to_all | solution.py:189
  74.3 0.1 shard_map.72
  74.4 7.2 %all_to_all.33 = bf16[4,32,512]{2,1,0:T(8,128)(2,1)S(1)} all-to-all(bf16[4,32,512]{2,1,0:T(8,128)(2,1)S(1)} %shard_map.72), channel_id=1, replica_groups=mesh['zl'=4,'x'=4,'y'=4,'zh'=4,'c'=2] {'y'}, dimensions={0} | all-to-all | bytes 262144 | tf_op jit(solution)/shard_map/all_to_all | solution.py:191
  81.7 5.9 %all_gather.27.new_ref = bf16[256,512]{1,0:T(8,128)(2,1)S(1)} all-gather(bf16[128,512]{1,0:T(8,128)(2,1)S(1)} %bitcast.16), channel_id=1, replica_groups=mesh['zl'=4,'x'=4,'y'=4,'zh'=4,'c'=2] {'c'}, dimensions={0}, use_global_device_ids=true | all-gather | bytes 393216 | tf_op jit(solution)/shard_map/all_gather | solution.py:192
  87.6 0.0 copy-done
  87.6 3.7 %shard_map.73 = (bf16[16,8,512]{2,1,0:T(8,128)(2,1)S(1)}, bf16[16,256]{1,0:T(8,128)(2,1)}, f32[8,512]{1,0:T(8,128)S(1)}) custom-call(s32[37]{0:T(128)S(1)} %concatenate.6.pos, f32[32,512]{1,0:T(8,128)S(1)} %get-tuple-element.9.s_ref, bf16[256,512]{1,0:T(8,128)(2,1)S(1)} %all_gather.27.new_ref, f32[128,512]{1,0:T(8,128)S(1)} %get-tuple-element.12.two, ...), custom_call_target="tpu_custom_call" | custom-call | flops 2147483648 | bytes 2097152 | tf_op jit(solution)/shard_map/pallas_call | solution.py:194
  91.3 14.1 %all_to_all.34.parts_ref = bf16[16,8,512]{2,1,0:T(8,128)(2,1)S(1)} all-to-all(bf16[16,8,512]{2,1,0:T(8,128)(2,1)S(1)} %get-tuple-element.15), channel_id=1, replica_groups=mesh['zl'=4,'x'=4,'y'=4,'zh'=4,'c'=2] {'zl','x'}, dimensions={0} | all-to-all | bytes 262144 | tf_op jit(solution)/shard_map/all_to_all | solution.py:203
  105.4 0.2 shard_map.74
  105.5 10.5 %all_to_all.35.in_ref = bf16[16,8,128]{2,1,0:T(8,128)(2,1)S(1)} all-to-all(bf16[16,8,128]{2,1,0:T(8,128)(2,1)S(1)} %shard_map.74), channel_id=1, replica_groups=mesh['zl'=4,'x'=4,'y'=4,'zh'=4,'c'=2] {'zl','x'}, dimensions={0} | all-to-all | bytes 65536 | tf_op jit(solution)/shard_map/all_to_all | solution.py:205
  116.0 0.7 shard_map.75
  (1 shorter events, 0.0 us)
Async XLA Ops:
  48.5 39.0 %copy-start = (bf16[32,256,128]{2,1,0:T(8,128)(2,1)S(1)}, bf16[32,256,128]{2,1,0:T(8,128)(2,1)}, u32[]{:S(2)}) copy-start(bf16[32,256,128]{2,1,0:T(8,128)(2,1)} %t.1) | copy-start | bytes 6291460

commit v7 on v5

--- a/solution.py
+++ b/solution.py
@@ -22,6 +22,7 @@
 TN = (((0,), (0,)), ((), ()))
 CHUNKS = 4
 BATCH = 32
+STEP = 8
 
 
 def dot(a, b, dims):
@@ -35,9 +36,9 @@
 
 
 def errors(s, left, two, t, k):
-    scaled = jnp.concatenate([two[...] * s[0:1], two[...] * s[1:2]], axis=0).astype(bf16)
+    scaled = jnp.concatenate([two[...] * s[q : q + 1] for q in range(STEP)], axis=0).astype(bf16)
     model = dot(left, scaled, NT)
-    target = jnp.concatenate([t[k], t[k + 1]], axis=1).astype(f32)
+    target = jnp.concatenate([t[k + q] for q in range(STEP)], axis=1).astype(f32)
     return scaled, jnp.tanh(model - target).astype(bf16)
 
 
@@ -56,43 +57,33 @@
 def first_kernel(pos, s_ref, both_ref, t, out_ref, own_ref, two_ref, one_t, one, two, acc):
     for b in range(16):
         for c in range(2):
-            for h in range(2):
-                one_t[pl.ds(32 * b + 16 * c, 16), pl.ds(128 * h, 128)] = both_ref[1, b, c, pl.ds(16 * h, 16), :]
+            for h in range(4):
+                rows, lanes = pl.ds(32 * b + 16 * c + 8 * (h // 2), 8), pl.ds(128 * (h % 2), 128)
+                one_t[rows, lanes] = both_ref[1, b, c, h]
     one[...] = one_t[...].T
-    two[...] = both_ref[0, :, pos[4]].reshape(R, 128).astype(f32).T
+    two[...] = both_ref[0, :, pos[3]].reshape(R, 128).astype(f32).T
     two_ref[...] = two[...]
     acc[...] = jnp.zeros_like(acc)
     own_ref[...] = dot(pick(pos[0], 32, 256), one[...], NN)
-    for k in range(0, BATCH, 2):
-        scaled, error = errors(s_ref[k : k + 2, :], one[...], two, t, k)
+    for k in range(0, BATCH, STEP):
+        scaled, error = errors(s_ref[k : k + STEP, :], one[...], two, t, k)
         acc[...] += dot(error, scaled, NN)
-    out_ref[...] = acc[...].astype(bf16)
+    out_ref[...] = acc[...].astype(bf16).reshape(8, 32, R)
 
 
 def second_kernel(pos, s_ref, new_ref, two, t, out_ref, block_ref, own_ref, acc):
     acc[...] = jnp.zeros_like(acc)
     block_ref[...] = dot(pick(pos[1], 16, R), new_ref[...], NT).astype(bf16)
     own_ref[...] = dot(pick(pos[2], 8, 128), two[...].astype(bf16), NN)
-    for k in range(0, BATCH, 2):
-        s = s_ref[k : k + 2, :]
+    for k in range(0, BATCH, STEP):
+        s = s_ref[k : k + STEP, :]
         _, error = errors(s, new_ref[...], two, t, k)
         both = dot(error, new_ref[...], TN)
-        acc[...] += both[:128] * s[0:1] + both[128:] * s[1:2]
+        total = acc[...]
+        for q in range(STEP):
+            total = total + both[128 * q : 128 * q + 128] * s[q : q + 1]
+        acc[...] = total
     out_ref[...] = acc[...].astype(bf16).reshape(16, 8, R)
-
-
-def spread_kernel(pos, blocks_ref, out_ref):
-    kind = pos[4]
-    for c in range(2):
-        block = blocks_ref[c, kind]
-        for b in range(16):
-            out_ref[b, c] = block
-
-
-def pair_kernel(pos, pair_ref, out_ref):
-    rows = pl.ds(pl.multiple_of(pos[3], 128), 128)
-    total = pair_ref[0, rows, :].astype(f32) + pair_ref[1, rows, :].astype(f32)
-    out_ref[...] = total.astype(bf16).reshape(4, 32, R)
 
 
 def sum_kernel(parts_ref, out_ref):
@@ -109,7 +100,7 @@
 
 def renew_one_kernel(own_ref, parts_ref, out_ref):
     new = renew(own_ref[...], parts_ref[...]).astype(bf16)
-    for b in range(4):
+    for b in range(8):
         out_ref[b] = new
 
 
@@ -154,12 +145,13 @@
 def body(slices, mode_one, mode_two, slice_table, chosen):
     y, c = lax.axis_index("y"), lax.axis_index("c")
     n, w = lax.axis_index(NARROW), lax.axis_index(WIDE)
-    pos = jnp.stack([c * 128 + y * 32, w * 16, n * 8, c * 128, c]).astype(jnp.int32)
+    pos = jnp.stack([(y * 2 + c) * 32, w * 16, n * 8, c]).astype(jnp.int32)
 
-    one_t = mode_one.T
-    blocks = jnp.concatenate([mode_two.T, one_t[:, :128], one_t[:, 128:]], axis=0)
-    blocks = lax.all_gather(blocks, "c", axis=0).reshape(2, 2, 32, 128)
-    mine = call(spread_kernel, [((16, 2, 32, 128), bf16)], [SM, VM])(pos, blocks)
+    tiles = mode_one.T.reshape(2, 8, 2, 128).transpose(0, 2, 1, 3).reshape(4, 8, 128)
+    blocks = jnp.concatenate([mode_two.T.reshape(4, 8, 128), tiles], axis=0)
+    blocks = lax.all_gather(blocks, "c", axis=0).reshape(2, 2, 4, 8, 128)
+    mine = lax.dynamic_index_in_dim(blocks, c, axis=1, keepdims=False)
+    mine = jnp.broadcast_to(mine[None], (16, 2, 4, 8, 128))
     both = lax.all_to_all(mine, ALL, 0, 0, axis_index_groups=groups(), tiled=True)
     both = lax.all_gather(both, "c", axis=0)
     one_hot = (
@@ -167,23 +159,20 @@
     ).astype(bf16)
     slice_rows = jnp.dot(one_hot, slice_table, preferred_element_type=f32)
     t = call(fetch_kernel, [((BATCH, 256, 128), bf16)], [HB], (pltpu.SemaphoreType.DMA((CHUNKS,)),), nbytes=1 << 21)(slices)
-    half, own_one, two = call(
+    partial_one, own_one, two = call(
         first_kernel,
-        [((256, R), bf16), ((32, R), f32), ((128, R), f32)],
+        [((8, 32, R), bf16), ((32, R), f32), ((128, R), f32)],
         [SM, VM, VM, VM],
         (pltpu.VMEM((R, 256), bf16), pltpu.VMEM((256, R), bf16), pltpu.VMEM((128, R), f32), pltpu.VMEM((256, R), f32)),
         flops=1 << 31,
         vmem=16,
         nbytes=1 << 21,
     )(pos, slice_rows, both, t)
-    pair = lax.all_gather(half, "c", axis=0)
-    half = call(pair_kernel, [((4, 32, R), bf16)], [SM, VM])(pos, pair)
-    parts = lax.all_to_all(half, "y", 0, 0, tiled=True)
+    parts = lax.all_to_all(partial_one, ("y", "c"), 0, 0, tiled=True)
     sums = call(sum_kernel, [((4, 32, R), bf16)], [VM])(parts)
     parts = lax.all_to_all(sums, "zh", 0, 0, tiled=True)
-    copies = call(renew_one_kernel, [((4, 32, R), bf16)], [VM, VM])(own_one, parts)
-    new_half = lax.all_to_all(copies, "y", 0, 0, tiled=True).reshape(128, R)
-    new_full = lax.all_gather(new_half, "c", axis=0, tiled=True)
+    copies = call(renew_one_kernel, [((8, 32, R), bf16)], [VM, VM])(own_one, parts)
+    new_full = lax.all_to_all(copies, ("y", "c"), 0, 0, tiled=True).reshape(256, R)
 
     partial_two, new_one_t, own_two = call(
         second_kernel,

time: 115 us -> 112 us (0.974); the launches traced: 115 us -> 110 us
  Pallas kernels: 10.2 us -> 7.55 us
  blocking collectives: 73.2 us -> 71.1 us
    all_gather x3 -> x1, blocking collectives: 16.4 us -> 8.31 us  [body(): blocks = lax.all_gather(blocks, 'c', axis=0).reshape(2, 2, 4, 8, 128)]
    all_to_all x2, blocking collectives: 14.5 us -> 21.1 us  [the longest x1 12.1 us: body(): lax.all_to_all(copies, ('y', 'c'), 0, 0, tiled=True).reshape(256, R)]
    pallas_call x4 -> x2, Pallas kernels: 5.4 us -> 3.2 us  [the longest x1 3.09 us: body(): call(first_kernel, [((8, 32, R), bf16), ((32, R), f32), ((128, R), f32)],...]
where the time goes in v7:
time: 112 us; the launch traced here: 110 us
  blocking collectives  71.1 us (63%)
  waiting for transfers between devices  14.4 us (13%)
  starting transfers between devices  12.2 us (11%)
  Pallas kernels  7.55 us (7%)
  local copies, waits for them, and re-layouts  2.73 us (2%)
    all_to_all x1, blocking collectives, body(): parts = lax.all_to_all(sums, 'zh', 0, 0, tiled=True)  15.4 us
    all_to_all x1, blocking collectives, body(): parts_two = lax.all_to_all(partial_two, NARROW, 0, 0, tiled=True)  14.6 us
    all_to_all x1, waiting for transfers between devices, body(): lax.all_to_all(mine, ALL, 0, 0, axis_index_groups=groups(), tiled=True)  14.4 us
    all_to_all x1, starting transfers between devices, body(): lax.all_to_all(mine, ALL, 0, 0, axis_index_groups=groups(), tiled=True)  12.2 us
    all_to_all x1, blocking collectives, body(): lax.all_to_all(copies, ('y', 'c'), 0, 0, tiled=True).reshape(256, R)  12.1 us
    all_to_all x1, blocking collectives, body(): blocks = lax.all_to_all(blocks, NARROW, 0, 0, tiled=True)  9.56 us
    all_to_all x1, blocking collectives, body(): parts = lax.all_to_all(partial_one, ('y', 'c'), 0, 0, tiled=True)  9.01 us
    all_gather x1, blocking collectives, body(): blocks = lax.all_gather(blocks, 'c', axis=0).reshape(2, 2, 4, 8, 128)  8.31 us
  transfers between devices with their start and end apart: 1, of which 1 were waited for; matrix products, arithmetic and copies ran while one was open for 0% of the time, Pallas kernels for 0%

profile of v7, /device:TPU:1, one launch (start us, length us, event | category | flops | bytes accessed | tf_op | source)
XLA Modules:
  0.0 109.9 jit_solution(15829631787730274596)
XLA Ops:
  0.6 0.0 copy-start
  0.7 0.8 pad_maximum_fusion
  1.5 8.3 %all-gather = bf16[16,8,128]{2,1,0:T(8,128)(2,1)S(1)} all-gather(bf16[8,8,128]{2,1,0:T(8,128)(2,1)S(1)} %pad_maximum_fusion), channel_id=2, replica_groups=mesh['zl'=4,'x'=4,'y'=4,'zh'=4,'c'=2] {'c'}, dimensions={0}, use_global_device_ids=true | all-gather | bytes 49152 | tf_op jit(solution)/shard_map/all_gather | solution.py:152
  9.8 0.8 broadcast_in_dim.10
  10.5 12.2 %all-to-all-start = ((bf16[16,2,4,8,128]{4,3,2,1,0:T(8,128)(2,1)}), bf16[16,2,4,8,128]{4,3,2,1,0:T(8,128)(2,1)S(1)}, u32[]{:S(2)}, u32[]{:S(2)}) async-start(bf16[16,2,4,8,128]{4,3,2,1,0:T(8,128)(2,1)} %broadcast_in_dim.10), calls=%async_computation | async-start | bytes 524288 | tf_op jit(solution)/shard_map/all_to_all | solution.py:155
  22.7 0.0 copy-start.1
  22.8 1.6 %copy-done.1 = bf16[32,256,128]{2,1,0:T(8,128)(2,1)S(1)} copy-done((bf16[32,256,128]{2,1,0:T(8,128)(2,1)S(1)}, bf16[32,256,128]{2,1,0:T(8,128)(2,1)}, u32[]{:S(2)}) %copy-start.1) | copy-done | bytes 2097176
  24.3 0.0 copy-start.2
  24.3 0.2 shard_map.68.t
  24.5 0.1 pad_add_fusion.pos
  24.6 0.0 copy-done
  24.6 0.4 copy-done.2
  25.0 0.3 fusion.s_ref
  25.3 14.4 %all-to-all-done = bf16[16,2,4,8,128]{4,3,2,1,0:T(8,128)(2,1)S(1)} async-done(((bf16[16,2,4,8,128]{4,3,2,1,0:T(8,128)(2,1)}), bf16[16,2,4,8,128]{4,3,2,1,0:T(8,128)(2,1)S(1)}, u32[]{:S(2)}, u32[]{:S(2)}) %all-to-all-start) | async-done | bytes 262176 | tf_op jit(solution)/shard_map/all_to_all | solution.py:155
  39.7 2.2 %all-gather.1 = bf16[32,2,4,8,128]{4,3,2,1,0:T(8,128)(2,1)S(1)} all-gather(bf16[16,2,4,8,128]{4,3,2,1,0:T(8,128)(2,1)S(1)} %all-to-all-done), channel_id=3, replica_groups=mesh['zl'=4,'x'=4,'y'=4,'zh'=4,'c'=2] {'c'}, dimensions={0}, use_global_device_ids=true | all-gather | bytes 786432 | tf_op jit(solution)/shard_map/all_gather | solution.py:156
  41.9 3.1 %shard_map.69 = (bf16[8,32,512]{2,1,0:T(8,128)(2,1)S(1)}, f32[32,512]{1,0:T(8,128)S(1)}, f32[128,512]{1,0:T(8,128)S(1)}) custom-call(s32[4]{0:T(128)S(1)} %pad_add_fusion.pos, f32[32,512]{1,0:T(8,128)S(1)} %fusion.s_ref, bf16[2,16,2,4,8,128]{5,4,3,2,1,0:T(8,128)(2,1)S(1)} %bitcast.22, bf16[32,256,128]{2,1,0:T(8,128)(2,1)S(1)} %shard_map.68.t), custom_call_target="tpu_custom_call" | custom-call | flops 2147483648 | bytes 2097152 | tf_op jit(solution)/shard_map/pallas_call | solution.py:162
  45.0 9.0 %all_to_all.30.parts_ref = bf16[8,32,512]{2,1,0:T(8,128)(2,1)S(1)} all-to-all(bf16[8,32,512]{2,1,0:T(8,128)(2,1)S(1)} %get-tuple-element.9), channel_id=1, replica_groups=mesh['zl'=4,'x'=4,'y'=4,'zh'=4,'c'=2] {'y','c'}, dimensions={0} | all-to-all | bytes 524288 | tf_op jit(solution)/shard_map/all_to_all | solution.py:171
  54.1 15.4 %all_to_all.31.parts_ref = bf16[4,32,512]{2,1,0:T(8,128)(2,1)S(1)} all-to-all(bf16[4,32,512]{2,1,0:T(8,128)(2,1)S(1)} %shard_map.70), channel_id=1, replica_groups=mesh['zl'=4,'x'=4,'y'=4,'zh'=4,'c'=2] {'zh'}, dimensions={0} | all-to-all | bytes 262144 | tf_op jit(solution)/shard_map/all_to_all | solution.py:173
  69.4 0.1 shard_map.71
  69.5 12.1 %all_to_all.32 = bf16[8,32,512]{2,1,0:T(8,128)(2,1)S(1)} all-to-all(bf16[8,32,512]{2,1,0:T(8,128)(2,1)S(1)} %shard_map.71), channel_id=1, replica_groups=mesh['zl'=4,'x'=4,'y'=4,'zh'=4,'c'=2] {'y','c'}, dimensions={0} | all-to-all | bytes 524288 | tf_op jit(solution)/shard_map/all_to_all | solution.py:175
  81.7 3.3 %shard_map.72 = (bf16[16,8,512]{2,1,0:T(8,128)(2,1)S(1)}, bf16[16,256]{1,0:T(8,128)(2,1)}, f32[8,512]{1,0:T(8,128)S(1)}) custom-call(s32[4]{0:T(128)S(1)} %pad_add_fusion.pos, f32[32,512]{1,0:T(8,128)S(1)} %fusion.s_ref, bf16[256,512]{1,0:T(8,128)(2,1)S(1)} %bitcast.23, f32[128,512]{1,0:T(8,128)S(1)} %get-tuple-element.10.two, ...), custom_call_target="tpu_custom_call" | custom-call | flops 2147483648 | bytes 2097152 | tf_op jit(solution)/shard_map/pallas_call | solution.py:177
  85.0 14.6 %all_to_all.33.parts_ref = bf16[16,8,512]{2,1,0:T(8,128)(2,1)S(1)} all-to-all(bf16[16,8,512]{2,1,0:T(8,128)(2,1)S(1)} %get-tuple-element.13), channel_id=1, replica_groups=mesh['zl'=4,'x'=4,'y'=4,'zh'=4,'c'=2] {'zl','x'}, dimensions={0} | all-to-all | bytes 262144 | tf_op jit(solution)/shard_map/all_to_all | solution.py:186
  99.5 0.2 shard_map.73
  99.7 9.6 %all_to_all.34.in_ref = bf16[16,8,128]{2,1,0:T(8,128)(2,1)S(1)} all-to-all(bf16[16,8,128]{2,1,0:T(8,128)(2,1)S(1)} %shard_map.73), channel_id=1, replica_groups=mesh['zl'=4,'x'=4,'y'=4,'zh'=4,'c'=2] {'zl','x'}, dimensions={0} | all-to-all | bytes 65536 | tf_op jit(solution)/shard_map/all_to_all | solution.py:188
  109.3 0.7 shard_map.74
  (2 shorter events, 0.0 us)
Async XLA Ops:
  0.6 24.0 %copy-start = (bf16[1024,512]{1,0:T(8,128)(2,1)S(1)}, bf16[1024,512]{1,0:T(8,128)(2,1)}, u32[]{:S(2)}) copy-start(bf16[1024,512]{1,0:T(8,128)(2,1)} %param.8) | copy-start | bytes 3145732
  10.5 29.2 %all-to-all-start = ((bf16[16,2,4,8,128]{4,3,2,1,0:T(8,128)(2,1)}), bf16[16,2,4,8,128]{4,3,2,1,0:T(8,128)(2,1)S(1)}, u32[]{:S(2)}, u32[]{:S(2)}) async-start(bf16[16,2,4,8,128]{4,3,2,1,0:T(8,128)(2,1)} %broadcast_in_dim.10), calls=%async_computation | async-start | bytes 524288 | tf_op jit(solution)/shard_map/all_to_all | solution.py:155
  22.7 1.6 %copy-start.1 = (bf16[32,256,128]{2,1,0:T(8,128)(2,1)S(1)}, bf16[32,256,128]{2,1,0:T(8,128)(2,1)}, u32[]{:S(2)}) copy-start(bf16[32,256,128]{2,1,0:T(8,128)(2,1)} %t_hbm.1) | copy-start | bytes 6291460
  24.3 0.7 copy-start.2

commit v8 on v7

--- a/solution.py
+++ b/solution.py
@@ -54,14 +54,16 @@
         copy.wait()
 
 
-def first_kernel(pos, s_ref, both_ref, t, out_ref, own_ref, two_ref, one_t, one, two, acc):
+def first_kernel(pos, s_ref, both_ref, t, out_ref, own_ref, two_ref, one_t, two_t, one, two, acc):
     for b in range(16):
         for c in range(2):
             for h in range(4):
                 rows, lanes = pl.ds(32 * b + 16 * c + 8 * (h // 2), 8), pl.ds(128 * (h % 2), 128)
                 one_t[rows, lanes] = both_ref[1, b, c, h]
     one[...] = one_t[...].T
-    two[...] = both_ref[0, :, pos[3]].reshape(R, 128).astype(f32).T
+    for p in range(16):
+        two_t[pl.ds(p % 4 * 128 + p // 4 * 32, 32), :] = both_ref[0, p, pos[3]].reshape(32, 128)
+    two[...] = two_t[...].astype(f32).T
     two_ref[...] = two[...]
     acc[...] = jnp.zeros_like(acc)
     own_ref[...] = dot(pick(pos[0], 32, 256), one[...], NN)
@@ -106,10 +108,11 @@
 
 def renew_two_kernel(own_ref, parts_ref, out_ref):
     new = renew(own_ref[...], parts_ref[...])
-    for b in range(16):
+    for p in range(16):
+        b = p % 4 * 4 + p // 4
         group = new[:, 128 * (b // 4) : 128 * (b // 4) + 128]
         turn = (128 - 32 * (b % 4)) % 128
-        out_ref[b] = (pltpu.roll(group, turn, 1) if turn else group).astype(bf16)
+        out_ref[p] = (pltpu.roll(group, turn, 1) if turn else group).astype(bf16)
 
 
 def last_kernel(in_ref, out_ref):
@@ -138,14 +141,14 @@
 def groups():
     device = lambda n, yz, c: (n * 16 + yz) * 2 + c
     first = [[device(n, yz, 1) for yz in range(16)] for n in range(16)]
-    second = [[device(n, yz, 0) for n in range(16)] for yz in range(16)]
+    second = [[device(p % 4 * 4 + p // 4, yz, 0) for p in range(16)] for yz in range(16)]
     return first + second
 
 
 def body(slices, mode_one, mode_two, slice_table, chosen):
     y, c = lax.axis_index("y"), lax.axis_index("c")
-    n, w = lax.axis_index(NARROW), lax.axis_index(WIDE)
-    pos = jnp.stack([(y * 2 + c) * 32, w * 16, n * 8, c]).astype(jnp.int32)
+    m, w = lax.axis_index(("x", "zl")), lax.axis_index(WIDE)
+    pos = jnp.stack([(c * 4 + y) * 32, w * 16, m * 8, c]).astype(jnp.int32)
 
     tiles = mode_one.T.reshape(2, 8, 2, 128).transpose(0, 2, 1, 3).reshape(4, 8, 128)
     blocks = jnp.concatenate([mode_two.T.reshape(4, 8, 128), tiles], axis=0)
@@ -163,16 +166,16 @@
         first_kernel,
         [((8, 32, R), bf16), ((32, R), f32), ((128, R), f32)],
         [SM, VM, VM, VM],
-        (pltpu.VMEM((R, 256), bf16), pltpu.VMEM((256, R), bf16), pltpu.VMEM((128, R), f32), pltpu.VMEM((256, R), f32)),
+        (pltpu.VMEM((R, 256), bf16), pltpu.VMEM((R, 128), bf16), pltpu.VMEM((256, R), bf16), pltpu.VMEM((128, R), f32), pltpu.VMEM((256, R), f32)),
         flops=1 << 31,
         vmem=16,
         nbytes=1 << 21,
     )(pos, slice_rows, both, t)
-    parts = lax.all_to_all(partial_one, ("y", "c"), 0, 0, tiled=True)
+    parts = lax.all_to_all(partial_one, ("c", "y"), 0, 0, tiled=True)
     sums = call(sum_kernel, [((4, 32, R), bf16)], [VM])(parts)
     parts = lax.all_to_all(sums, "zh", 0, 0, tiled=True)
     copies = call(renew_one_kernel, [((8, 32, R), bf16)], [VM, VM])(own_one, parts)
-    new_full = lax.all_to_all(copies, ("y", "c"), 0, 0, tiled=True).reshape(256, R)
+    new_full = lax.all_to_all(copies, ("c", "y"), 0, 0, tiled=True).reshape(256, R)
 
     partial_two, new_one_t, own_two = call(
         second_kernel,
@@ -183,9 +186,9 @@
         vmem=16,
         nbytes=1 << 21,
     )(pos, slice_rows, new_full, two, t)
-    parts_two = lax.all_to_all(partial_two, NARROW, 0, 0, tiled=True)
+    parts_two = lax.all_to_all(partial_two, ("x", "zl"), 0, 0, tiled=True)
     blocks = call(renew_two_kernel, [((16, 8, 128), bf16)], [VM, VM])(own_two, parts_two)
-    blocks = lax.all_to_all(blocks, NARROW, 0, 0, tiled=True)
+    blocks = lax.all_to_all(blocks, ("x", "zl"), 0, 0, tiled=True)
     new_two_t = call(last_kernel, [((32, 128), bf16)], [VM])(blocks)
     return (new_one_t.T, new_two_t.T)
 

time: 112 us -> 111 us (level); the launches traced: 110 us -> 110 us
  no operation moved by 1% of the time
where the time goes in v8:
time: 111 us; the launch traced here: 110 us
  blocking collectives  71.3 us (64%)
  waiting for transfers between devices  14.4 us (13%)
  starting transfers between devices  12.2 us (11%)
  Pallas kernels  7.58 us (7%)
  local copies, waits for them, and re-layouts  2.73 us (2%)
    all_to_all x1, blocking collectives, body(): parts = lax.all_to_all(sums, 'zh', 0, 0, tiled=True)  14.6 us
    all_to_all x1, waiting for transfers between devices, body(): lax.all_to_all(mine, ALL, 0, 0, axis_index_groups=groups(), tiled=True)  14.4 us
    all_to_all x1, blocking collectives, body(): parts_two = lax.all_to_all(partial_two, ('x', 'zl'), 0, 0, tiled=True)  13.7 us
    all_to_all x1, blocking collectives, body(): lax.all_to_all(copies, ('c', 'y'), 0, 0, tiled=True).reshape(256, R)  12.9 us
    all_to_all x1, starting transfers between devices, body(): lax.all_to_all(mine, ALL, 0, 0, axis_index_groups=groups(), tiled=True)  12.2 us
    all_to_all x1, blocking collectives, body(): blocks = lax.all_to_all(blocks, ('x', 'zl'), 0, 0, tiled=True)  10.5 us
    all_to_all x1, blocking collectives, body(): parts = lax.all_to_all(partial_one, ('c', 'y'), 0, 0, tiled=True)  9.08 us
    all_gather x1, blocking collectives, body(): blocks = lax.all_gather(blocks, 'c', axis=0).reshape(2, 2, 4, 8, 128)  8.31 us
  transfers between devices with their start and end apart: 1, of which 1 were waited for; matrix products, arithmetic and copies ran while one was open for 0% of the time, Pallas kernels for 0%

profile of v8, /device:TPU:1, one launch (start us, length us, event | category | flops | bytes accessed | tf_op | source)
XLA Modules:
  0.0 110.2 jit_solution(17127193381535536299)
XLA Ops:
  0.6 0.0 copy-start
  0.7 0.8 pad_maximum_fusion
  1.5 8.3 %all-gather = bf16[16,8,128]{2,1,0:T(8,128)(2,1)S(1)} all-gather(bf16[8,8,128]{2,1,0:T(8,128)(2,1)S(1)} %pad_maximum_fusion), channel_id=2, replica_groups=mesh['zl'=4,'x'=4,'y'=4,'zh'=4,'c'=2] {'c'}, dimensions={0}, use_global_device_ids=true | all-gather | bytes 49152 | tf_op jit(solution)/shard_map/all_gather | solution.py:155
  9.8 0.8 broadcast_in_dim.10
  10.5 12.2 %all-to-all-start = ((bf16[16,2,4,8,128]{4,3,2,1,0:T(8,128)(2,1)}), bf16[16,2,4,8,128]{4,3,2,1,0:T(8,128)(2,1)S(1)}, u32[]{:S(2)}, u32[]{:S(2)}) async-start(bf16[16,2,4,8,128]{4,3,2,1,0:T(8,128)(2,1)} %broadcast_in_dim.10), calls=%async_computation | async-start | bytes 524288 | tf_op jit(solution)/shard_map/all_to_all | solution.py:158
  22.7 0.0 copy-start.1
  22.8 1.6 %copy-done.1 = bf16[32,256,128]{2,1,0:T(8,128)(2,1)S(1)} copy-done((bf16[32,256,128]{2,1,0:T(8,128)(2,1)S(1)}, bf16[32,256,128]{2,1,0:T(8,128)(2,1)}, u32[]{:S(2)}) %copy-start.1) | copy-done | bytes 2097176
  24.3 0.0 copy-start.2
  24.3 0.2 shard_map.68.t
  24.5 0.1 pad_add_fusion.pos
  24.6 0.0 copy-done
  24.6 0.4 copy-done.2
  25.0 0.3 fusion.s_ref
  25.3 14.4 %all-to-all-done = bf16[16,2,4,8,128]{4,3,2,1,0:T(8,128)(2,1)S(1)} async-done(((bf16[16,2,4,8,128]{4,3,2,1,0:T(8,128)(2,1)}), bf16[16,2,4,8,128]{4,3,2,1,0:T(8,128)(2,1)S(1)}, u32[]{:S(2)}, u32[]{:S(2)}) %all-to-all-start) | async-done | bytes 262176 | tf_op jit(solution)/shard_map/all_to_all | solution.py:158
  39.7 2.2 %all-gather.1 = bf16[32,2,4,8,128]{4,3,2,1,0:T(8,128)(2,1)S(1)} all-gather(bf16[16,2,4,8,128]{4,3,2,1,0:T(8,128)(2,1)S(1)} %all-to-all-done), channel_id=3, replica_groups=mesh['zl'=4,'x'=4,'y'=4,'zh'=4,'c'=2] {'c'}, dimensions={0}, use_global_device_ids=true | all-gather | bytes 786432 | tf_op jit(solution)/shard_map/all_gather | solution.py:159
  41.9 3.1 %shard_map.69 = (bf16[8,32,512]{2,1,0:T(8,128)(2,1)S(1)}, f32[32,512]{1,0:T(8,128)S(1)}, f32[128,512]{1,0:T(8,128)S(1)}) custom-call(s32[4]{0:T(128)S(1)} %pad_add_fusion.pos, f32[32,512]{1,0:T(8,128)S(1)} %fusion.s_ref, bf16[2,16,2,4,8,128]{5,4,3,2,1,0:T(8,128)(2,1)S(1)} %bitcast.22, bf16[32,256,128]{2,1,0:T(8,128)(2,1)S(1)} %shard_map.68.t), custom_call_target="tpu_custom_call" | custom-call | flops 2147483648 | bytes 2097152 | tf_op jit(solution)/shard_map/pallas_call | solution.py:165
  45.0 9.1 %all_to_all.30.parts_ref = bf16[8,32,512]{2,1,0:T(8,128)(2,1)S(1)} all-to-all(bf16[8,32,512]{2,1,0:T(8,128)(2,1)S(1)} %get-tuple-element.9), channel_id=1, replica_groups=mesh['zl'=4,'x'=4,'y'=4,'zh'=4,'c'=2] {'c','y'}, dimensions={0} | all-to-all | bytes 524288 | tf_op jit(solution)/shard_map/all_to_all | solution.py:174
  54.1 14.6 %all_to_all.31.parts_ref = bf16[4,32,512]{2,1,0:T(8,128)(2,1)S(1)} all-to-all(bf16[4,32,512]{2,1,0:T(8,128)(2,1)S(1)} %shard_map.70), channel_id=1, replica_groups=mesh['zl'=4,'x'=4,'y'=4,'zh'=4,'c'=2] {'zh'}, dimensions={0} | all-to-all | bytes 262144 | tf_op jit(solution)/shard_map/all_to_all | solution.py:176
  68.7 0.1 shard_map.71
  68.8 12.9 %all_to_all.32 = bf16[8,32,512]{2,1,0:T(8,128)(2,1)S(1)} all-to-all(bf16[8,32,512]{2,1,0:T(8,128)(2,1)S(1)} %shard_map.71), channel_id=1, replica_groups=mesh['zl'=4,'x'=4,'y'=4,'zh'=4,'c'=2] {'c','y'}, dimensions={0} | all-to-all | bytes 524288 | tf_op jit(solution)/shard_map/all_to_all | solution.py:178
  81.7 3.3 %shard_map.72 = (bf16[16,8,512]{2,1,0:T(8,128)(2,1)S(1)}, bf16[16,256]{1,0:T(8,128)(2,1)}, f32[8,512]{1,0:T(8,128)S(1)}) custom-call(s32[4]{0:T(128)S(1)} %pad_add_fusion.pos, f32[32,512]{1,0:T(8,128)S(1)} %fusion.s_ref, bf16[256,512]{1,0:T(8,128)(2,1)S(1)} %bitcast.23, f32[128,512]{1,0:T(8,128)S(1)} %get-tuple-element.10.two, ...), custom_call_target="tpu_custom_call" | custom-call | flops 2147483648 | bytes 2097152 | tf_op jit(solution)/shard_map/pallas_call | solution.py:180
  85.0 13.7 %all_to_all.33.parts_ref = bf16[16,8,512]{2,1,0:T(8,128)(2,1)S(1)} all-to-all(bf16[16,8,512]{2,1,0:T(8,128)(2,1)S(1)} %get-tuple-element.13), channel_id=1, replica_groups=mesh['zl'=4,'x'=4,'y'=4,'zh'=4,'c'=2] {'x','zl'}, dimensions={0} | all-to-all | bytes 262144 | tf_op jit(solution)/shard_map/all_to_all | solution.py:189
  98.8 0.2 shard_map.73
  99.0 10.5 %all_to_all.34.in_ref = bf16[16,8,128]{2,1,0:T(8,128)(2,1)S(1)} all-to-all(bf16[16,8,128]{2,1,0:T(8,128)(2,1)S(1)} %shard_map.73), channel_id=1, replica_groups=mesh['zl'=4,'x'=4,'y'=4,'zh'=4,'c'=2] {'x','zl'}, dimensions={0} | all-to-all | bytes 65536 | tf_op jit(solution)/shard_map/all_to_all | solution.py:191
  109.5 0.7 shard_map.74
  (2 shorter events, 0.0 us)
Async XLA Ops:
  0.6 24.0 %copy-start = (bf16[1024,512]{1,0:T(8,128)(2,1)S(1)}, bf16[1024,512]{1,0:T(8,128)(2,1)}, u32[]{:S(2)}) copy-start(bf16[1024,512]{1,0:T(8,128)(2,1)} %param.8) | copy-start | bytes 3145732
  10.5 29.2 %all-to-all-start = ((bf16[16,2,4,8,128]{4,3,2,1,0:T(8,128)(2,1)}), bf16[16,2,4,8,128]{4,3,2,1,0:T(8,128)(2,1)S(1)}, u32[]{:S(2)}, u32[]{:S(2)}) async-start(bf16[16,2,4,8,128]{4,3,2,1,0:T(8,128)(2,1)} %broadcast_in_dim.10), calls=%async_computation | async-start | bytes 524288 | tf_op jit(solution)/shard_map/all_to_all | solution.py:158
  22.7 1.6 %copy-start.1 = (bf16[32,256,128]{2,1,0:T(8,128)(2,1)S(1)}, bf16[32,256,128]{2,1,0:T(8,128)(2,1)}, u32[]{:S(2)}) copy-start(bf16[32,256,128]{2,1,0:T(8,128)(2,1)} %t_hbm.1) | copy-start | bytes 6291460
  24.3 0.7 copy-start.2

commit v9 on v8

--- a/solution.py
+++ b/solution.py
@@ -89,9 +89,7 @@
 
 
 def sum_kernel(parts_ref, out_ref):
-    total = jnp.sum(parts_ref[...].astype(f32), axis=0).astype(bf16)
-    for b in range(4):
-        out_ref[b] = total
+    out_ref[...] = jnp.sum(parts_ref[...].astype(f32), axis=0).astype(bf16)
 
 
 def renew(own, parts):
@@ -172,8 +170,9 @@
         nbytes=1 << 21,
     )(pos, slice_rows, both, t)
     parts = lax.all_to_all(partial_one, ("c", "y"), 0, 0, tiled=True)
-    sums = call(sum_kernel, [((4, 32, R), bf16)], [VM])(parts)
-    parts = lax.all_to_all(sums, "zh", 0, 0, tiled=True)
+    add = call(sum_kernel, [((32, R), bf16)], [VM])
+    parts = lax.all_gather(add(parts), "zh", axis=0, axis_index_groups=[[0, 1], [2, 3]])
+    parts = lax.all_gather(add(parts), "zh", axis=0, axis_index_groups=[[1, 2], [3, 0]])
     copies = call(renew_one_kernel, [((8, 32, R), bf16)], [VM, VM])(own_one, parts)
     new_full = lax.all_to_all(copies, ("c", "y"), 0, 0, tiled=True).reshape(256, R)
 

time: 111 us -> 110 us (level)
    all_gather x0 -> x2, blocking collectives: none -> 14.7 us  [the longest x1 7.34 us: body(): lax.all_gather(add(parts), 'zh', axis=0, axis_index_groups=[[0, 1], [2, 3]])]
    all_to_all x1 -> x0, blocking collectives: 14.6 us -> none  [body(): parts = lax.all_to_all(sums, 'zh', 0, 0, tiled=True)]
    all_to_all x1, blocking collectives: 13.7 us -> 12.6 us  [body(): parts_two = lax.all_to_all(partial_two, ('x', 'zl'), 0, 0, tiled=True)]
where the time goes in v9:
time: 110 us; the launch traced here: 109 us
  blocking collectives  70.2 us (64%)
  waiting for transfers between devices  14.4 us (13%)
  starting transfers between devices  12.2 us (11%)
  Pallas kernels  7.57 us (7%)
  local copies, waits for them, and re-layouts  2.73 us (2%)
    all_to_all x1, waiting for transfers between devices, body(): lax.all_to_all(mine, ALL, 0, 0, axis_index_groups=groups(), tiled=True)  14.4 us
    all_to_all x1, blocking collectives, body(): lax.all_to_all(copies, ('c', 'y'), 0, 0, tiled=True).reshape(256, R)  12.9 us
    all_to_all x1, blocking collectives, body(): parts_two = lax.all_to_all(partial_two, ('x', 'zl'), 0, 0, tiled=True)  12.6 us
    all_to_all x1, starting transfers between devices, body(): lax.all_to_all(mine, ALL, 0, 0, axis_index_groups=groups(), tiled=True)  12.2 us
    all_to_all x1, blocking collectives, body(): blocks = lax.all_to_all(blocks, ('x', 'zl'), 0, 0, tiled=True)  10.5 us
    all_to_all x1, blocking collectives, body(): parts = lax.all_to_all(partial_one, ('c', 'y'), 0, 0, tiled=True)  9.08 us
    all_gather x1, blocking collectives, body(): blocks = lax.all_gather(blocks, 'c', axis=0).reshape(2, 2, 4, 8, 128)  8.31 us
    all_gather x1, blocking collectives, body(): lax.all_gather(add(parts), 'zh', axis=0, axis_index_groups=[[0, 1], [2, 3]])  7.34 us
  transfers between devices with their start and end apart: 1, of which 1 were waited for; matrix products, arithmetic and copies ran while one was open for 0% of the time, Pallas kernels for 0%

profile of v9, /device:TPU:1, one launch (start us, length us, event | category | flops | bytes accessed | tf_op | source)
XLA Modules:
  0.0 109.1 jit_solution(17332245544063015674)
XLA Ops:
  0.6 0.0 copy-start
  0.7 0.8 pad_maximum_fusion
  1.5 8.3 %all-gather = bf16[16,8,128]{2,1,0:T(8,128)(2,1)S(1)} all-gather(bf16[8,8,128]{2,1,0:T(8,128)(2,1)S(1)} %pad_maximum_fusion), channel_id=2, replica_groups=mesh['zl'=4,'x'=4,'y'=4,'zh'=4,'c'=2] {'c'}, dimensions={0}, use_global_device_ids=true | all-gather | bytes 49152 | tf_op jit(solution)/shard_map/all_gather | solution.py:153
  9.8 0.8 broadcast_in_dim.10
  10.5 12.2 %all-to-all-start = ((bf16[16,2,4,8,128]{4,3,2,1,0:T(8,128)(2,1)}), bf16[16,2,4,8,128]{4,3,2,1,0:T(8,128)(2,1)S(1)}, u32[]{:S(2)}, u32[]{:S(2)}) async-start(bf16[16,2,4,8,128]{4,3,2,1,0:T(8,128)(2,1)} %broadcast_in_dim.10), calls=%async_computation | async-start | bytes 524288 | tf_op jit(solution)/shard_map/all_to_all | solution.py:156
  22.7 0.0 copy-start.1
  22.8 1.6 %copy-done.1 = bf16[32,256,128]{2,1,0:T(8,128)(2,1)S(1)} copy-done((bf16[32,256,128]{2,1,0:T(8,128)(2,1)S(1)}, bf16[32,256,128]{2,1,0:T(8,128)(2,1)}, u32[]{:S(2)}) %copy-start.1) | copy-done | bytes 2097176
  24.3 0.0 copy-start.2
  24.3 0.2 shard_map.68.t
  24.5 0.1 pad_add_fusion.pos
  24.6 0.0 copy-done
  24.6 0.4 copy-done.2
  25.0 0.3 fusion.s_ref
  25.3 14.4 %all-to-all-done = bf16[16,2,4,8,128]{4,3,2,1,0:T(8,128)(2,1)S(1)} async-done(((bf16[16,2,4,8,128]{4,3,2,1,0:T(8,128)(2,1)}), bf16[16,2,4,8,128]{4,3,2,1,0:T(8,128)(2,1)S(1)}, u32[]{:S(2)}, u32[]{:S(2)}) %all-to-all-start) | async-done | bytes 262176 | tf_op jit(solution)/shard_map/all_to_all | solution.py:156
  39.7 2.2 %all-gather.1 = bf16[32,2,4,8,128]{4,3,2,1,0:T(8,128)(2,1)S(1)} all-gather(bf16[16,2,4,8,128]{4,3,2,1,0:T(8,128)(2,1)S(1)} %all-to-all-done), channel_id=3, replica_groups=mesh['zl'=4,'x'=4,'y'=4,'zh'=4,'c'=2] {'c'}, dimensions={0}, use_global_device_ids=true | all-gather | bytes 786432 | tf_op jit(solution)/shard_map/all_gather | solution.py:157
  41.9 3.1 %shard_map.69 = (bf16[8,32,512]{2,1,0:T(8,128)(2,1)S(1)}, f32[32,512]{1,0:T(8,128)S(1)}, f32[128,512]{1,0:T(8,128)S(1)}) custom-call(s32[4]{0:T(128)S(1)} %pad_add_fusion.pos, f32[32,512]{1,0:T(8,128)S(1)} %fusion.s_ref, bf16[2,16,2,4,8,128]{5,4,3,2,1,0:T(8,128)(2,1)S(1)} %bitcast.24, bf16[32,256,128]{2,1,0:T(8,128)(2,1)S(1)} %shard_map.68.t), custom_call_target="tpu_custom_call" | custom-call | flops 2147483648 | bytes 2097152 | tf_op jit(solution)/shard_map/pallas_call | solution.py:163
  45.0 9.1 %all_to_all.25.parts_ref = bf16[8,32,512]{2,1,0:T(8,128)(2,1)S(1)} all-to-all(bf16[8,32,512]{2,1,0:T(8,128)(2,1)S(1)} %get-tuple-element.9), channel_id=1, replica_groups=mesh['zl'=4,'x'=4,'y'=4,'zh'=4,'c'=2] {'c','y'}, dimensions={0} | all-to-all | bytes 524288 | tf_op jit(solution)/shard_map/all_to_all | solution.py:172
  54.1 7.3 %all-gather.2 = bf16[64,512]{1,0:T(8,128)(2,1)S(1)} all-gather(bf16[32,512]{1,0:T(8,128)(2,1)S(1)} %shard_map.70), channel_id=4, replica_groups={{0,2},{4,6},{1,3},{5,7},{8,10},{12,14},{9,11},{13,15},{16,18},{20,22},{..., dimensions={0}, use_global_device_ids=true | all-gather | bytes 98304 | tf_op jit(solution)/shard_map/all_gather | solution.py:174
  61.5 7.3 %all-gather.3 = bf16[64,512]{1,0:T(8,128)(2,1)S(1)} all-gather(bf16[32,512]{1,0:T(8,128)(2,1)S(1)} %shard_map.71), channel_id=5, replica_groups={{2,4},{6,0},{3,5},{7,1},{10,12},{14,8},{11,13},{15,9},{18,20},{22,16},{..., dimensions={0}, use_global_device_ids=true | all-gather | bytes 98304 | tf_op jit(solution)/shard_map/all_gather | solution.py:175
  68.8 0.1 shard_map.72
  68.9 12.9 %all_to_all.26 = bf16[8,32,512]{2,1,0:T(8,128)(2,1)S(1)} all-to-all(bf16[8,32,512]{2,1,0:T(8,128)(2,1)S(1)} %shard_map.72), channel_id=1, replica_groups=mesh['zl'=4,'x'=4,'y'=4,'zh'=4,'c'=2] {'c','y'}, dimensions={0} | all-to-all | bytes 524288 | tf_op jit(solution)/shard_map/all_to_all | solution.py:177
  81.8 3.3 %shard_map.73 = (bf16[16,8,512]{2,1,0:T(8,128)(2,1)S(1)}, bf16[16,256]{1,0:T(8,128)(2,1)}, f32[8,512]{1,0:T(8,128)S(1)}) custom-call(s32[4]{0:T(128)S(1)} %pad_add_fusion.pos, f32[32,512]{1,0:T(8,128)S(1)} %fusion.s_ref, bf16[256,512]{1,0:T(8,128)(2,1)S(1)} %bitcast.26, f32[128,512]{1,0:T(8,128)S(1)} %get-tuple-element.10.two, ...), custom_call_target="tpu_custom_call" | custom-call | flops 2147483648 | bytes 2097152 | tf_op jit(solution)/shard_map/pallas_call | solution.py:179
  85.1 12.6 %all_to_all.27.parts_ref = bf16[16,8,512]{2,1,0:T(8,128)(2,1)S(1)} all-to-all(bf16[16,8,512]{2,1,0:T(8,128)(2,1)S(1)} %get-tuple-element.13), channel_id=1, replica_groups=mesh['zl'=4,'x'=4,'y'=4,'zh'=4,'c'=2] {'x','zl'}, dimensions={0} | all-to-all | bytes 262144 | tf_op jit(solution)/shard_map/all_to_all | solution.py:188
  97.7 0.2 shard_map.74
  97.9 10.5 %all_to_all.28.in_ref = bf16[16,8,128]{2,1,0:T(8,128)(2,1)S(1)} all-to-all(bf16[16,8,128]{2,1,0:T(8,128)(2,1)S(1)} %shard_map.74), channel_id=1, replica_groups=mesh['zl'=4,'x'=4,'y'=4,'zh'=4,'c'=2] {'x','zl'}, dimensions={0} | all-to-all | bytes 65536 | tf_op jit(solution)/shard_map/all_to_all | solution.py:190
  108.4 0.7 shard_map.75
  (3 shorter events, 0.1 us)
Async XLA Ops:
  0.6 24.0 %copy-start = (bf16[1024,512]{1,0:T(8,128)(2,1)S(1)}, bf16[1024,512]{1,0:T(8,128)(2,1)}, u32[]{:S(2)}) copy-start(bf16[1024,512]{1,0:T(8,128)(2,1)} %param.8) | copy-start | bytes 3145732
  10.5 29.2 %all-to-all-start = ((bf16[16,2,4,8,128]{4,3,2,1,0:T(8,128)(2,1)}), bf16[16,2,4,8,128]{4,3,2,1,0:T(8,128)(2,1)S(1)}, u32[]{:S(2)}, u32[]{:S(2)}) async-start(bf16[16,2,4,8,128]{4,3,2,1,0:T(8,128)(2,1)} %broadcast_in_dim.10), calls=%async_computation | async-start | bytes 524288 | tf_op jit(solution)/shard_map/all_to_all | solution.py:156
  22.7 1.6 %copy-start.1 = (bf16[32,256,128]{2,1,0:T(8,128)(2,1)S(1)}, bf16[32,256,128]{2,1,0:T(8,128)(2,1)}, u32[]{:S(2)}) copy-start(bf16[32,256,128]{2,1,0:T(8,128)(2,1)} %t_hbm.1) | copy-start | bytes 6291460
  24.3 0.7 copy-start.2

commit v10 on v9

--- a/solution.py
+++ b/solution.py
@@ -23,6 +23,10 @@
 CHUNKS = 4
 BATCH = 32
 STEP = 8
+
+
+def far_first(p):
+    return p // 4 * 4 + (0, 2, 1, 3)[p % 4]
 
 
 def dot(a, b, dims):
@@ -59,7 +63,7 @@
         for c in range(2):
             for h in range(4):
                 rows, lanes = pl.ds(32 * b + 16 * c + 8 * (h // 2), 8), pl.ds(128 * (h % 2), 128)
-                one_t[rows, lanes] = both_ref[1, b, c, h]
+                one_t[rows, lanes] = both_ref[1, far_first(b), c, h]
     one[...] = one_t[...].T
     for p in range(16):
         two_t[pl.ds(p % 4 * 128 + p // 4 * 32, 32), :] = both_ref[0, p, pos[3]].reshape(32, 128)
@@ -138,7 +142,7 @@
 
 def groups():
     device = lambda n, yz, c: (n * 16 + yz) * 2 + c
-    first = [[device(n, yz, 1) for yz in range(16)] for n in range(16)]
+    first = [[device(n, far_first(p), 1) for p in range(16)] for n in range(16)]
     second = [[device(p % 4 * 4 + p // 4, yz, 0) for p in range(16)] for yz in range(16)]
     return first + second
 

time: 110 us -> 109 us (level)
  waiting for transfers between devices: 14.4 us -> 12.6 us
  blocking collectives: 70.2 us -> 71.6 us
    all_to_all x1, waiting for transfers between devices: 14.4 us -> 12.6 us  [body(): lax.all_to_all(mine, ALL, 0, 0, axis_index_groups=groups(), tiled=True)]
where the time goes in v10:
time: 109 us
  blocking collectives  71.6 us (66%)
  waiting for transfers between devices  12.6 us (12%)
  starting transfers between devices  12.2 us (11%)
  Pallas kernels  7.57 us (7%)
  local copies, waits for them, and re-layouts  2.73 us (3%)
    all_to_all x1, blocking collectives, body(): parts_two = lax.all_to_all(partial_two, ('x', 'zl'), 0, 0, tiled=True)  13.5 us
    all_to_all x1, waiting for transfers between devices, body(): lax.all_to_all(mine, ALL, 0, 0, axis_index_groups=groups(), tiled=True)  12.6 us
    all_to_all x1, blocking collectives, body(): lax.all_to_all(copies, ('c', 'y'), 0, 0, tiled=True).reshape(256, R)  12.4 us
    all_to_all x1, starting transfers between devices, body(): lax.all_to_all(mine, ALL, 0, 0, axis_index_groups=groups(), tiled=True)  12.2 us
    all_to_all x1, blocking collectives, body(): blocks = lax.all_to_all(blocks, ('x', 'zl'), 0, 0, tiled=True)  10.5 us
    all_to_all x1, blocking collectives, body(): parts = lax.all_to_all(partial_one, ('c', 'y'), 0, 0, tiled=True)  10.1 us
    all_gather x1, blocking collectives, body(): blocks = lax.all_gather(blocks, 'c', axis=0).reshape(2, 2, 4, 8, 128)  8.31 us
    all_gather x1, blocking collectives, body(): lax.all_gather(add(parts), 'zh', axis=0, axis_index_groups=[[0, 1], [2, 3]])  7.34 us
  transfers between devices with their start and end apart: 1, of which 1 were waited for; matrix products, arithmetic and copies ran while one was open for 0% of the time, Pallas kernels for 0%

profile of v10, /device:TPU:1, one launch (start us, length us, event | category | flops | bytes accessed | tf_op | source)
XLA Modules:
  0.0 108.6 jit_solution(12777540179925726041)
XLA Ops:
  0.6 0.0 copy-start
  0.7 0.8 pad_maximum_fusion
  1.5 8.3 %all-gather = bf16[16,8,128]{2,1,0:T(8,128)(2,1)S(1)} all-gather(bf16[8,8,128]{2,1,0:T(8,128)(2,1)S(1)} %pad_maximum_fusion), channel_id=2, replica_groups=mesh['zl'=4,'x'=4,'y'=4,'zh'=4,'c'=2] {'c'}, dimensions={0}, use_global_device_ids=true | all-gather | bytes 49152 | tf_op jit(solution)/shard_map/all_gather | solution.py:157
  9.8 0.8 broadcast_in_dim.10
  10.5 12.2 %all-to-all-start = ((bf16[16,2,4,8,128]{4,3,2,1,0:T(8,128)(2,1)}), bf16[16,2,4,8,128]{4,3,2,1,0:T(8,128)(2,1)S(1)}, u32[]{:S(2)}, u32[]{:S(2)}) async-start(bf16[16,2,4,8,128]{4,3,2,1,0:T(8,128)(2,1)} %broadcast_in_dim.10), calls=%async_computation | async-start | bytes 524288 | tf_op jit(solution)/shard_map/all_to_all | solution.py:160
  22.7 0.0 copy-start.1
  22.8 1.6 %copy-done.1 = bf16[32,256,128]{2,1,0:T(8,128)(2,1)S(1)} copy-done((bf16[32,256,128]{2,1,0:T(8,128)(2,1)S(1)}, bf16[32,256,128]{2,1,0:T(8,128)(2,1)}, u32[]{:S(2)}) %copy-start.1) | copy-done | bytes 2097176
  24.3 0.0 copy-start.2
  24.3 0.2 shard_map.68.t
  24.5 0.1 pad_add_fusion.pos
  24.6 0.0 copy-done
  24.6 0.4 copy-done.2
  25.0 0.3 fusion.s_ref
  25.3 12.6 %all-to-all-done = bf16[16,2,4,8,128]{4,3,2,1,0:T(8,128)(2,1)S(1)} async-done(((bf16[16,2,4,8,128]{4,3,2,1,0:T(8,128)(2,1)}), bf16[16,2,4,8,128]{4,3,2,1,0:T(8,128)(2,1)S(1)}, u32[]{:S(2)}, u32[]{:S(2)}) %all-to-all-start) | async-done | bytes 262176 | tf_op jit(solution)/shard_map/all_to_all | solution.py:160
  37.9 2.2 %all-gather.1 = bf16[32,2,4,8,128]{4,3,2,1,0:T(8,128)(2,1)S(1)} all-gather(bf16[16,2,4,8,128]{4,3,2,1,0:T(8,128)(2,1)S(1)} %all-to-all-done), channel_id=3, replica_groups=mesh['zl'=4,'x'=4,'y'=4,'zh'=4,'c'=2] {'c'}, dimensions={0}, use_global_device_ids=true | all-gather | bytes 786432 | tf_op jit(solution)/shard_map/all_gather | solution.py:161
  40.1 3.1 %shard_map.69 = (bf16[8,32,512]{2,1,0:T(8,128)(2,1)S(1)}, f32[32,512]{1,0:T(8,128)S(1)}, f32[128,512]{1,0:T(8,128)S(1)}) custom-call(s32[4]{0:T(128)S(1)} %pad_add_fusion.pos, f32[32,512]{1,0:T(8,128)S(1)} %fusion.s_ref, bf16[2,16,2,4,8,128]{5,4,3,2,1,0:T(8,128)(2,1)S(1)} %bitcast.24, bf16[32,256,128]{2,1,0:T(8,128)(2,1)S(1)} %shard_map.68.t), custom_call_target="tpu_custom_call" | custom-call | flops 2147483648 | bytes 2097152 | tf_op jit(solution)/shard_map/pallas_call | solution.py:167
  43.2 10.1 %all_to_all.25.parts_ref = bf16[8,32,512]{2,1,0:T(8,128)(2,1)S(1)} all-to-all(bf16[8,32,512]{2,1,0:T(8,128)(2,1)S(1)} %get-tuple-element.9), channel_id=1, replica_groups=mesh['zl'=4,'x'=4,'y'=4,'zh'=4,'c'=2] {'c','y'}, dimensions={0} | all-to-all | bytes 524288 | tf_op jit(solution)/shard_map/all_to_all | solution.py:176
  53.3 7.3 %all-gather.2 = bf16[64,512]{1,0:T(8,128)(2,1)S(1)} all-gather(bf16[32,512]{1,0:T(8,128)(2,1)S(1)} %shard_map.70), channel_id=4, replica_groups={{0,2},{4,6},{1,3},{5,7},{8,10},{12,14},{9,11},{13,15},{16,18},{20,22},{..., dimensions={0}, use_global_device_ids=true | all-gather | bytes 98304 | tf_op jit(solution)/shard_map/all_gather | solution.py:178
  60.7 7.3 %all-gather.3 = bf16[64,512]{1,0:T(8,128)(2,1)S(1)} all-gather(bf16[32,512]{1,0:T(8,128)(2,1)S(1)} %shard_map.71), channel_id=5, replica_groups={{2,4},{6,0},{3,5},{7,1},{10,12},{14,8},{11,13},{15,9},{18,20},{22,16},{..., dimensions={0}, use_global_device_ids=true | all-gather | bytes 98304 | tf_op jit(solution)/shard_map/all_gather | solution.py:179
  68.0 0.1 shard_map.72
  68.1 12.4 %all_to_all.26 = bf16[8,32,512]{2,1,0:T(8,128)(2,1)S(1)} all-to-all(bf16[8,32,512]{2,1,0:T(8,128)(2,1)S(1)} %shard_map.72), channel_id=1, replica_groups=mesh['zl'=4,'x'=4,'y'=4,'zh'=4,'c'=2] {'c','y'}, dimensions={0} | all-to-all | bytes 524288 | tf_op jit(solution)/shard_map/all_to_all | solution.py:181
  80.5 3.3 %shard_map.73 = (bf16[16,8,512]{2,1,0:T(8,128)(2,1)S(1)}, bf16[16,256]{1,0:T(8,128)(2,1)}, f32[8,512]{1,0:T(8,128)S(1)}) custom-call(s32[4]{0:T(128)S(1)} %pad_add_fusion.pos, f32[32,512]{1,0:T(8,128)S(1)} %fusion.s_ref, bf16[256,512]{1,0:T(8,128)(2,1)S(1)} %bitcast.26, f32[128,512]{1,0:T(8,128)S(1)} %get-tuple-element.10.two, ...), custom_call_target="tpu_custom_call" | custom-call | flops 2147483648 | bytes 2097152 | tf_op jit(solution)/shard_map/pallas_call | solution.py:183
  83.8 13.5 %all_to_all.27.parts_ref = bf16[16,8,512]{2,1,0:T(8,128)(2,1)S(1)} all-to-all(bf16[16,8,512]{2,1,0:T(8,128)(2,1)S(1)} %get-tuple-element.13), channel_id=1, replica_groups=mesh['zl'=4,'x'=4,'y'=4,'zh'=4,'c'=2] {'x','zl'}, dimensions={0} | all-to-all | bytes 262144 | tf_op jit(solution)/shard_map/all_to_all | solution.py:192
  97.3 0.2 shard_map.74
  97.5 10.5 %all_to_all.28.in_ref = bf16[16,8,128]{2,1,0:T(8,128)(2,1)S(1)} all-to-all(bf16[16,8,128]{2,1,0:T(8,128)(2,1)S(1)} %shard_map.74), channel_id=1, replica_groups=mesh['zl'=4,'x'=4,'y'=4,'zh'=4,'c'=2] {'x','zl'}, dimensions={0} | all-to-all | bytes 65536 | tf_op jit(solution)/shard_map/all_to_all | solution.py:194
  108.0 0.7 shard_map.75
  (3 shorter events, 0.1 us)
Async XLA Ops:
  0.6 24.0 %copy-start = (bf16[1024,512]{1,0:T(8,128)(2,1)S(1)}, bf16[1024,512]{1,0:T(8,128)(2,1)}, u32[]{:S(2)}) copy-start(bf16[1024,512]{1,0:T(8,128)(2,1)} %param.8) | copy-start | bytes 3145732
  10.5 27.4 %all-to-all-start = ((bf16[16,2,4,8,128]{4,3,2,1,0:T(8,128)(2,1)}), bf16[16,2,4,8,128]{4,3,2,1,0:T(8,128)(2,1)S(1)}, u32[]{:S(2)}, u32[]{:S(2)}) async-start(bf16[16,2,4,8,128]{4,3,2,1,0:T(8,128)(2,1)} %broadcast_in_dim.10), calls=%async_computation | async-start | bytes 524288 | tf_op jit(solution)/shard_map/all_to_all | solution.py:160
  22.7 1.6 %copy-start.1 = (bf16[32,256,128]{2,1,0:T(8,128)(2,1)S(1)}, bf16[32,256,128]{2,1,0:T(8,128)(2,1)}, u32[]{:S(2)}) copy-start(bf16[32,256,128]{2,1,0:T(8,128)(2,1)} %t_hbm.1) | copy-start | bytes 6291460
  24.3 0.7 copy-start.2

commit v11 on v10

--- a/solution.py
+++ b/solution.py
@@ -74,10 +74,14 @@
     for k in range(0, BATCH, STEP):
         scaled, error = errors(s_ref[k : k + STEP, :], one[...], two, t, k)
         acc[...] += dot(error, scaled, NN)
-    out_ref[...] = acc[...].astype(bf16).reshape(8, 32, R)
-
-
-def second_kernel(pos, s_ref, new_ref, two, t, out_ref, block_ref, own_ref, acc):
+    total = acc[...].astype(bf16).reshape(8, 32, R)
+    out_ref[pl.ds(4 * pos[4], 4)] = total[:4]
+    out_ref[pl.ds(4 * (1 - pos[4]), 4)] = total[4:]
+
+
+def second_kernel(pos, s_ref, halves_ref, two, t, out_ref, block_ref, own_ref, new_ref, acc):
+    new_ref[:128] = halves_ref[pl.ds(4 * pos[4], 4)].reshape(128, R)
+    new_ref[128:] = halves_ref[pl.ds(4 * (1 - pos[4]), 4)].reshape(128, R)
     acc[...] = jnp.zeros_like(acc)
     block_ref[...] = dot(pick(pos[1], 16, R), new_ref[...], NT).astype(bf16)
     own_ref[...] = dot(pick(pos[2], 8, 128), two[...].astype(bf16), NN)
@@ -147,10 +151,15 @@
     return first + second
 
 
+def pairs(first):
+    return [[z % 4 * 2 + c, (z + 1) % 4 * 2 + 1 - c] for z in (first, first + 2) for c in range(2)]
+
+
 def body(slices, mode_one, mode_two, slice_table, chosen):
     y, c = lax.axis_index("y"), lax.axis_index("c")
+    odd = lax.axis_index("zh") & 1
     m, w = lax.axis_index(("x", "zl")), lax.axis_index(WIDE)
-    pos = jnp.stack([(c * 4 + y) * 32, w * 16, m * 8, c]).astype(jnp.int32)
+    pos = jnp.stack([((c ^ odd) * 4 + y) * 32, w * 16, m * 8, c, odd]).astype(jnp.int32)
 
     tiles = mode_one.T.reshape(2, 8, 2, 128).transpose(0, 2, 1, 3).reshape(4, 8, 128)
     blocks = jnp.concatenate([mode_two.T.reshape(4, 8, 128), tiles], axis=0)
@@ -175,16 +184,16 @@
     )(pos, slice_rows, both, t)
     parts = lax.all_to_all(partial_one, ("c", "y"), 0, 0, tiled=True)
     add = call(sum_kernel, [((32, R), bf16)], [VM])
-    parts = lax.all_gather(add(parts), "zh", axis=0, axis_index_groups=[[0, 1], [2, 3]])
-    parts = lax.all_gather(add(parts), "zh", axis=0, axis_index_groups=[[1, 2], [3, 0]])
+    parts = lax.all_gather(add(parts), ("zh", "c"), axis=0, axis_index_groups=pairs(0))
+    parts = lax.all_gather(add(parts), ("zh", "c"), axis=0, axis_index_groups=pairs(1))
     copies = call(renew_one_kernel, [((8, 32, R), bf16)], [VM, VM])(own_one, parts)
-    new_full = lax.all_to_all(copies, ("c", "y"), 0, 0, tiled=True).reshape(256, R)
+    new_full = lax.all_to_all(copies, ("c", "y"), 0, 0, tiled=True)
 
     partial_two, new_one_t, own_two = call(
         second_kernel,
         [((16, 8, R), bf16), ((16, 256), bf16), ((8, R), f32)],
         [SM, VM, VM, VM, VM],
-        (pltpu.VMEM((128, R), f32),),
+        (pltpu.VMEM((256, R), bf16), pltpu.VMEM((128, R), f32)),
         flops=1 << 31,
         vmem=16,
         nbytes=1 << 21,

time: 109 us -> 109 us (level)
    all_to_all x1, blocking collectives: 12.4 us -> 10.1 us  [body(): new_full = lax.all_to_all(copies, ('c', 'y'), 0, 0, tiled=True)]
    all_gather x2, blocking collectives: 14.7 us -> 15.9 us  [the longest x1 7.93 us: body(): lax.all_gather(add(parts), ('zh', 'c'), axis=0, axis_index_groups=pairs(1))]
where the time goes in v11:
time: 109 us; the launch traced here: 108 us
  blocking collectives  71 us (65%)
  waiting for transfers between devices  12.6 us (12%)
  starting transfers between devices  12.2 us (11%)
  Pallas kernels  7.59 us (7%)
  local copies, waits for them, and re-layouts  2.81 us (3%)
    all_to_all x1, blocking collectives, body(): parts_two = lax.all_to_all(partial_two, ('x', 'zl'), 0, 0, tiled=True)  14 us
    all_to_all x1, waiting for transfers between devices, body(): lax.all_to_all(mine, ALL, 0, 0, axis_index_groups=groups(), tiled=True)  12.6 us
    all_to_all x1, starting transfers between devices, body(): lax.all_to_all(mine, ALL, 0, 0, axis_index_groups=groups(), tiled=True)  12.2 us
    all_to_all x1, blocking collectives, body(): blocks = lax.all_to_all(blocks, ('x', 'zl'), 0, 0, tiled=True)  10.5 us
    all_to_all x1, blocking collectives, body(): parts = lax.all_to_all(partial_one, ('c', 'y'), 0, 0, tiled=True)  10.1 us
    all_to_all x1, blocking collectives, body(): new_full = lax.all_to_all(copies, ('c', 'y'), 0, 0, tiled=True)  10.1 us
    all_gather x1, blocking collectives, body(): blocks = lax.all_gather(blocks, 'c', axis=0).reshape(2, 2, 4, 8, 128)  8.31 us
    all_gather x1, blocking collectives, body(): lax.all_gather(add(parts), ('zh', 'c'), axis=0, axis_index_groups=pairs(1))  7.93 us
  transfers between devices with their start and end apart: 1, of which 1 were waited for; matrix products, arithmetic and copies ran while one was open for 0% of the time, Pallas kernels for 0%

profile of v11, /device:TPU:1, one launch (start us, length us, event | category | flops | bytes accessed | tf_op | source)
XLA Modules:
  0.0 108.0 jit_solution(10239123400784007455)
XLA Ops:
  0.6 0.0 copy-start
  0.7 0.8 pad_maximum_fusion
  1.5 8.3 %all-gather = bf16[16,8,128]{2,1,0:T(8,128)(2,1)S(1)} all-gather(bf16[8,8,128]{2,1,0:T(8,128)(2,1)S(1)} %pad_maximum_fusion), channel_id=2, replica_groups=mesh['zl'=4,'x'=4,'y'=4,'zh'=4,'c'=2] {'c'}, dimensions={0}, use_global_device_ids=true | all-gather | bytes 49152 | tf_op jit(solution)/shard_map/all_gather | solution.py:166
  9.8 0.8 broadcast_in_dim.10
  10.5 12.2 %all-to-all-start = ((bf16[16,2,4,8,128]{4,3,2,1,0:T(8,128)(2,1)}), bf16[16,2,4,8,128]{4,3,2,1,0:T(8,128)(2,1)S(1)}, u32[]{:S(2)}, u32[]{:S(2)}) async-start(bf16[16,2,4,8,128]{4,3,2,1,0:T(8,128)(2,1)} %broadcast_in_dim.10), calls=%async_computation | async-start | bytes 524288 | tf_op jit(solution)/shard_map/all_to_all | solution.py:169
  22.7 0.0 copy-start.1
  22.8 1.6 %copy-done.1 = bf16[32,256,128]{2,1,0:T(8,128)(2,1)S(1)} copy-done((bf16[32,256,128]{2,1,0:T(8,128)(2,1)S(1)}, bf16[32,256,128]{2,1,0:T(8,128)(2,1)}, u32[]{:S(2)}) %copy-start.1) | copy-done | bytes 2097176
  24.3 0.0 copy-start.2
  24.3 0.2 shard_map.68.t
  24.5 0.1 stack.23.pos
  24.6 0.0 copy-done
  24.6 0.4 copy-done.2
  25.0 0.3 fusion.s_ref
  25.3 12.6 %all-to-all-done = bf16[16,2,4,8,128]{4,3,2,1,0:T(8,128)(2,1)S(1)} async-done(((bf16[16,2,4,8,128]{4,3,2,1,0:T(8,128)(2,1)}), bf16[16,2,4,8,128]{4,3,2,1,0:T(8,128)(2,1)S(1)}, u32[]{:S(2)}, u32[]{:S(2)}) %all-to-all-start) | async-done | bytes 262176 | tf_op jit(solution)/shard_map/all_to_all | solution.py:169
  37.9 2.2 %all-gather.1 = bf16[32,2,4,8,128]{4,3,2,1,0:T(8,128)(2,1)S(1)} all-gather(bf16[16,2,4,8,128]{4,3,2,1,0:T(8,128)(2,1)S(1)} %all-to-all-done), channel_id=3, replica_groups=mesh['zl'=4,'x'=4,'y'=4,'zh'=4,'c'=2] {'c'}, dimensions={0}, use_global_device_ids=true | all-gather | bytes 786432 | tf_op jit(solution)/shard_map/all_gather | solution.py:170
  40.1 3.1 %shard_map.69 = (bf16[8,32,512]{2,1,0:T(8,128)(2,1)S(1)}, f32[32,512]{1,0:T(8,128)S(1)}, f32[128,512]{1,0:T(8,128)S(1)}) custom-call(s32[5]{0:T(128)S(1)} %stack.23.pos, f32[32,512]{1,0:T(8,128)S(1)} %fusion.s_ref, bf16[2,16,2,4,8,128]{5,4,3,2,1,0:T(8,128)(2,1)S(1)} %bitcast.24, bf16[32,256,128]{2,1,0:T(8,128)(2,1)S(1)} %shard_map.68.t), custom_call_target="tpu_custom_call" | custom-call | flops 2147483648 | bytes 2097152 | tf_op jit(solution)/shard_map/pallas_call | solution.py:176
  43.2 10.1 %all_to_all.25.parts_ref = bf16[8,32,512]{2,1,0:T(8,128)(2,1)S(1)} all-to-all(bf16[8,32,512]{2,1,0:T(8,128)(2,1)S(1)} %get-tuple-element.9), channel_id=1, replica_groups=mesh['zl'=4,'x'=4,'y'=4,'zh'=4,'c'=2] {'c','y'}, dimensions={0} | all-to-all | bytes 524288 | tf_op jit(solution)/shard_map/all_to_all | solution.py:185
  53.3 7.9 %all-gather.2 = bf16[64,512]{1,0:T(8,128)(2,1)S(1)} all-gather(bf16[32,512]{1,0:T(8,128)(2,1)S(1)} %shard_map.70), channel_id=4, replica_groups={{0,3},{1,2},{4,7},{5,6},{8,11},{9,10},{12,15},{13,14},{16,19},{17,18},{..., dimensions={0}, use_global_device_ids=true | all-gather | bytes 98304 | tf_op jit(solution)/shard_map/all_gather | solution.py:187
  61.3 7.9 %all-gather.3 = bf16[64,512]{1,0:T(8,128)(2,1)S(1)} all-gather(bf16[32,512]{1,0:T(8,128)(2,1)S(1)} %shard_map.71), channel_id=5, replica_groups={{2,5},{3,4},{6,1},{7,0},{10,13},{11,12},{14,9},{15,8},{18,21},{19,20},{..., dimensions={0}, use_global_device_ids=true | all-gather | bytes 98304 | tf_op jit(solution)/shard_map/all_gather | solution.py:188
  69.2 0.1 shard_map.72
  69.3 10.1 %all_to_all.26.halves_ref = bf16[8,32,512]{2,1,0:T(8,128)(2,1)S(1)} all-to-all(bf16[8,32,512]{2,1,0:T(8,128)(2,1)S(1)} %shard_map.72), channel_id=1, replica_groups=mesh['zl'=4,'x'=4,'y'=4,'zh'=4,'c'=2] {'c','y'}, dimensions={0} | all-to-all | bytes 524288 | tf_op jit(solution)/shard_map/all_to_all | solution.py:190
  79.4 3.3 %shard_map.73 = (bf16[16,8,512]{2,1,0:T(8,128)(2,1)S(1)}, bf16[16,256]{1,0:T(8,128)(2,1)}, f32[8,512]{1,0:T(8,128)S(1)}) custom-call(s32[5]{0:T(128)S(1)} %stack.23.pos, f32[32,512]{1,0:T(8,128)S(1)} %fusion.s_ref, bf16[8,32,512]{2,1,0:T(8,128)(2,1)S(1)} %all_to_all.26.halves_ref, f32[128,512]{1,0:T(8,128)S(1)} %get-tuple-element.10.two, ...), custom_call_target="tpu_custom_call" | custom-call | flops 2147483648 | bytes 2097152 | tf_op jit(solution)/shard_map/pallas_call | solution.py:192
  82.7 14.0 %all_to_all.27.parts_ref = bf16[16,8,512]{2,1,0:T(8,128)(2,1)S(1)} all-to-all(bf16[16,8,512]{2,1,0:T(8,128)(2,1)S(1)} %get-tuple-element.13), channel_id=1, replica_groups=mesh['zl'=4,'x'=4,'y'=4,'zh'=4,'c'=2] {'x','zl'}, dimensions={0} | all-to-all | bytes 262144 | tf_op jit(solution)/shard_map/all_to_all | solution.py:201
  96.7 0.2 shard_map.74
  96.9 10.5 %all_to_all.28.in_ref = bf16[16,8,128]{2,1,0:T(8,128)(2,1)S(1)} all-to-all(bf16[16,8,128]{2,1,0:T(8,128)(2,1)S(1)} %shard_map.74), channel_id=1, replica_groups=mesh['zl'=4,'x'=4,'y'=4,'zh'=4,'c'=2] {'x','zl'}, dimensions={0} | all-to-all | bytes 65536 | tf_op jit(solution)/shard_map/all_to_all | solution.py:203
  107.4 0.7 shard_map.75
  (3 shorter events, 0.1 us)
Async XLA Ops:
  0.6 24.0 %copy-start = (bf16[1024,512]{1,0:T(8,128)(2,1)S(1)}, bf16[1024,512]{1,0:T(8,128)(2,1)}, u32[]{:S(2)}) copy-start(bf16[1024,512]{1,0:T(8,128)(2,1)} %param.8) | copy-start | bytes 3145732
  10.5 27.4 %all-to-all-start = ((bf16[16,2,4,8,128]{4,3,2,1,0:T(8,128)(2,1)}), bf16[16,2,4,8,128]{4,3,2,1,0:T(8,128)(2,1)S(1)}, u32[]{:S(2)}, u32[]{:S(2)}) async-start(bf16[16,2,4,8,128]{4,3,2,1,0:T(8,128)(2,1)} %broadcast_in_dim.10), calls=%async_computation | async-start | bytes 524288 | tf_op jit(solution)/shard_map/all_to_all | solution.py:169
  22.7 1.6 %copy-start.1 = (bf16[32,256,128]{2,1,0:T(8,128)(2,1)S(1)}, bf16[32,256,128]{2,1,0:T(8,128)(2,1)}, u32[]{:S(2)}) copy-start(bf16[32,256,128]{2,1,0:T(8,128)(2,1)} %t_hbm.1) | copy-start | bytes 6291460
  24.3 0.7 copy-start.2

commit v12 on v11

--- a/solution.py
+++ b/solution.py
@@ -23,6 +23,7 @@
 CHUNKS = 4
 BATCH = 32
 STEP = 8
+WIDE_STEP = 16
 
 
 def far_first(p):
@@ -40,9 +41,10 @@
 
 
 def errors(s, left, two, t, k):
-    scaled = jnp.concatenate([two[...] * s[q : q + 1] for q in range(STEP)], axis=0).astype(bf16)
+    count = s.shape[0]
+    scaled = jnp.concatenate([two[...] * s[q : q + 1] for q in range(count)], axis=0).astype(bf16)
     model = dot(left, scaled, NT)
-    target = jnp.concatenate([t[k + q] for q in range(STEP)], axis=1).astype(f32)
+    target = jnp.concatenate([t[k + q] for q in range(count)], axis=1).astype(f32)
     return scaled, jnp.tanh(model - target).astype(bf16)
 
 
@@ -85,12 +87,12 @@
     acc[...] = jnp.zeros_like(acc)
     block_ref[...] = dot(pick(pos[1], 16, R), new_ref[...], NT).astype(bf16)
     own_ref[...] = dot(pick(pos[2], 8, 128), two[...].astype(bf16), NN)
-    for k in range(0, BATCH, STEP):
-        s = s_ref[k : k + STEP, :]
+    for k in range(0, BATCH, WIDE_STEP):
+        s = s_ref[k : k + WIDE_STEP, :]
         _, error = errors(s, new_ref[...], two, t, k)
         both = dot(error, new_ref[...], TN)
         total = acc[...]
-        for q in range(STEP):
+        for q in range(WIDE_STEP):
             total = total + both[128 * q : 128 * q + 128] * s[q : q + 1]
         acc[...] = total
     out_ref[...] = acc[...].astype(bf16).reshape(16, 8, R)

time: 109 us -> 108 us (level)
  no operation moved by 1% of the time
where the time goes in v12:
time: 108 us
  blocking collectives  71 us (66%)
  waiting for transfers between devices  12.6 us (12%)
  starting transfers between devices  12.2 us (11%)
  Pallas kernels  7.45 us (7%)
  local copies, waits for them, and re-layouts  2.81 us (3%)
    all_to_all x1, blocking collectives, body(): parts_two = lax.all_to_all(partial_two, ('x', 'zl'), 0, 0, tiled=True)  14 us
    all_to_all x1, waiting for transfers between devices, body(): lax.all_to_all(mine, ALL, 0, 0, axis_index_groups=groups(), tiled=True)  12.6 us
    all_to_all x1, starting transfers between devices, body(): lax.all_to_all(mine, ALL, 0, 0, axis_index_groups=groups(), tiled=True)  12.2 us
    all_to_all x1, blocking collectives, body(): blocks = lax.all_to_all(blocks, ('x', 'zl'), 0, 0, tiled=True)  10.5 us
    all_to_all x1, blocking collectives, body(): parts = lax.all_to_all(partial_one, ('c', 'y'), 0, 0, tiled=True)  10.1 us
    all_to_all x1, blocking collectives, body(): new_full = lax.all_to_all(copies, ('c', 'y'), 0, 0, tiled=True)  10.1 us
    all_gather x1, blocking collectives, body(): blocks = lax.all_gather(blocks, 'c', axis=0).reshape(2, 2, 4, 8, 128)  8.31 us
    all_gather x1, blocking collectives, body(): lax.all_gather(add(parts), ('zh', 'c'), axis=0, axis_index_groups=pairs(1))  7.93 us
  transfers between devices with their start and end apart: 1, of which 1 were waited for; matrix products, arithmetic and copies ran while one was open for 0% of the time, Pallas kernels for 0%

profile of v12, /device:TPU:1, one launch (start us, length us, event | category | flops | bytes accessed | tf_op | source)
XLA Modules:
  0.0 107.9 jit_solution(8091395412796392072)
XLA Ops:
  0.6 0.0 copy-start
  0.7 0.8 pad_maximum_fusion
  1.5 8.3 %all-gather = bf16[16,8,128]{2,1,0:T(8,128)(2,1)S(1)} all-gather(bf16[8,8,128]{2,1,0:T(8,128)(2,1)S(1)} %pad_maximum_fusion), channel_id=2, replica_groups=mesh['zl'=4,'x'=4,'y'=4,'zh'=4,'c'=2] {'c'}, dimensions={0}, use_global_device_ids=true | all-gather | bytes 49152 | tf_op jit(solution)/shard_map/all_gather | solution.py:168
  9.8 0.8 broadcast_in_dim.10
  10.5 12.2 %all-to-all-start = ((bf16[16,2,4,8,128]{4,3,2,1,0:T(8,128)(2,1)}), bf16[16,2,4,8,128]{4,3,2,1,0:T(8,128)(2,1)S(1)}, u32[]{:S(2)}, u32[]{:S(2)}) async-start(bf16[16,2,4,8,128]{4,3,2,1,0:T(8,128)(2,1)} %broadcast_in_dim.10), calls=%async_computation | async-start | bytes 524288 | tf_op jit(solution)/shard_map/all_to_all | solution.py:171
  22.7 0.0 copy-start.1
  22.8 1.6 %copy-done.1 = bf16[32,256,128]{2,1,0:T(8,128)(2,1)S(1)} copy-done((bf16[32,256,128]{2,1,0:T(8,128)(2,1)S(1)}, bf16[32,256,128]{2,1,0:T(8,128)(2,1)}, u32[]{:S(2)}) %copy-start.1) | copy-done | bytes 2097176
  24.3 0.0 copy-start.2
  24.3 0.2 shard_map.68.t
  24.5 0.1 stack.23.pos
  24.6 0.0 copy-done
  24.6 0.4 copy-done.2
  25.0 0.3 fusion.s_ref
  25.3 12.6 %all-to-all-done = bf16[16,2,4,8,128]{4,3,2,1,0:T(8,128)(2,1)S(1)} async-done(((bf16[16,2,4,8,128]{4,3,2,1,0:T(8,128)(2,1)}), bf16[16,2,4,8,128]{4,3,2,1,0:T(8,128)(2,1)S(1)}, u32[]{:S(2)}, u32[]{:S(2)}) %all-to-all-start) | async-done | bytes 262176 | tf_op jit(solution)/shard_map/all_to_all | solution.py:171
  37.9 2.2 %all-gather.1 = bf16[32,2,4,8,128]{4,3,2,1,0:T(8,128)(2,1)S(1)} all-gather(bf16[16,2,4,8,128]{4,3,2,1,0:T(8,128)(2,1)S(1)} %all-to-all-done), channel_id=3, replica_groups=mesh['zl'=4,'x'=4,'y'=4,'zh'=4,'c'=2] {'c'}, dimensions={0}, use_global_device_ids=true | all-gather | bytes 786432 | tf_op jit(solution)/shard_map/all_gather | solution.py:172
  40.1 3.1 %shard_map.69 = (bf16[8,32,512]{2,1,0:T(8,128)(2,1)S(1)}, f32[32,512]{1,0:T(8,128)S(1)}, f32[128,512]{1,0:T(8,128)S(1)}) custom-call(s32[5]{0:T(128)S(1)} %stack.23.pos, f32[32,512]{1,0:T(8,128)S(1)} %fusion.s_ref, bf16[2,16,2,4,8,128]{5,4,3,2,1,0:T(8,128)(2,1)S(1)} %bitcast.24, bf16[32,256,128]{2,1,0:T(8,128)(2,1)S(1)} %shard_map.68.t), custom_call_target="tpu_custom_call" | custom-call | flops 2147483648 | bytes 2097152 | tf_op jit(solution)/shard_map/pallas_call | solution.py:178
  43.2 10.1 %all_to_all.25.parts_ref = bf16[8,32,512]{2,1,0:T(8,128)(2,1)S(1)} all-to-all(bf16[8,32,512]{2,1,0:T(8,128)(2,1)S(1)} %get-tuple-element.9), channel_id=1, replica_groups=mesh['zl'=4,'x'=4,'y'=4,'zh'=4,'c'=2] {'c','y'}, dimensions={0} | all-to-all | bytes 524288 | tf_op jit(solution)/shard_map/all_to_all | solution.py:187
  53.3 7.9 %all-gather.2 = bf16[64,512]{1,0:T(8,128)(2,1)S(1)} all-gather(bf16[32,512]{1,0:T(8,128)(2,1)S(1)} %shard_map.70), channel_id=4, replica_groups={{0,3},{1,2},{4,7},{5,6},{8,11},{9,10},{12,15},{13,14},{16,19},{17,18},{..., dimensions={0}, use_global_device_ids=true | all-gather | bytes 98304 | tf_op jit(solution)/shard_map/all_gather | solution.py:189
  61.3 7.9 %all-gather.3 = bf16[64,512]{1,0:T(8,128)(2,1)S(1)} all-gather(bf16[32,512]{1,0:T(8,128)(2,1)S(1)} %shard_map.71), channel_id=5, replica_groups={{2,5},{3,4},{6,1},{7,0},{10,13},{11,12},{14,9},{15,8},{18,21},{19,20},{..., dimensions={0}, use_global_device_ids=true | all-gather | bytes 98304 | tf_op jit(solution)/shard_map/all_gather | solution.py:190
  69.2 0.1 shard_map.72
  69.3 10.1 %all_to_all.26.halves_ref = bf16[8,32,512]{2,1,0:T(8,128)(2,1)S(1)} all-to-all(bf16[8,32,512]{2,1,0:T(8,128)(2,1)S(1)} %shard_map.72), channel_id=1, replica_groups=mesh['zl'=4,'x'=4,'y'=4,'zh'=4,'c'=2] {'c','y'}, dimensions={0} | all-to-all | bytes 524288 | tf_op jit(solution)/shard_map/all_to_all | solution.py:192
  79.4 3.2 %shard_map.73 = (bf16[16,8,512]{2,1,0:T(8,128)(2,1)S(1)}, bf16[16,256]{1,0:T(8,128)(2,1)}, f32[8,512]{1,0:T(8,128)S(1)}) custom-call(s32[5]{0:T(128)S(1)} %stack.23.pos, f32[32,512]{1,0:T(8,128)S(1)} %fusion.s_ref, bf16[8,32,512]{2,1,0:T(8,128)(2,1)S(1)} %all_to_all.26.halves_ref, f32[128,512]{1,0:T(8,128)S(1)} %get-tuple-element.10.two, ...), custom_call_target="tpu_custom_call" | custom-call | flops 2147483648 | bytes 2097152 | tf_op jit(solution)/shard_map/pallas_call | solution.py:194
  82.5 14.0 %all_to_all.27.parts_ref = bf16[16,8,512]{2,1,0:T(8,128)(2,1)S(1)} all-to-all(bf16[16,8,512]{2,1,0:T(8,128)(2,1)S(1)} %get-tuple-element.13), channel_id=1, replica_groups=mesh['zl'=4,'x'=4,'y'=4,'zh'=4,'c'=2] {'x','zl'}, dimensions={0} | all-to-all | bytes 262144 | tf_op jit(solution)/shard_map/all_to_all | solution.py:203
  96.5 0.2 shard_map.74
  96.7 10.5 %all_to_all.28.in_ref = bf16[16,8,128]{2,1,0:T(8,128)(2,1)S(1)} all-to-all(bf16[16,8,128]{2,1,0:T(8,128)(2,1)S(1)} %shard_map.74), channel_id=1, replica_groups=mesh['zl'=4,'x'=4,'y'=4,'zh'=4,'c'=2] {'x','zl'}, dimensions={0} | all-to-all | bytes 65536 | tf_op jit(solution)/shard_map/all_to_all | solution.py:205
  107.2 0.7 shard_map.75
  (3 shorter events, 0.1 us)
Async XLA Ops:
  0.6 24.0 %copy-start = (bf16[1024,512]{1,0:T(8,128)(2,1)S(1)}, bf16[1024,512]{1,0:T(8,128)(2,1)}, u32[]{:S(2)}) copy-start(bf16[1024,512]{1,0:T(8,128)(2,1)} %param.8) | copy-start | bytes 3145732
  10.5 27.4 %all-to-all-start = ((bf16[16,2,4,8,128]{4,3,2,1,0:T(8,128)(2,1)}), bf16[16,2,4,8,128]{4,3,2,1,0:T(8,128)(2,1)S(1)}, u32[]{:S(2)}, u32[]{:S(2)}) async-start(bf16[16,2,4,8,128]{4,3,2,1,0:T(8,128)(2,1)} %broadcast_in_dim.10), calls=%async_computation | async-start | bytes 524288 | tf_op jit(solution)/shard_map/all_to_all | solution.py:171
  22.7 1.6 %copy-start.1 = (bf16[32,256,128]{2,1,0:T(8,128)(2,1)S(1)}, bf16[32,256,128]{2,1,0:T(8,128)(2,1)}, u32[]{:S(2)}) copy-start(bf16[32,256,128]{2,1,0:T(8,128)(2,1)} %t_hbm.1) | copy-start | bytes 6291460
  24.3 0.7 copy-start.2
